TPU v7x, 32 devices: a whole 2x2x4 slice. The times are simulated.
32 devices in a mesh: batch: 8 (over z, y), expert: 4 (over x, core).
Axes of the slice: x: 2, y: 2, z: 4, core: 2. Of those that a mesh axis runs over, the one named last changes fastest.
Arguments:
- tokens: bfloat16 [32768, 768], P(('batch', 'expert')), may hold values from -6 to 6
- condition: bfloat16 [128, 768], P(('batch', 'expert')), may hold values from -6 to 6
- lengths: int32 [128], P(('batch', 'expert')), may hold values from 32 to 256, as said below
- routes: int32 [32768, 2], P(('batch', 'expert')), may hold values from 0 to 7, all different within a row
- cotangent: bfloat16 [32768, 768], P(('batch', 'expert')), may hold values from -6 to 6
- ada_weight: bfloat16 [768, 4608], replicated, may hold values from -0.21875 to 0.21875
- qkv_weight: bfloat16 [768, 2304], replicated, may hold values from -0.21875 to 0.21875
- out_weight: bfloat16 [768, 768], replicated, may hold values from -0.875 to 0.875
- router_weight: bfloat16 [768, 8], replicated, may hold values from -0.15625 to 0.15625
- shared_in: bfloat16 [768, 3072], replicated, may hold values from -0.21875 to 0.21875
- shared_out: bfloat16 [3072, 768], replicated, may hold values from -0.109375 to 0.109375
- expert_in: bfloat16 [8, 768, 3072], P('expert'), may hold values from -0.21875 to 0.21875
- expert_out: bfloat16 [8, 3072, 768], P('expert'), may hold values from -0.109375 to 0.109375
Outputs:
- out: bfloat16 [32768, 768], P(('batch', 'expert'))
- grad_tokens: float32 [32768, 768], P(('batch', 'expert'))
- grad_ada: float32 [768, 4608], P('batch', 'expert')
- grad_qkv: float32 [768, 2304], P('batch', 'expert')
- grad_out_proj: float32 [768, 768], P('batch', 'expert')
- grad_router: float32 [768, 8], P('batch', 'expert')
- grad_shared_in: float32 [768, 3072], P('batch', 'expert')
- grad_shared_out: float32 [3072, 768], P('batch', 'expert')
- grad_expert_in: float32 [8, 768, 3072], P('expert', 'batch')
- grad_expert_out: float32 [8, 3072, 768], P('expert', 'batch')
Inputs may be any that keep to these rules, and one draw needn't show every extreme that they name: `lengths`: the live patches of an item come first, the rest are padding. Item 0 is full.
All inputs are finite; a program needn't handle non-finite values.
Results may differ from a plain program's by a relative error of at most 0.014.
The roundings to bfloat16 on the way count: a program that leaves them out, or rounds other values in their place, can miss the bound.
Values may be sent and summed in bfloat16 or wider, within the bound.
A program may use at most 320 MiB of HBM per device.

v0:
```python
import jax
import jax.numpy as jnp
from jax import lax
from jax.sharding import PartitionSpec as P

D = 768
HEADS = 12
HEAD_DIM = 64
EXPERTS = 8
SEQ = 256
CAP = 256


GELU_C = 0.7978845608028654
GELU_A = 0.044715
EPSILON = 1e-06
MASKED = -1000000000.0


def gelu_tanh(values):
    inside_arg = GELU_C * (values + GELU_A * values * values * values)
    return 0.5 * values * (1.0 + jnp.tanh(inside_arg))


def gelu_slope(values):
    tangent = jnp.tanh(GELU_C * (values + GELU_A * values * values * values))
    return 0.5 * (1.0 + tangent) + 0.5 * values * (1.0 - tangent * tangent) * GELU_C * (
        1.0 + 3.0 * GELU_A * values * values
    )


def normalize(values):
    centre = values - jnp.mean(values, -1, keepdims=True)
    factor = lax.rsqrt(jnp.mean(centre * centre, -1, keepdims=True) + EPSILON)
    return (centre * factor, factor)


def norm_back(grad_norm, normed, factor):
    return factor * (
        grad_norm
        - jnp.mean(grad_norm, -1, keepdims=True)
        - normed * jnp.mean(grad_norm * normed, -1, keepdims=True)
    )


def attention_scores(queries, keys_all, key_mask, scale_qk):
    raw_scores = (
        jnp.einsum("iqhd,ikhd->ihqk", queries, keys_all, preferred_element_type=jnp.float32)
        * scale_qk
    )
    return jnp.where(key_mask, raw_scores, MASKED)


def per_device(
    tokens,
    condition,
    lengths,
    routes,
    cotangent,
    ada_weight,
    qkv_weight,
    out_weight,
    router_weight,
    shared_in,
    shared_out,
    expert_in,
    expert_out,
):
    groups = lax.axis_size("expert")
    local_experts = expert_in.shape[0]
    item_count = lengths.shape[0]
    token_count = tokens.shape[0]
    scale_qk = HEAD_DIM ** (-0.5)
    live_mask = jnp.arange(SEQ)[None, :] < lengths[:, None]
    live_flat = live_mask.reshape(token_count)
    key_mask = live_mask[:, None, None, :]
    cond_act = jax.nn.silu(condition.astype(jnp.float32)).astype(jnp.bfloat16)
    modulation = jnp.dot(cond_act, ada_weight, preferred_element_type=jnp.float32).reshape(
        item_count, 6, 1, D
    )
    shift_attn, scale_attn, gate_attn, shift_mlp, scale_mlp, gate_mlp = [
        modulation[:, index_col] for index_col in range(6)
    ]
    expert_ids = jnp.arange(EXPERTS)
    route_float = (routes[:, :, None] == expert_ids).astype(jnp.float32)
    route_hot = (routes[:, :, None] == expert_ids).astype(jnp.int32) * live_flat[
        :, None, None
    ].astype(jnp.int32)
    flat_hot = route_hot.reshape(token_count * 2, EXPERTS)
    earlier = jnp.cumsum(flat_hot, axis=0) - flat_hot
    position = jnp.sum(earlier * flat_hot, -1).reshape(token_count, 2)
    kept_pair = live_flat[:, None] & (position < CAP)
    slot_index = routes * CAP + position
    slot_total = EXPERTS * CAP
    target = jnp.where(kept_pair, slot_index, slot_total).reshape(token_count * 2)
    slot_pair = (
        jnp.zeros(slot_total, jnp.int32)
        .at[target]
        .set(jnp.arange(token_count * 2, dtype=jnp.int32), mode="drop")
    )
    filled_low = (
        jnp.zeros(slot_total, jnp.float32)
        .at[target]
        .set(1.0, mode="drop")
        .astype(jnp.bfloat16)[:, None]
    )
    slot_token = slot_pair // 2
    safe_slot = jnp.where(kept_pair, slot_index, 0)
    kept_float = kept_pair.astype(jnp.float32)
    input_items = tokens.astype(jnp.float32).reshape(item_count, SEQ, D)
    normed_attn, factor_attn = normalize(input_items)
    h_attn = (
        (normed_attn * (1.0 + scale_attn) + shift_attn).astype(jnp.bfloat16).reshape(token_count, D)
    )
    qkv_all = (
        jnp.dot(h_attn, qkv_weight, preferred_element_type=jnp.float32)
        .astype(jnp.bfloat16)
        .reshape(item_count, SEQ, 3, HEADS, HEAD_DIM)
    )
    queries = qkv_all[:, :, 0]
    keys_all = qkv_all[:, :, 1]
    values_all = qkv_all[:, :, 2]
    scores = attention_scores(queries, keys_all, key_mask, scale_qk)
    peak = jnp.max(scores, -1, keepdims=True)
    log_total = peak + jnp.log(jnp.sum(jnp.exp(scores - peak), -1, keepdims=True))
    probabilities = jnp.exp(scores - log_total)
    heads_out = jnp.einsum(
        "ihqk,ikhd->iqhd",
        probabilities.astype(jnp.bfloat16),
        values_all,
        preferred_element_type=jnp.float32,
    )
    heads_low = heads_out.astype(jnp.bfloat16).reshape(token_count, D)
    attn_out = jnp.dot(heads_low, out_weight, preferred_element_type=jnp.float32).reshape(
        item_count, SEQ, D
    )
    x_mid = input_items + gate_attn * attn_out
    normed_mlp, factor_mlp = normalize(x_mid)
    h_mlp = (
        (normed_mlp * (1.0 + scale_mlp) + shift_mlp).astype(jnp.bfloat16).reshape(token_count, D)
    )
    shared_pre = jnp.dot(h_mlp, shared_in, preferred_element_type=jnp.float32)
    shared_act = gelu_tanh(shared_pre).astype(jnp.bfloat16)
    shared_res = jnp.dot(shared_act, shared_out, preferred_element_type=jnp.float32)
    logits = jnp.dot(h_mlp, router_weight, preferred_element_type=jnp.float32)
    gate_weights = jax.nn.softmax(jnp.sum(route_float * logits[:, None, :], -1), -1)
    send_rows = (h_mlp[slot_token] * filled_low).reshape(groups, local_experts, CAP, D)
    received = lax.all_to_all(send_rows, "expert", split_axis=0, concat_axis=0, tiled=True)
    expert_pre = jnp.einsum(
        "sjcd,jdf->sjcf", received, expert_in, preferred_element_type=jnp.float32
    )
    expert_act = gelu_tanh(expert_pre).astype(jnp.bfloat16)
    expert_rows = jnp.einsum(
        "sjcf,jfd->sjcd", expert_act, expert_out, preferred_element_type=jnp.float32
    ).astype(jnp.bfloat16)
    outputs = (expert_rows, expert_pre, received)
    expert_rows = outputs[0]
    rows_in = outputs[-1]
    returned = lax.all_to_all(
        expert_rows, "expert", split_axis=0, concat_axis=0, tiled=True
    ).reshape(slot_total, D)
    pair_rows = returned[safe_slot].astype(jnp.float32) * kept_float[:, :, None]
    moe_out = jnp.sum(gate_weights[:, :, None] * pair_rows, 1)
    mlp_out = (shared_res + moe_out).reshape(item_count, SEQ, D)
    result = (x_mid + gate_mlp * mlp_out).reshape(token_count, D).astype(jnp.bfloat16)
    grad_y = cotangent.astype(jnp.float32).reshape(item_count, SEQ, D)
    grad_gate_mlp = jnp.sum(grad_y * mlp_out, 1)
    grad_mlp = (gate_mlp * grad_y).reshape(token_count, D)
    g_shared = grad_mlp.astype(jnp.bfloat16)
    grad_w_sh2 = jnp.einsum("tf,td->fd", shared_act, g_shared, preferred_element_type=jnp.float32)
    g_pre = (
        jnp.einsum("td,fd->tf", g_shared, shared_out, preferred_element_type=jnp.float32)
        * gelu_slope(shared_pre)
    ).astype(jnp.bfloat16)
    grad_w_sh1 = jnp.einsum("td,tf->df", h_mlp, g_pre, preferred_element_type=jnp.float32)
    grad_h = jnp.einsum("tf,df->td", g_pre, shared_in, preferred_element_type=jnp.float32)
    g_gate = jnp.sum(grad_mlp[:, None, :] * pair_rows, -1)
    g_row = (
        (gate_weights[:, :, None] * kept_float[:, :, None] * grad_mlp[:, None, :])
        .astype(jnp.bfloat16)
        .reshape(token_count * 2, D)
    )
    send_grad = (g_row[slot_pair] * filled_low).reshape(groups, local_experts, CAP, D)
    grad_rows = lax.all_to_all(send_grad, "expert", split_axis=0, concat_axis=0, tiled=True)
    expert_pre = outputs[1]
    expert_act = gelu_tanh(expert_pre).astype(jnp.bfloat16)
    grad_w_e2 = jnp.einsum(
        "sjcf,sjcd->jfd", expert_act, grad_rows, preferred_element_type=jnp.float32
    )
    g_epre = (
        jnp.einsum("sjcd,jfd->sjcf", grad_rows, expert_out, preferred_element_type=jnp.float32)
        * gelu_slope(expert_pre)
    ).astype(jnp.bfloat16)
    grad_w_e1 = jnp.einsum("sjcd,sjcf->jdf", rows_in, g_epre, preferred_element_type=jnp.float32)
    g_in = jnp.einsum(
        "sjcf,jdf->sjcd", g_epre, expert_in, preferred_element_type=jnp.float32
    ).astype(jnp.bfloat16)
    grad_back = lax.all_to_all(g_in, "expert", split_axis=0, concat_axis=0, tiled=True).reshape(
        slot_total, D
    )
    grad_h = grad_h + jnp.sum(grad_back[safe_slot].astype(jnp.float32) * kept_float[:, :, None], 1)
    weighted = jnp.sum(gate_weights * g_gate, -1, keepdims=True)
    g_sel = gate_weights * (g_gate - weighted)
    grad_logits = jnp.sum(route_float * g_sel[:, :, None], 1)
    grad_w_router = jnp.dot(
        h_mlp.astype(jnp.float32).T, grad_logits, precision=lax.Precision.HIGHEST
    )
    grad_h = grad_h + jnp.dot(
        grad_logits, router_weight.astype(jnp.float32).T, precision=lax.Precision.HIGHEST
    )
    grad_h_items = grad_h.reshape(item_count, SEQ, D)
    grad_shift_mlp = jnp.sum(grad_h_items, 1)
    grad_scale_mlp = jnp.sum(grad_h_items * normed_mlp, 1)
    grad_mid = grad_y + norm_back(grad_h_items * (1.0 + scale_mlp), normed_mlp, factor_mlp)
    grad_gate_attn = jnp.sum(grad_mid * attn_out, 1)
    g_attn = (gate_attn * grad_mid).astype(jnp.bfloat16).reshape(token_count, D)
    grad_w_out = jnp.einsum("td,te->de", heads_low, g_attn, preferred_element_type=jnp.float32)
    g_heads = (
        jnp.einsum("te,de->td", g_attn, out_weight, preferred_element_type=jnp.float32)
        .astype(jnp.bfloat16)
        .reshape(item_count, SEQ, HEADS, HEAD_DIM)
    )
    scores_again = attention_scores(queries, keys_all, key_mask, scale_qk)
    probs_again = jnp.exp(scores_again - log_total)
    grad_values = jnp.einsum(
        "ihqk,iqhd->ikhd",
        probs_again.astype(jnp.bfloat16),
        g_heads,
        preferred_element_type=jnp.float32,
    )
    g_probs = jnp.einsum("iqhd,ikhd->ihqk", g_heads, values_all, preferred_element_type=jnp.float32)
    g_scores = (probs_again * (g_probs - jnp.sum(probs_again * g_probs, -1, keepdims=True))).astype(
        jnp.bfloat16
    )
    grad_queries = (
        jnp.einsum("ihqk,ikhd->iqhd", g_scores, keys_all, preferred_element_type=jnp.float32)
        * scale_qk
    )
    grad_keys = (
        jnp.einsum("ihqk,iqhd->ikhd", g_scores, queries, preferred_element_type=jnp.float32)
        * scale_qk
    )
    g_qkv = (
        jnp.stack([grad_queries, grad_keys, grad_values], 2)
        .astype(jnp.bfloat16)
        .reshape(token_count, 3 * D)
    )
    grad_w_qkv = jnp.einsum("td,te->de", h_attn, g_qkv, preferred_element_type=jnp.float32)
    g_h_attn = jnp.einsum(
        "te,de->td", g_qkv, qkv_weight, preferred_element_type=jnp.float32
    ).reshape(item_count, SEQ, D)
    grad_shift_attn = jnp.sum(g_h_attn, 1)
    grad_scale_attn = jnp.sum(g_h_attn * normed_attn, 1)
    grad_input = grad_mid + norm_back(g_h_attn * (1.0 + scale_attn), normed_attn, factor_attn)
    grad_mod = jnp.stack(
        [
            grad_shift_attn,
            grad_scale_attn,
            grad_gate_attn,
            grad_shift_mlp,
            grad_scale_mlp,
            grad_gate_mlp,
        ],
        1,
    ).reshape(item_count, 6 * D)
    grad_w_ada = jnp.dot(cond_act.astype(jnp.float32).T, grad_mod, precision=lax.Precision.HIGHEST)
    dense_grads = (grad_w_ada, grad_w_qkv, grad_w_out, grad_w_router, grad_w_sh1, grad_w_sh2)
    partial_sums = (
        lax.psum_scatter(dense_grads[0], "batch", scatter_dimension=0, tiled=True),
        lax.psum_scatter(dense_grads[1], "batch", scatter_dimension=0, tiled=True),
        lax.psum_scatter(dense_grads[2], "batch", scatter_dimension=0, tiled=True),
        lax.psum_scatter(dense_grads[3], "batch", scatter_dimension=0, tiled=True),
        lax.psum_scatter(dense_grads[4], "batch", scatter_dimension=0, tiled=True),
        lax.psum_scatter(dense_grads[5], "batch", scatter_dimension=0, tiled=True),
    )
    reduced = (
        lax.psum_scatter(partial_sums[0], "expert", scatter_dimension=1, tiled=True),
        lax.psum_scatter(partial_sums[1], "expert", scatter_dimension=1, tiled=True),
        lax.psum_scatter(partial_sums[2], "expert", scatter_dimension=1, tiled=True),
        lax.psum_scatter(partial_sums[3], "expert", scatter_dimension=1, tiled=True),
        lax.psum_scatter(partial_sums[4], "expert", scatter_dimension=1, tiled=True),
        lax.psum_scatter(partial_sums[5], "expert", scatter_dimension=1, tiled=True),
    )
    expert_sums = (
        lax.psum_scatter(grad_w_e1, "batch", scatter_dimension=1, tiled=True),
        lax.psum_scatter(grad_w_e2, "batch", scatter_dimension=1, tiled=True),
    )
    return (
        result,
        grad_input.reshape(token_count, D),
        reduced[0],
        reduced[1],
        reduced[2],
        reduced[3],
        reduced[4],
        reduced[5],
        expert_sums[0],
        expert_sums[1],
    )


def solution(mesh):
    placed = (
        P(("batch", "expert"), None),
        P(("batch", "expert"), None),
        P(("batch", "expert")),
        P(("batch", "expert"), None),
        P(("batch", "expert"), None),
        P(),
        P(),
        P(),
        P(),
        P(),
        P(),
        P("expert", None, None),
        P("expert", None, None),
    )
    return jax.shard_map(
        per_device,
        mesh=mesh,
        in_specs=placed,
        out_specs=(
            P(("batch", "expert"), None),
            P(("batch", "expert"), None),
            P("batch", "expert"),
            P("batch", "expert"),
            P("batch", "expert"),
            P("batch", "expert"),
            P("batch", "expert"),
            P("batch", "expert"),
            P("expert", "batch", None),
            P("expert", "batch", None),
        ),
        check_vma=False,
    )
```

profile of v0, /device:TPU:0, one launch (start us, length us, event | category | flops | bytes accessed | tf_op | source)
XLA Modules:
  0.0 2148.6 jit_solution(755846030988849100)
XLA Ops:
  14.1 4.7 fusion.72
  29.3 5.4 convolution_convert_fusion
  34.7 6.7 copy.167
  41.4 8.9 reshape.459
  50.2 4.7 fusion.75
  55.0 4.8 fusion.16
  67.9 4.1 multiply_add_fusion.4
  100.6 5.1 reduce-window.6
  116.4 4.6 mul.461
  121.0 8.5 mul.462
  137.6 8.2 scatter_custom_fusion
  146.4 12.3 gather_fusion
  159.3 9.1 scatter_custom_fusion.1
  171.7 4.8 multiply_convert_fusion.3
  176.6 12.4 gather_fusion.2
  188.9 4.3 broadcast_multiply_fusion
  193.2 41.0 %all_to_all.20 = bf16[4,2,256,768]{3,2,1,0:T(8,128)(2,1)} all-to-all(bf16[4,2,256,768]{3,2,1,0:T(8,128)(2,1)S(1)} %get-tuple-element.99), channel_id=1, replica_groups=mesh['batch'=8,'expert'=4] {'expert'}, dimensions={0} | all-to-all | bytes 6291456 | tf_op jit(solution)/shard_map/all_to_all | solution.py:148
  234.2 4.7 all-to-all-start.2
  238.9 10.3 fusion.77
  249.2 16.9 fusion.19
  266.1 9.9 all-to-all-done.2
  275.9 28.6 %fusion.6 = bf16[4,2,256,3072]{3,2,0,1:T(8,128)(2,1)} fusion(f32[2,4,256,3072]{3,2,1,0:T(8,128)} %fusion.19, bf16[2,3072,768]{2,1,0:T(8,128)(2,1)} %param.25, bf16[4,2,256,768]{3,2,1,0:T(8,128)(2,1)} %all-to-all-done.2), kind=kOutput, calls=%fused_computation.14 | convolution fusion | flops 9783214080 | bytes 50331648 | tf_op jit(solution)/shard_map/sjcd,jfd->sjcf/dot_general | solution.py:191
  304.6 15.8 convert_bitcast_fusion
  322.3 4.6 all-to-all-start.3
  327.0 18.8 convert_bitcast_fusion.1
  347.7 16.2 all-to-all-done.3
  364.0 4.7 all-to-all-start.1
  368.7 17.0 fusion.13
  392.4 9.1 fusion.79
  401.5 12.4 gather_fusion.3
  413.9 8.2 reshape.529
  422.1 12.4 gather_fusion.1
  434.5 7.8 reshape.528
  442.3 37.8 %multiply_reduce_fusion.1 = (f32[1024,2]{1,0:T(8,128)}, f32[1024,768]{1,0:T(8,128)S(1)}, f32[1024,768]{1,0:T(8,128)}) fusion(f32[1024,2,768]{2,1,0:T(2,128)} %reshape.528, f32[1024,768]{1,0:T(8,128)} %copy-done.11, f32[1024,2]{1,0:T(8,128)} %fusion.74, f32[1024,2]{1,0:T(8,128)} %copy.173, f32[1024,2,768]{2,1,0:T(2,128)} %reshape.529), kind=kLoop, calls=%fused_computation.46 | loop fusion | flops 9435136 | bytes 22044672 | tf_op jit(solution)/shard_map/reduce_sum | solution.py:177
  480.1 14.1 multiply_reduce_fusion.4
  498.3 4.9 fusion.30
  507.8 8.1 multiply_reduce_fusion.5
  528.0 4.7 fusion.81
  532.8 11.4 multiply_reduce_fusion
  544.3 8.1 multiply_convert_fusion.1
  557.9 4.0 convolution_bitcast_fusion.1
  564.0 4.6 copy.195
  570.1 6.0 fusion.80
  576.2 10.1 fusion.83
  586.3 13.9 fusion.46
  604.5 7.3 multiply_reduce_fusion.11
  611.9 8.9 fusion.70
  621.0 3.9 fusion.82
  627.0 109.1 %reduce-scatter.26.cloned.1.call-done = f32[96,2304]{1,0:T(8,128)} async-done(((f32[768,2304]{1,0:T(8,128)}), f32[96,2304]{1,0:T(8,128)}) %reduce-scatter.26.cloned.1.call-update) | async-done | bytes 884752 | tf_op jit(solution)/shard_map/reduce_scatter | solution.py:270
  738.8 163.9 %reduce-scatter.30.cloned.1.call-done = f32[96,3072]{1,0:T(8,128)} async-done(((f32[768,3072]{1,0:T(8,128)}), f32[96,3072]{1,0:T(8,128)}) %reduce-scatter.30.cloned.1.call-update) | async-done | bytes 1179664 | tf_op jit(solution)/shard_map/reduce_scatter | solution.py:273
  902.8 166.2 %reduce-scatter.34.cloned.1.call-done = f32[384,768]{1,0:T(8,128)} async-done(((f32[3072,768]{1,0:T(8,128)}), f32[384,768]{1,0:T(8,128)}) %reduce-scatter.34.cloned.1.call-update) | async-done | bytes 1179664 | tf_op jit(solution)/shard_map/reduce_scatter | solution.py:274
  1071.8 229.5 %reduce-scatter.22.cloned.1.call-done = f32[96,4608]{1,0:T(8,128)} async-done(((f32[768,4608]{1,0:T(8,128)}), f32[96,4608]{1,0:T(8,128)}) %reduce-scatter.22.cloned.1.call-update) | async-done | bytes 1769488 | tf_op jit(solution)/shard_map/reduce_scatter | solution.py:269
  1301.4 17.6 fusion.24
  1319.3 25.0 %convolution_bitcast_fusion = f32[2,3072,768]{2,1,0:T(8,128)} fusion(bf16[4,2,256,768]{3,2,1,0:T(8,128)(2,1)} %all-to-all-done.2, f32[2,4,256,3072]{3,2,1,0:T(8,128)} %fusion.19), kind=kOutput, calls=%fused_computation.44 | convolution fusion | flops 9720299520 | bytes 47185920 | tf_op jit(solution)/shard_map/sjcf,sjcd->jfd/dot_general | solution.py:187
  1347.6 5.0 multiply_add_fusion.2
  1352.6 12.7 reduce-scatter.44.cloned.1.call-done
  1366.1 5.6 all-reduce
  1372.4 15.4 reduce-scatter.42.cloned.1.call-done
  1389.4 26.8 %reduce-scatter.40.cloned.1.call-done = f32[576,96]{1,0:T(8,128)} async-done(((f32[2304,96]{1,0:T(8,128)}), f32[576,96]{1,0:T(8,128)}) %reduce-scatter.40.cloned.1.call-update) | async-done | bytes 221200
  1418.1 27.1 %reduce-scatter.32.cloned.1.call-done = f32[96,768]{1,0:T(8,128)} async-done(((f32[96,3072]{1,0:T(8,128)}), f32[96,768]{1,0:T(8,128)}) %reduce-scatter.32.cloned.1.call-update) | async-done | bytes 294928 | tf_op jit(solution)/shard_map/reduce_scatter | solution.py:281
  1445.1 28.9 %reduce-scatter.46.cloned.1.call-done = f32[192,384]{1,0:T(8,128)} async-done(((f32[768,384]{1,0:T(8,128)}), f32[192,384]{1,0:T(8,128)}) %reduce-scatter.46.cloned.1.call-update) | async-done | bytes 294928
  1474.0 32.6 %reduce-scatter.24.cloned.1.call-done = f32[96,1152]{1,0:T(8,128)} async-done(((f32[96,4608]{1,0:T(8,128)}), f32[96,1152]{1,0:T(8,128)}) %reduce-scatter.24.cloned.1.call-update) | async-done | bytes 442384 | tf_op jit(solution)/shard_map/reduce_scatter | solution.py:277
  1506.6 317.6 %reduce-scatter.36.cloned.1.call-done = f32[2,96,3072]{2,1,0:T(8,128)} async-done(((f32[2,768,3072]{2,1,0:T(8,128)}), f32[2,96,3072]{2,1,0:T(8,128)}) %reduce-scatter.36.cloned.1.call-update) | async-done | bytes 2359312 | tf_op jit(solution)/shard_map/reduce_scatter | solution.py:285
  1824.2 317.4 %reduce-scatter.38.cloned.1.call-done = f32[2,384,768]{2,1,0:T(8,128)} async-done(((f32[2,3072,768]{2,1,0:T(8,128)}), f32[2,384,768]{2,1,0:T(8,128)}) %reduce-scatter.38.cloned.1.call-update) | async-done | bytes 2359312 | tf_op jit(solution)/shard_map/reduce_scatter | solution.py:286
  (270 shorter events, 137.4 us)
Async XLA Ops:
  7.2 22.1 %copy-start = (bf16[768,2304]{1,0:T(8,128)(2,1)S(1)}, bf16[768,2304]{1,0:T(8,128)(2,1)}, u32[]{:S(2)}) copy-start(bf16[768,2304]{1,0:T(8,128)(2,1)} %param.19) | copy-start | bytes 10616836
  20.4 7.0 copy-start.7
  24.1 3.3 copy-start.44
  50.2 4.7 copy-start.64
  55.0 8.8 copy-start.32
  55.0 55.4 %copy-start.59 = (pred[1024]{0:T(1024)(128)(4,1)}, pred[1024]{0:T(1024)(128)(4,1)S(1)}, u32[]{:S(2)}) copy-start(pred[1024]{0:T(1024)(128)(4,1)S(1)} %lt.76) | copy-start | bytes 3076
  59.9 4.7 copy-start.2
  59.9 4.7 copy-start.14
  63.8 4.1 copy-start.25
  64.6 3.3 copy-start.8
  64.6 3.3 copy-start.23
  64.6 3.3 copy-start.36
  67.9 4.2 copy-start.16
  72.1 6.1 copy-start.51
  74.8 3.4 copy-start.52
  74.8 3.4 copy-start.3
  75.6 3.8 copy-start.38
  81.2 33.6 %copy-start.30 = (f32[1024,2]{0,1:T(2,128)}, f32[1024,2]{0,1:T(2,128)S(1)}, u32[]{:S(2)}) copy-start(f32[1024,2]{0,1:T(2,128)S(1)} %select_reduce_fusion.1) | copy-start | bytes 24580
  81.2 33.6 %copy-start.40 = (f32[1024]{0:T(1024)}, f32[1024]{0:T(1024)S(1)}, u32[]{:S(2)}) copy-start(f32[1024]{0:T(1024)S(1)} %reduce_max.19) | copy-start | bytes 12292
  121.0 10.7 copy-start.56
  146.4 24.6 %copy-start.57 = (f32[2048]{0:T(1024)S(1)}, f32[2048]{0:T(1024)}, u32[]{:S(2)}) copy-start(f32[2048]{0:T(1024)} %div.73) | copy-start | bytes 24580
  171.7 4.8 copy-start.58
  176.6 12.4 copy-start.62
  234.2 41.7 %all-to-all-start.2 = ((bf16[4,2,256,768]{3,2,1,0:T(8,128)(2,1)}), bf16[4,2,256,768]{3,2,1,0:T(8,128)(2,1)}, u32[]{:S(2)}, u32[]{:S(2)}) async-start(bf16[4,2,256,768]{3,2,1,0:T(8,128)(2,1)} %get-tuple-element.98), calls=%async_computation.2 | async-start | bytes 6291456 | tf_op jit(solution)/shard_map/all_to_all | solution.py:184
  238.9 10.3 copy-start.18
  322.3 41.6 %all-to-all-start.3 = ((bf16[4,2,256,768]{3,2,1,0:T(8,128)(2,1)}), bf16[4,2,256,768]{3,2,1,0:T(8,128)(2,1)}, u32[]{:S(2)}, u32[]{:S(2)}) async-start(bf16[4,2,256,768]{3,2,1,0:T(8,128)(2,1)} %copy.184), calls=%async_computation.3 | async-start | bytes 6291456 | tf_op jit(solution)/shard_map/all_to_all | solution.py:198
  364.0 58.1 %all-to-all-start.1 = ((bf16[4,2,256,768]{3,2,1,0:T(8,128)(2,1)}), bf16[4,2,256,768]{3,2,1,0:T(8,128)(2,1)}, u32[]{:S(2)}, u32[]{:S(2)}) async-start(bf16[4,2,256,768]{3,2,1,0:T(8,128)(2,1)} %copy.181), calls=%async_computation.1 | async-start | bytes 6291456 | tf_op jit(solution)/shard_map/all_to_all | solution.py:159
  368.6 256.4 %reduce-scatter.28.cloned.1.call-start = ((), (), s32[]{:S(2)}) async-start(), calls=%async_computation.20 | async-start | bytes 2654208 | tf_op jit(solution)/shard_map/reduce_scatter | solution.py:271
  387.0 4.4 copy-start.17
  387.0 4.4 copy-start.60
  387.1 5.3 copy-start.65
  442.3 37.8 %copy-start.21 = (bf16[1024,768]{1,0:T(8,128)(2,1)S(1)}, bf16[1024,768]{1,0:T(8,128)(2,1)}, u32[]{:S(2)}) copy-start(bf16[1024,768]{1,0:T(8,128)(2,1)} %param.17) | copy-start | bytes 4718596
  480.1 16.0 copy-start.41
  480.1 18.2 copy-start.28
  498.3 5.0 copy-start.29
  498.3 5.0 copy-start.4
  498.3 5.0 copy-start.39
  498.3 5.0 copy-start.43
  507.8 9.8 copy-start.37
  528.0 4.7 copy-start.33
  532.7 203.4 %reduce-scatter.26.cloned.1.call-start = ((), (), s32[]{:S(2)}) async-start(), calls=%async_computation.19 | async-start | bytes 7962624 | tf_op jit(solution)/shard_map/reduce_scatter | solution.py:270
  532.8 11.4 copy-start.26
  544.2 8.2 copy-start.13
  544.2 9.2 copy-start.12
  552.4 3.5 slice-start.1
  553.4 4.0 slice-start.2
  553.4 4.5 copy-start.15
  564.0 4.6 copy-start.6
  576.1 326.5 %reduce-scatter.30.cloned.1.call-start = ((), (), s32[]{:S(2)}) async-start(), calls=%async_computation.21 | async-start | bytes 10616832 | tf_op jit(solution)/shard_map/reduce_scatter | solution.py:273
  586.3 482.7 %reduce-scatter.34.cloned.1.call-start = ((), (), s32[]{:S(2)}) async-start(), calls=%async_computation.23 | async-start | bytes 10616832 | tf_op jit(solution)/shard_map/reduce_scatter | solution.py:274
  600.2 701.1 %reduce-scatter.22.cloned.1.call-start = ((), (), s32[]{:S(2)}) async-start(), calls=%async_computation.17 | async-start | bytes 15925248 | tf_op jit(solution)/shard_map/reduce_scatter | solution.py:269
  604.4 7.4 copy-start.50
  604.4 7.4 copy-start.49
  604.4 7.4 copy-start.48
  604.4 7.4 copy-start.63
  604.5 7.4 copy-start.55
  620.8 744.5 %reduce-scatter.44.cloned.1.call-start = ((), (), s32[]{:S(2)}) async-start(), calls=%async_computation.28 | async-start | bytes 442368
  625.0 762.8 %reduce-scatter.42.cloned.1.call-start = ((), (), s32[]{:S(2)}) async-start(), calls=%async_computation.27 | async-start | bytes 491520
  627.0 789.3 %reduce-scatter.40.cloned.1.call-start = ((), (), s32[]{:S(2)}) async-start(), calls=%async_computation.26 | async-start | bytes 1474560
  738.7 706.4 %reduce-scatter.32.cloned.1.call-start = ((), (), s32[]{:S(2)}) async-start(), calls=%async_computation.22 | async-start | bytes 1474560 | tf_op jit(solution)/shard_map/reduce_scatter | solution.py:281
  902.7 571.3 %reduce-scatter.46.cloned.1.call-start = ((), (), s32[]{:S(2)}) async-start(), calls=%async_computation.29 | async-start | bytes 1474560
  1071.7 434.9 %reduce-scatter.24.cloned.1.call-start = ((), (), s32[]{:S(2)}) async-start(), calls=%async_computation.18 | async-start | bytes 2211840 | tf_op jit(solution)/shard_map/reduce_scatter | solution.py:277
  1301.3 522.9 %reduce-scatter.36.cloned.1.call-start = ((), (), s32[]{:S(2)}) async-start(), calls=%async_computation.24 | async-start | bytes 21233664 | tf_op jit(solution)/shard_map/reduce_scatter | solution.py:285
  1319.0 822.6 %reduce-scatter.38.cloned.1.call-start = ((), (), s32[]{:S(2)}) async-start(), calls=%async_computation.25 | async-start | bytes 21233664 | tf_op jit(solution)/shard_map/reduce_scatter | solution.py:286
  (21 other events, 40.3 us)
Sparse Core Ops, SparseCore 0:
  532.9 71.4 reduce-scatter.27
  608.1 128.0 reduce-scatter.25
  740.1 162.5 reduce-scatter.29
  906.6 162.3 reduce-scatter.33
  1072.9 228.3 reduce-scatter.21
  1304.8 60.4 reduce-scatter.43
  1367.9 19.8 reduce-scatter.41
  1390.5 25.6 reduce-scatter.39
  1419.4 25.6 reduce-scatter.31
  1448.3 25.7 reduce-scatter.45
  1477.2 29.3 reduce-scatter.23
  1511.4 312.7 reduce-scatter.35
  1829.2 312.3 reduce-scatter.37
where the time goes:
time: 2160 us; the launch traced here: 2150 us
  waiting for transfers between devices  1470 us (68%)
  matrix products  277 us (13%)
  local copies, waits for them, and re-layouts  204 us (9%)
  other arithmetic  117 us (5%)
  blocking collectives  46.7 us (2%)
    reduce_scatter x1, waiting for transfers between devices, per_device(): lax.psum_scatter(grad_w_e1, 'batch', scatter_dimension=1, tiled=True)  318 us
    reduce_scatter x1, waiting for transfers between devices, per_device(): lax.psum_scatter(grad_w_e2, 'batch', scatter_dimension=1, tiled=True)  317 us
    reduce_scatter x1, waiting for transfers between devices, per_device(): lax.psum_scatter(dense_grads[0], 'batch', scatter_dimension=0, tiled=True)  230 us
    reduce_scatter x1, waiting for transfers between devices, per_device(): lax.psum_scatter(dense_grads[5], 'batch', scatter_dimension=0, tiled=True)  166 us
    reduce_scatter x1, waiting for transfers between devices, per_device(): lax.psum_scatter(dense_grads[4], 'batch', scatter_dimension=0, tiled=True)  164 us
    reduce_scatter x1, waiting for transfers between devices, per_device(): lax.psum_scatter(dense_grads[1], 'batch', scatter_dimension=0, tiled=True)  109 us
    unnamed x17, waiting for transfers between devices  84.1 us
  transfers between devices with their start and end apart: 16, of which 14 were waited for; matrix products, arithmetic and copies ran while one was open for 12% of the time, Pallas kernels for 0%

commit v1 on v0

--- a/solution.py
+++ b/solution.py
@@ -49,6 +49,71 @@
         * scale_qk
     )
     return jnp.where(key_mask, raw_scores, MASKED)
+
+
+def axis_split(size):
+    inner = 2 if size <= 8 else 8
+    return (size // inner, inner)
+
+
+def group_sum(blocks, axis, groups):
+    width = len(groups[0])
+    if width == 1:
+        return blocks[0].astype(jnp.float32)
+    low = blocks.astype(jnp.bfloat16)
+    if width == 2:
+        pairs = [(g[0], g[1]) for g in groups] + [(g[1], g[0]) for g in groups]
+        place = jnp.zeros((), jnp.int32)
+        index = lax.axis_index(axis)
+        for g in groups:
+            place = jnp.where(index == g[1], 1, place)
+        sent = lax.dynamic_index_in_dim(low, 1 - place, 0, keepdims=False)
+        kept = lax.dynamic_index_in_dim(low, place, 0, keepdims=False)
+        got = lax.ppermute(sent, axis, pairs)
+        return kept.astype(jnp.float32) + got.astype(jnp.float32)
+    got = lax.all_to_all(low, axis, 0, 0, tiled=True, axis_index_groups=groups)
+    return jnp.sum(got.astype(jnp.float32), 0)
+
+
+def inner_groups(outer, inner):
+    return [[o * inner + i for i in range(inner)] for o in range(outer)]
+
+
+def outer_groups(outer, inner):
+    return [[o * inner + i for o in range(outer)] for i in range(inner)]
+
+
+def reduce_batch(blocks):
+    size = lax.axis_size("batch")
+    outer, inner = axis_split(size)
+    rest = blocks.shape[1:]
+    v = jnp.moveaxis(blocks.reshape((outer, inner) + rest), 1, 0)
+    v = group_sum(v, "batch", inner_groups(outer, inner))
+    return group_sum(v, "batch", outer_groups(outer, inner))
+
+
+def reduce_expert(blocks):
+    size = lax.axis_size("expert")
+    outer, inner = size // 2, 2
+    rest = blocks.shape[1:]
+    v = jnp.moveaxis(blocks.reshape((outer, inner) + rest), 1, 0)
+    v = group_sum(v, "expert", inner_groups(outer, inner))
+    return group_sum(v, "expert", outer_groups(outer, inner))
+
+
+def reduce_dense(grad):
+    nb, ne = lax.axis_size("batch"), lax.axis_size("expert")
+    r, c = grad.shape
+    v = jnp.transpose(grad.astype(jnp.bfloat16).reshape(r, ne, c // ne), (1, 0, 2))
+    v = reduce_expert(v)
+    return reduce_batch(v.reshape(nb, r // nb, c // ne))
+
+
+def reduce_local(grad):
+    nb = lax.axis_size("batch")
+    n, r, c = grad.shape
+    v = jnp.transpose(grad.astype(jnp.bfloat16).reshape(n, nb, r // nb, c), (1, 0, 2, 3))
+    return reduce_batch(v)
 
 
 def per_device(
@@ -263,28 +328,33 @@
         ],
         1,
     ).reshape(item_count, 6 * D)
-    grad_w_ada = jnp.dot(cond_act.astype(jnp.float32).T, grad_mod, precision=lax.Precision.HIGHEST)
-    dense_grads = (grad_w_ada, grad_w_qkv, grad_w_out, grad_w_router, grad_w_sh1, grad_w_sh2)
-    partial_sums = (
-        lax.psum_scatter(dense_grads[0], "batch", scatter_dimension=0, tiled=True),
-        lax.psum_scatter(dense_grads[1], "batch", scatter_dimension=0, tiled=True),
-        lax.psum_scatter(dense_grads[2], "batch", scatter_dimension=0, tiled=True),
-        lax.psum_scatter(dense_grads[3], "batch", scatter_dimension=0, tiled=True),
-        lax.psum_scatter(dense_grads[4], "batch", scatter_dimension=0, tiled=True),
-        lax.psum_scatter(dense_grads[5], "batch", scatter_dimension=0, tiled=True),
+    nb = lax.axis_size("batch")
+    ada_cols = grad_mod.shape[1] // groups
+    mod_parts = jnp.transpose(grad_mod.reshape(item_count, groups, ada_cols), (1, 0, 2))
+    mod_mine = lax.all_to_all(mod_parts, "expert", 0, 0, tiled=True).reshape(
+        groups * item_count, ada_cols
+    )
+    mod_all = lax.all_gather(mod_mine, "batch", axis=0, tiled=True)
+    act_all = lax.all_gather(cond_act, ("batch", "expert"), axis=0, tiled=True)
+    ada_rows = D // nb
+    act_mine = lax.dynamic_slice_in_dim(act_all, lax.axis_index("batch") * ada_rows, ada_rows, 1)
+    grad_ada = jnp.dot(
+        act_mine.astype(jnp.float32).T, mod_all, precision=lax.Precision.HIGHEST
     )
     reduced = (
-        lax.psum_scatter(partial_sums[0], "expert", scatter_dimension=1, tiled=True),
-        lax.psum_scatter(partial_sums[1], "expert", scatter_dimension=1, tiled=True),
-        lax.psum_scatter(partial_sums[2], "expert", scatter_dimension=1, tiled=True),
-        lax.psum_scatter(partial_sums[3], "expert", scatter_dimension=1, tiled=True),
-        lax.psum_scatter(partial_sums[4], "expert", scatter_dimension=1, tiled=True),
-        lax.psum_scatter(partial_sums[5], "expert", scatter_dimension=1, tiled=True),
-    )
-    expert_sums = (
-        lax.psum_scatter(grad_w_e1, "batch", scatter_dimension=1, tiled=True),
-        lax.psum_scatter(grad_w_e2, "batch", scatter_dimension=1, tiled=True),
-    )
+        grad_ada,
+        reduce_dense(grad_w_qkv),
+        reduce_dense(grad_w_out),
+        lax.psum_scatter(
+            lax.psum_scatter(grad_w_router, "batch", scatter_dimension=0, tiled=True),
+            "expert",
+            scatter_dimension=1,
+            tiled=True,
+        ),
+        reduce_dense(grad_w_sh1),
+        reduce_dense(grad_w_sh2),
+    )
+    expert_sums = (reduce_local(grad_w_e1), reduce_local(grad_w_e2))
     return (
         result,
         grad_input.reshape(token_count, D),

time: 2160 us -> 1210 us (0.56)
  waiting for transfers between devices: 1470 us -> 240 us
  blocking collectives: 46.7 us -> 158 us
  local copies, waits for them, and re-layouts: 204 us -> 282 us
  other arithmetic: 117 us -> 182 us
  starting transfers between devices: 14.9 us -> 66.4 us
  matrix products: 277 us -> 251 us
    reduce_scatter x9 -> x0, waiting for transfers between devices: 1360 us -> none  [the longest x1 318 us: per_device(): lax.psum_scatter(grad_w_e1, 'batch', scatter_dimension=1, tiled=True)]
    all_gather x0 -> x2, blocking collectives: none -> 152 us  [the longest x1 120 us: per_device(): act_all = lax.all_gather(cond_act, ('batch', 'expert'), axis=0, tiled=True)]
    ppermute x0 -> x14, waiting for transfers between devices: none -> 126 us  [group_sum(): got = lax.ppermute(sent, axis, pairs)]
    all_to_all x1 -> x0, blocking collectives: 41 us -> none  [per_device(): lax.all_to_all(send_rows, 'expert', split_axis=0, concat_axis=0, tiled=True)]
    all_to_all x0 -> x8, starting transfers between devices: none -> 37.4 us  [the longest x6 28.8 us: group_sum(): got = lax.all_to_all(low, axis, 0, 0, tiled=True, axis_index_groups=groups)]
    convert_element_type x0 -> x14, other arithmetic: none -> 35.8 us  [group_sum(): low = blocks.astype(jnp.bfloat16)]
    squeeze x0 -> x14, local copies, waits for them, and re-layouts: none -> 25.8 us  [group_sum(): sent = lax.dynamic_index_in_dim(low, 1 - place, 0, keepdims=False)]
    unnamed x17 -> x2, waiting for transfers between devices: 84.1 us -> 60.1 us
  transfers between devices with their start and end apart: 16 -> 26, of which waited for: 14 -> 8; matrix products, arithmetic and copies ran while one was open for 12% -> 42% of each run, Pallas kernels for 0% -> 0%
where the time goes in v1:
time: 1210 us; the launch traced here: 1200 us
  local copies, waits for them, and re-layouts  282 us (23%)
  matrix products  251 us (21%)
  waiting for transfers between devices  240 us (20%)
  other arithmetic  182 us (15%)
  blocking collectives  158 us (13%)
  starting transfers between devices  66.4 us (5%)
  between operations  16.3 us (1%)
    ppermute x14, waiting for transfers between devices, group_sum(): got = lax.ppermute(sent, axis, pairs)  126 us
    all_gather x1, blocking collectives, per_device(): act_all = lax.all_gather(cond_act, ('batch', 'expert'), axis=0, tiled=True)  120 us
    unnamed x2, waiting for transfers between devices  60.1 us
    reduce_sum x1, other arithmetic, per_device(): g_gate = jnp.sum(grad_mlp[:, None, :] * pair_rows, -1)  38 us
    convert_element_type x14, other arithmetic, group_sum(): low = blocks.astype(jnp.bfloat16)  35.8 us
    unnamed x167, local copies, waits for them, and re-layouts  34.9 us
    all_gather x1, blocking collectives, per_device(): mod_all = lax.all_gather(mod_mine, 'batch', axis=0, tiled=True)  31.7 us
    all_to_all x1, waiting for transfers between devices, per_device(): lax.all_to_all(send_grad, 'expert', split_axis=0, concat_axis=0, tiled=True)  29.8 us
  transfers between devices with their start and end apart: 26, of which 8 were waited for; matrix products, arithmetic and copies ran while one was open for 42% of the time, Pallas kernels for 0%

profile of v1, /device:TPU:0, one launch (start us, length us, event | category | flops | bytes accessed | tf_op | source)
XLA Modules:
  0.0 1195.8 jit_solution(9637182771565097979)
XLA Ops:
  14.2 4.7 fusion.85
  29.3 5.5 convolution_convert_fusion
  34.7 6.7 copy.283
  41.4 8.9 reshape.571
  50.3 4.6 fusion.88
  55.6 4.8 fusion.16
  101.9 5.1 reduce-window.6
  123.1 8.5 mul.465
  141.8 8.8 scatter_custom_fusion
  151.8 12.3 %gather_fusion = bf16[2048,768]{1,0:T(8,128)(2,1)} fusion(bf16[1024,768]{1,0:T(8,128)(2,1)} %bitcast.307, s32[2048]{0:T(1024)} %get-tuple-element.81), kind=kCustom, calls=%fused_computation | custom fusion | bytes 6299648 | tf_op jit(solution)/shard_map/gather | solution.py:212
  164.7 8.8 scatter_custom_fusion.1
  176.8 4.8 multiply_convert_fusion.3
  181.6 12.6 %gather_fusion.2 = bf16[2048,768]{1,0:T(8,128)(2,1)} fusion(bf16[2048,768]{1,0:T(8,128)(2,1)} %multiply_convert_fusion.3, s32[2048]{0:T(1024)S(1)} %copy-done.67), kind=kCustom, calls=%fused_computation.2 | custom fusion | bytes 6299648 | tf_op jit(solution)/shard_map/gather | solution.py:248
  194.2 4.8 broadcast_multiply_fusion
  199.0 4.7 all-to-all-start
  203.7 7.5 fusion.90
  215.7 7.2 convolution_convert_fusion.1
  226.7 14.2 %fusion.13 = bf16[1024,3072]{1,0:T(8,128)(2,1)S(1)} fusion(f32[1024,3072]{1,0:T(8,128)} %copy-done.74, bf16[3072,768]{1,0:T(8,128)(2,1)} %param.23, f32[1024,768]{1,0:T(8,128)S(1)} %copy-done.16), kind=kOutput, calls=%fused_computation.27 | convolution fusion | flops 4892393472 | bytes 26738688 | tf_op jit(solution)/shard_map/td,fd->tf/dot_general | solution.py:237
  241.0 5.8 convolution_convert_fusion.2
  260.4 9.8 fusion.92
  278.8 4.7 all-to-all-start.2
  290.9 18.9 %fusion.21 = f32[2,4,256,3072]{3,2,1,0:T(8,128)} fusion(bf16[2,768,3072]{2,1,0:T(8,128)(2,1)} %param.24, bf16[4,2,256,768]{3,2,1,0:T(8,128)(2,1)} %all-to-all-done), kind=kOutput, calls=%fused_computation.44 | convolution fusion | flops 9663676416 | bytes 37748736 | tf_op jit(solution)/shard_map/sjcd,jdf->sjcf/dot_general | solution.py:214
  309.8 29.8 %all-to-all-done.2 = bf16[4,2,256,768]{3,2,1,0:T(8,128)(2,1)} async-done(((bf16[4,2,256,768]{3,2,1,0:T(8,128)(2,1)}), bf16[4,2,256,768]{3,2,1,0:T(8,128)(2,1)}, u32[]{:S(2)}, u32[]{:S(2)}) %all-to-all-start.2) | async-done | bytes 3145760 | tf_op jit(solution)/shard_map/all_to_all | solution.py:249
  339.6 28.7 %fusion.6 = bf16[4,2,256,3072]{3,2,0,1:T(8,128)(2,1)} fusion(f32[2,4,256,3072]{3,2,1,0:T(8,128)} %fusion.21, bf16[2,3072,768]{2,1,0:T(8,128)(2,1)} %param.25, bf16[4,2,256,768]{3,2,1,0:T(8,128)(2,1)} %all-to-all-done.2), kind=kOutput, calls=%fused_computation.14 | convolution fusion | flops 9783214080 | bytes 50331648 | tf_op jit(solution)/shard_map/sjcd,jfd->sjcf/dot_general | solution.py:256
  368.3 15.8 %convert_bitcast_fusion = bf16[4,2,256,768]{3,2,0,1:T(8,128)(2,1)S(1)} fusion(bf16[4,2,256,3072]{3,2,0,1:T(8,128)(2,1)} %fusion.6, bf16[2,768,3072]{2,1,0:T(8,128)(2,1)} %param.24), kind=kOutput, calls=%fused_computation.93 | convolution fusion | flops 9665249280 | bytes 25165824 | tf_op jit(solution)/shard_map/sjcf,jdf->sjcd/dot_general | solution.py:260
  386.0 4.7 all-to-all-start.3
  390.7 18.8 %convert_bitcast_fusion.1 = bf16[4,2,256,768]{3,2,0,1:T(8,128)(2,1)S(1)} fusion(bf16[2,3072,768]{2,1,0:T(8,128)(2,1)} %param.25, f32[2,4,256,3072]{3,2,1,0:T(8,128)} %fusion.21), kind=kOutput, calls=%fused_computation.95 | convolution fusion | flops 9721872384 | bytes 37748736 | tf_op jit(solution)/shard_map/sjcf,jfd->sjcd/dot_general | solution.py:218
  411.4 16.3 %all-to-all-done.3 = bf16[4,2,256,768]{3,2,1,0:T(8,128)(2,1)} async-done(((bf16[4,2,256,768]{3,2,1,0:T(8,128)(2,1)}), bf16[4,2,256,768]{3,2,1,0:T(8,128)(2,1)}, u32[]{:S(2)}, u32[]{:S(2)}) %all-to-all-start.3) | async-done | bytes 3145760 | tf_op jit(solution)/shard_map/all_to_all | solution.py:263
  427.7 4.9 all-to-all-start.1
  432.6 24.0 %bitcast_convert_fusion = bf16[2,3072,768]{2,1,0:T(8,128)(2,1)} fusion(bf16[4,2,256,768]{3,2,1,0:T(8,128)(2,1)} %all-to-all-done.2, f32[2,4,256,3072]{3,2,1,0:T(8,128)} %fusion.21), kind=kOutput, calls=%fused_computation.19 | convolution fusion | flops 9725018112 | bytes 37748736 | tf_op jit(solution)/shard_map/sjcf,sjcd->jfd/dot_general | solution.py:252
  456.6 8.2 copy.329
  464.8 5.0 dynamic-slice_bitcast_fusion
  479.0 5.0 constant_dynamic-slice_fusion
  490.9 12.4 %gather_fusion.3 = bf16[2048,768]{1,0:T(8,128)(2,1)} fusion(bf16[2048,768]{1,0:T(8,128)(2,1)} %bitcast.30, s32[2048]{0:T(1024)S(1)} %copy-done.4), kind=kCustom, calls=%fused_computation.3 | custom fusion | bytes 6299648 | tf_op jit(solution)/shard_map/gather | solution.py:266
  503.3 7.8 reshape.667
  511.1 12.4 %gather_fusion.1 = bf16[2048,768]{1,0:T(8,128)(2,1)} fusion(bf16[2048,768]{1,0:T(8,128)(2,1)} %bitcast.20, s32[2048]{0:T(1024)S(1)} %copy-done.4), kind=kCustom, calls=%fused_computation.1 | custom fusion | bytes 6299648 | tf_op jit(solution)/shard_map/gather | solution.py:227
  523.5 7.8 reshape.666
  531.3 38.0 %multiply_reduce_fusion.1 = (f32[1024,2]{1,0:T(8,128)}, f32[1024,768]{1,0:T(8,128)S(1)}, f32[1024,768]{1,0:T(8,128)}) fusion(f32[1024,2,768]{2,1,0:T(2,128)} %reshape.666, f32[1024,768]{1,0:T(8,128)} %copy-done.14, f32[1024,2]{1,0:T(8,128)} %fusion.87, f32[1024,2]{1,0:T(8,128)} %copy.289, f32[1024,2,768]{2,1,0:T(2,128)} %reshape.667), kind=kLoop, calls=%fused_computation.52 | loop fusion | flops 9435136 | bytes 22044672 | tf_op jit(solution)/shard_map/reduce_sum | solution.py:242
  569.3 14.0 %multiply_reduce_fusion.4 = (f32[4,768]{1,0:T(4,128)}, f32[1024,768]{1,0:T(8,128)}, f32[1024,768]{1,0:T(8,128)}) fusion(bf16[1024,768]{1,0:T(8,128)(2,1)S(1)} %copy-done.33, f32[1024,768]{1,0:T(8,128)S(1)} %get-tuple-element.51, bf16[3072,768]{1,0:T(8,128)(2,1)} %param.23, f32[1024,3072]{1,0:T(8,128)} %copy-done.74), kind=kOutput, calls=%fused_computation.81 | convolution fusion | flops 4863292416 | bytes 28323840 | tf_op jit(solution)/shard_map/dot_general | solution.py:209
  587.4 4.9 fusion.34
  596.8 8.1 multiply_reduce_fusion.5
  617.3 11.2 multiply_reduce_fusion
  628.6 8.1 multiply_convert_fusion.1
  654.2 5.5 convolution_convert_fusion.3
  659.7 5.9 copy.313
  677.3 7.2 multiply_reduce_fusion.11
  703.3 4.9 all-to-all-start.8
  711.9 17.9 %collective-permute-done.4 = bf16[768,192]{0,1:T(8,128)(2,1)S(1)} collective-permute-done((bf16[768,192]{0,1:T(8,128)(2,1)S(1)}, bf16[768,192]{0,1:T(8,128)(2,1)S(1)}, u32[]{:S(2)}, u32[]{:S(2)}) %collective-permute-start.4) | collective-permute-done | bytes 294944 | tf_op jit(solution)/shard_map/ppermute | solution.py:72
  732.8 4.9 all-to-all-start.7
  752.7 8.5 collective-permute-done.5
  763.1 4.8 all-to-all-start.6
  778.6 7.1 fusion.17
  789.6 5.0 all-to-all-start.10
  794.6 17.6 %bitcast_convert_fusion.1 = bf16[2,768,3072]{2,1,0:T(8,128)(2,1)} fusion(bf16[4,2,256,768]{3,2,1,0:T(8,128)(2,1)} %all-to-all-done, bf16[4,2,256,3072]{3,2,0,1:T(8,128)(2,1)} %fusion.6), kind=kOutput, calls=%fused_computation.20 | convolution fusion | flops 9668395008 | bytes 25165824 | tf_op jit(solution)/shard_map/sjcd,sjcf->jdf/dot_general | solution.py:259
  812.2 8.5 copy.326
  824.3 99.3 %collective-permute-done.12 = bf16[4,2,96,3072]{3,2,1,0:T(8,128)(2,1)S(1)} collective-permute-done((bf16[4,2,96,3072]{3,2,1,0:T(8,128)(2,1)S(1)}, bf16[4,2,96,3072]{3,2,1,0:T(8,128)(2,1)S(1)}, u32[]{:S(2)}, u32[]{:S(2)}) %collective-permute-start.12) | collective-permute-done | bytes 4718624 | tf_op jit(solution)/shard_map/ppermute | solution.py:72
  927.8 5.0 all-to-all-start.9
  933.6 120.4 %all-gather = bf16[32,4,768]{2,1,0:T(4,128)(2,1)} all-gather(bf16[1,4,768]{2,1,0:T(4,128)(2,1)S(1)} %fusion.84), channel_id=1, replica_groups=mesh['batch'=8,'expert'=4] {'batch','expert'}, dimensions={0}, use_global_device_ids=true | all-gather | bytes 202752 | tf_op jit(solution)/shard_map/all_gather | solution.py:338
  1062.8 4.9 multiply_add_fusion.2
  1067.7 60.1 %reduce-scatter.4.cloned.1.call-done = f32[96,8]{1,0:T(8,128)} async-done(((f32[768,8]{1,0:T(8,128)}), f32[96,8]{1,0:T(8,128)}) %reduce-scatter.4.cloned.1.call-update) | async-done | bytes 3088
  1128.7 5.6 all-reduce
  1136.4 31.7 %all_gather.7 = f32[128,1152]{1,0:T(8,128)S(1)} all-gather(f32[16,1152]{1,0:T(8,128)} %reshape.584), channel_id=1, replica_groups=mesh['batch'=8,'expert'=4] {'batch'}, dimensions={0}, use_global_device_ids=true | all-gather | bytes 663552 | tf_op jit(solution)/shard_map/all_gather | solution.py:337
  1179.0 4.7 convert_reduce_fusion
  1183.7 4.8 convert_reduce_fusion.1
  (346 shorter events, 285.7 us)
Async XLA Ops:
  7.2 22.1 %copy-start = (bf16[768,2304]{1,0:T(8,128)(2,1)S(1)}, bf16[768,2304]{1,0:T(8,128)(2,1)}, u32[]{:S(2)}) copy-start(bf16[768,2304]{1,0:T(8,128)(2,1)} %param.19) | copy-start | bytes 10616836
  20.4 6.9 copy-start.9
  50.3 4.6 copy-start.72
  55.0 9.4 copy-start.46
  60.4 4.7 copy-start.3
  60.4 4.7 copy-start.20
  72.7 6.1 copy-start.63
  81.8 34.9 %copy-start.44 = (f32[1024,2]{0,1:T(2,128)}, f32[1024,2]{0,1:T(2,128)S(1)}, u32[]{:S(2)}) copy-start(f32[1024,2]{0,1:T(2,128)S(1)} %select_reduce_fusion.1) | copy-start | bytes 24580
  81.9 34.8 %copy-start.54 = (f32[1024]{0:T(1024)}, f32[1024]{0:T(1024)S(1)}, u32[]{:S(2)}) copy-start(f32[1024]{0:T(1024)S(1)} %reduce_max.19) | copy-start | bytes 12292
  123.1 12.4 %copy-start.68 = (pred[1024]{0:T(1024)(128)(4,1)S(1)}, pred[1024]{0:T(1024)(128)(4,1)}, u32[]{:S(2)}) copy-start(pred[1024]{0:T(1024)(128)(4,1)} %lt.127) | copy-start | bytes 3076
  176.8 4.9 copy-start.67
  199.0 79.8 %all-to-all-start = ((bf16[4,2,256,768]{3,2,1,0:T(8,128)(2,1)}), bf16[4,2,256,768]{3,2,1,0:T(8,128)(2,1)}, u32[]{:S(2)}, u32[]{:S(2)}) async-start(bf16[4,2,256,768]{3,2,1,0:T(8,128)(2,1)} %get-tuple-element.83), calls=%async_computation | async-start | bytes 6291456 | tf_op jit(solution)/shard_map/all_to_all | solution.py:213
  203.7 12.0 %copy-start.15 = (f32[1024,768]{1,0:T(8,128)S(1)}, f32[1024,768]{1,0:T(8,128)}, u32[]{:S(2)}) copy-start(f32[1024,768]{1,0:T(8,128)} %copy-done.14) | copy-start | bytes 9437188
  211.2 4.5 copy-start.74
  226.3 14.7 %copy-start.2 = (bf16[4,256,768]{2,1,0:T(8,128)(2,1)S(1)}, bf16[4,256,768]{2,1,0:T(8,128)(2,1)}, u32[]{:S(2)}) copy-start(bf16[4,256,768]{2,1,0:T(8,128)(2,1)} %copy-done.1) | copy-start | bytes 4718596
  226.3 43.9 %collective-permute-start.9 = (bf16[2,3072,192]{1,2,0:T(8,128)(2,1)}, bf16[2,3072,192]{1,2,0:T(8,128)(2,1)}, u32[]{:S(2)}, u32[]{:S(2)}) collective-permute-start(bf16[2,3072,192]{1,2,0:T(8,128)(2,1)} %dynamic-slice_bitcast_fusion.2), channel_id=1, source_target_pairs={{0,1},{2,3},{1,0},{3,2},{4,5},{6,7},{5,4},{7,6},{8,9},{10,11},{9,8... | collective-permute-start | bytes 7077896 | tf_op jit(solution)/shard_map/ppermute | solution.py:72
  241.0 5.9 copy-start.73
  250.9 32.6 %collective-permute-start.6 = (bf16[2,768,768]{2,1,0:T(8,128)(2,1)}, bf16[2,768,768]{2,1,0:T(8,128)(2,1)}, u32[]{:S(2)}, u32[]{:S(2)}) collective-permute-start(bf16[2,768,768]{2,1,0:T(8,128)(2,1)} %dynamic-slice_bitcast_fusion.3), channel_id=1, source_target_pairs={{0,1},{2,3},{1,0},{3,2},{4,5},{6,7},{5,4},{7,6},{8,9},{10,11},{9,8... | collective-permute-start | bytes 7077896 | tf_op jit(solution)/shard_map/ppermute | solution.py:72
  276.0 195.9 %collective-permute-start.10 = (bf16[3072,192]{0,1:T(8,128)(2,1)}, bf16[3072,192]{0,1:T(8,128)(2,1)}, u32[]{:S(2)}, u32[]{:S(2)}) collective-permute-start(bf16[3072,192]{0,1:T(8,128)(2,1)} %dynamic-slice_bitcast_fusion.5), channel_id=1, source_target_pairs={{0,2},{1,3},{2,0},{3,1},{4,6},{5,7},{6,4},{7,5},{8,10},{9,11},{10,... | collective-permute-start | bytes 3538952 | tf_op jit(solution)/shard_map/ppermute | solution.py:72
  278.8 60.8 %all-to-all-start.2 = ((bf16[4,2,256,768]{3,2,1,0:T(8,128)(2,1)}), bf16[4,2,256,768]{3,2,1,0:T(8,128)(2,1)}, u32[]{:S(2)}, u32[]{:S(2)}) async-start(bf16[4,2,256,768]{3,2,1,0:T(8,128)(2,1)} %get-tuple-element.82), calls=%async_computation.2 | async-start | bytes 6291456 | tf_op jit(solution)/shard_map/all_to_all | solution.py:249
  289.0 196.5 %collective-permute-start.7 = (bf16[768,768]{1,0:T(8,128)(2,1)}, bf16[768,768]{1,0:T(8,128)(2,1)}, u32[]{:S(2)}, u32[]{:S(2)}) collective-permute-start(bf16[768,768]{1,0:T(8,128)(2,1)} %dynamic-slice_bitcast_fusion.6), channel_id=1, source_target_pairs={{0,2},{1,3},{2,0},{3,1},{4,6},{5,7},{6,4},{7,5},{8,10},{9,11},{10,... | collective-permute-start | bytes 3538952 | tf_op jit(solution)/shard_map/ppermute | solution.py:72
  386.0 41.7 %all-to-all-start.3 = ((bf16[4,2,256,768]{3,2,1,0:T(8,128)(2,1)}), bf16[4,2,256,768]{3,2,1,0:T(8,128)(2,1)}, u32[]{:S(2)}, u32[]{:S(2)}) async-start(bf16[4,2,256,768]{3,2,1,0:T(8,128)(2,1)} %copy.300), calls=%async_computation.3 | async-start | bytes 6291456 | tf_op jit(solution)/shard_map/all_to_all | solution.py:263
  427.7 83.4 %all-to-all-start.1 = ((bf16[4,2,256,768]{3,2,1,0:T(8,128)(2,1)}), bf16[4,2,256,768]{3,2,1,0:T(8,128)(2,1)}, u32[]{:S(2)}, u32[]{:S(2)}) async-start(bf16[4,2,256,768]{3,2,1,0:T(8,128)(2,1)} %copy.297), calls=%async_computation.1 | async-start | bytes 6291456 | tf_op jit(solution)/shard_map/all_to_all | solution.py:224
  464.8 7.2 copy-start.23
  469.8 308.8 %collective-permute-start.13 = (bf16[4,2,384,768]{3,2,1,0:T(8,128)(2,1)}, bf16[4,2,384,768]{3,2,1,0:T(8,128)(2,1)}, u32[]{:S(2)}, u32[]{:S(2)}) collective-permute-start(bf16[4,2,384,768]{3,2,1,0:T(8,128)(2,1)} %dynamic-slice_bitcast_fusion), channel_id=1, source_target_pairs={{0,4},{8,12},{16,20},{24,28},{4,0},{12,8},{20,16},{28,24},{1,5},{9... | collective-permute-start | bytes 14155784 | tf_op jit(solution)/shard_map/ppermute | solution.py:72
  479.0 6.4 copy-start.25
  484.1 6.8 copy-start.4
  485.4 183.1 %collective-permute-start.11 = (bf16[4,384,192]{1,0,2:T(4,128)(2,1)}, bf16[4,384,192]{1,0,2:T(4,128)(2,1)}, u32[]{:S(2)}, u32[]{:S(2)}) collective-permute-start(bf16[4,384,192]{1,0,2:T(4,128)(2,1)} %copy.322), channel_id=1, source_target_pairs={{0,4},{8,12},{16,20},{24,28},{4,0},{12,8},{20,16},{28,24},{1,5},{9... | collective-permute-start | bytes 1769480 | tf_op jit(solution)/shard_map/ppermute | solution.py:72
  488.9 220.9 %collective-permute-start.8 = (bf16[4,96,768]{2,1,0:T(8,128)(2,1)}, bf16[4,96,768]{2,1,0:T(8,128)(2,1)}, u32[]{:S(2)}, u32[]{:S(2)}) collective-permute-start(bf16[4,96,768]{2,1,0:T(8,128)(2,1)} %dynamic-slice_bitcast_fusion.8), channel_id=1, source_target_pairs={{0,4},{8,12},{16,20},{24,28},{4,0},{12,8},{20,16},{28,24},{1,5},{9... | collective-permute-start | bytes 1769480 | tf_op jit(solution)/shard_map/ppermute | solution.py:72
  531.3 38.0 %copy-start.33 = (bf16[1024,768]{1,0:T(8,128)(2,1)S(1)}, bf16[1024,768]{1,0:T(8,128)(2,1)}, u32[]{:S(2)}) copy-start(bf16[1024,768]{1,0:T(8,128)(2,1)} %param.17) | copy-start | bytes 4718596
  569.3 15.8 %copy-start.55 = (f32[1024]{0:T(1024)S(1)}, f32[1024]{0:T(1024)}, u32[]{:S(2)}) copy-start(f32[1024]{0:T(1024)} %copy-done.54) | copy-start | bytes 12292
  569.3 18.0 %copy-start.42 = (f32[4,768]{1,0:T(4,128)S(1)}, f32[4,768]{1,0:T(4,128)}, u32[]{:S(2)}) copy-start(f32[4,768]{1,0:T(4,128)} %copy-done.41) | copy-start | bytes 36868
  587.4 5.0 copy-start.43
  587.4 5.0 copy-start.6
  587.4 5.0 copy-start.53
  587.4 5.0 copy-start.57
  596.8 9.8 copy-start.51
  610.7 6.6 copy-start.47
  617.3 11.2 copy-start.40
  628.5 8.1 copy-start.19
  628.5 9.2 copy-start.17
  637.7 4.2 copy-start.21
  648.1 4.6 copy-start.8
  668.5 28.2 %collective-permute-start = (bf16[2,768,576]{1,2,0:T(8,128)(2,1)}, bf16[2,768,576]{1,2,0:T(8,128)(2,1)}, u32[]{:S(2)}, u32[]{:S(2)}) collective-permute-start(bf16[2,768,576]{1,2,0:T(8,128)(2,1)} %dynamic-slice_bitcast_fusion.4), channel_id=1, source_target_pairs={{0,1},{2,3},{1,0},{3,2},{4,5},{6,7},{5,4},{7,6},{8,9},{10,11},{9,8... | collective-permute-start | bytes 5308424 | tf_op jit(solution)/shard_map/ppermute | solution.py:72
  675.8 8.7 copy-start.36
  676.7 31.5 %collective-permute-start.3 = (bf16[2,768,192]{1,2,0:T(8,128)(2,1)}, bf16[2,768,192]{1,2,0:T(8,128)(2,1)}, u32[]{:S(2)}, u32[]{:S(2)}) collective-permute-start(bf16[2,768,192]{1,2,0:T(8,128)(2,1)} %dynamic-slice_bitcast_fusion.9), channel_id=1, source_target_pairs={{0,1},{2,3},{1,0},{3,2},{4,5},{6,7},{5,4},{7,6},{8,9},{10,11},{9,8... | collective-permute-start | bytes 1769480 | tf_op jit(solution)/shard_map/ppermute | solution.py:72
  677.3 8.5 copy-start.62
  677.3 9.1 copy-start.71
  677.3 9.7 copy-start.61
  677.3 10.3 copy-start.60
  692.8 10.6 all-to-all-start.4
  701.3 36.4 %collective-permute-start.1 = (bf16[768,576]{0,1:T(8,128)(2,1)}, bf16[768,576]{0,1:T(8,128)(2,1)}, u32[]{:S(2)}, u32[]{:S(2)}) collective-permute-start(bf16[768,576]{0,1:T(8,128)(2,1)} %dynamic-slice_bitcast_fusion.7), channel_id=1, source_target_pairs={{0,2},{1,3},{2,0},{3,1},{4,6},{5,7},{6,4},{7,5},{8,10},{9,11},{10,... | collective-permute-start | bytes 2654216 | tf_op jit(solution)/shard_map/ppermute | solution.py:72
  703.3 29.5 %all-to-all-start.8 = ((bf16[4,384,192]{1,2,0:T(8,128)(2,1)}), bf16[4,384,192]{1,2,0:T(8,128)(2,1)}, u32[]{:S(2)}, u32[]{:S(2)}) async-start(bf16[4,384,192]{1,2,0:T(8,128)(2,1)} %copy.323), calls=%async_computation.8 | async-start | bytes 1179648 | tf_op jit(solution)/shard_map/all_to_all | solution.py:74
  709.6 20.2 %collective-permute-start.4 = (bf16[768,192]{0,1:T(8,128)(2,1)S(1)}, bf16[768,192]{0,1:T(8,128)(2,1)S(1)}, u32[]{:S(2)}, u32[]{:S(2)}) collective-permute-start(bf16[768,192]{0,1:T(8,128)(2,1)S(1)} %dynamic-slice_bitcast_fusion.11), channel_id=1, source_target_pairs={{0,2},{1,3},{2,0},{3,1},{4,6},{5,7},{6,4},{7,5},{8,10},{9,11},{10,... | collective-permute-start | bytes 884744 | tf_op jit(solution)/shard_map/ppermute | solution.py:72
  732.8 30.3 %all-to-all-start.7 = ((bf16[4,96,768]{2,1,0:T(8,128)(2,1)}), bf16[4,96,768]{2,1,0:T(8,128)(2,1)}, u32[]{:S(2)}, u32[]{:S(2)}) async-start(bf16[4,96,768]{2,1,0:T(8,128)(2,1)} %fusion.52), calls=%async_computation.7 | async-start | bytes 1179648 | tf_op jit(solution)/shard_map/all_to_all | solution.py:74
  744.3 23.6 %collective-permute-start.2 = (bf16[4,96,576]{2,1,0:T(8,128)(2,1)}, bf16[4,96,576]{2,1,0:T(8,128)(2,1)}, u32[]{:S(2)}, u32[]{:S(2)}) collective-permute-start(bf16[4,96,576]{2,1,0:T(8,128)(2,1)} %dynamic-slice_bitcast_fusion.10), channel_id=1, source_target_pairs={{0,4},{8,12},{16,20},{24,28},{4,0},{12,8},{20,16},{28,24},{1,5},{9... | collective-permute-start | bytes 1327112 | tf_op jit(solution)/shard_map/ppermute | solution.py:72
  751.2 10.1 collective-permute-start.5
  763.1 11.2 all-to-all-start.6
  774.2 15.4 %all-to-all-start.5 = ((bf16[4,96,576]{2,1,0:T(8,128)(2,1)}), bf16[4,96,576]{2,1,0:T(8,128)(2,1)}, u32[]{:S(2)}, u32[]{:S(2)}) async-start(bf16[4,96,576]{2,1,0:T(8,128)(2,1)} %fusion.56), calls=%async_computation.5 | async-start | bytes 983040 | tf_op jit(solution)/shard_map/all_to_all | solution.py:74
  789.6 138.2 %all-to-all-start.10 = ((bf16[4,2,384,768]{3,2,1,0:T(8,128)(2,1)}), bf16[4,2,384,768]{3,2,1,0:T(8,128)(2,1)}, u32[]{:S(2)}, u32[]{:S(2)}) async-start(bf16[4,2,384,768]{3,2,1,0:T(8,128)(2,1)} %fusion.17), calls=%async_computation.10 | async-start | bytes 9437184 | tf_op jit(solution)/shard_map/all_to_all | solution.py:74
  820.7 102.9 %copy-start.12 = (bf16[2,8,96,3072]{3,2,0,1:T(8,128)(2,1)S(1)}, bf16[2,8,96,3072]{3,2,0,1:T(8,128)(2,1)}, u32[]{:S(2)}) copy-start(bf16[2,8,96,3072]{3,2,0,1:T(8,128)(2,1)} %copy.326) | copy-start | bytes 28311556
  823.7 99.9 %collective-permute-start.12 = (bf16[4,2,96,3072]{3,2,1,0:T(8,128)(2,1)S(1)}, bf16[4,2,96,3072]{3,2,1,0:T(8,128)(2,1)S(1)}, u32[]{:S(2)}, u32[]{:S(2)}) collective-permute-start(bf16[4,2,96,3072]{3,2,1,0:T(8,128)(2,1)S(1)} %dynamic-slice_bitcast_fusion.1), channel_id=1, source_target_pairs={{0,4},{8,12},{16,20},{24,28},{4,0},{12,8},{20,16},{28,24},{1,5},{9... | collective-permute-start | bytes 14155784 | tf_op jit(solution)/shard_map/ppermute | solution.py:72
  927.8 255.9 %all-to-all-start.9 = ((bf16[4,2,96,3072]{3,2,1,0:T(8,128)(2,1)}), bf16[4,2,96,3072]{3,2,1,0:T(8,128)(2,1)}, u32[]{:S(2)}, u32[]{:S(2)}) async-start(bf16[4,2,96,3072]{3,2,1,0:T(8,128)(2,1)} %fusion.18), calls=%async_computation.9 | async-start | bytes 9437184 | tf_op jit(solution)/shard_map/all_to_all | solution.py:74
  932.8 195.0 %reduce-scatter.4.cloned.1.call-start = ((), (), s32[]{:S(2)}) async-start(), calls=%async_computation.12 | async-start | bytes 442368
  (40 other events, 103.2 us)
Sparse Core Ops, SparseCore 0:
  1061.5 66.2 reduce-scatter.3

commit v2 on v1

v2 whole, which is shorter than its diff:
```python
import functools
import math

import jax
import jax.numpy as jnp
from jax import lax
from jax.experimental import pallas as pl
from jax.experimental.pallas import tpu as pltpu
from jax.sharding import PartitionSpec as P

D = 768
HEADS = 12
HEAD_DIM = 64
FF = 3072
EXPERTS = 8
SEQ = 256
CAP = 256
LANES = 128
PAIRS = HEADS // 2
H_MLP, G_SHARED, H_ATTN, HEADS_OUT = range(4)

GELU_C = 0.7978845608028654
GELU_A = 0.044715
EPSILON = 1e-06
MASKED = -1000000000.0
LOG2E = math.log2(math.e)
SCALE = HEAD_DIM ** (-0.5)

F32 = jnp.float32
BF16 = jnp.bfloat16
VMEM_LIMIT = 60 * 1024 * 1024
COST = 0.5


def dot_nn(a, b):
    return jnp.dot(a, b, preferred_element_type=F32)


def dot_nt(a, b):
    return lax.dot_general(a, b, (((1,), (1,)), ((), ())), preferred_element_type=F32)


def dot_tn(a, b):
    return lax.dot_general(a, b, (((0,), (0,)), ((), ())), preferred_element_type=F32)


def normalize(values):
    centre = values - jnp.mean(values, -1, keepdims=True)
    factor = lax.rsqrt(jnp.mean(centre * centre, -1, keepdims=True) + EPSILON)
    return (centre * factor, factor)


def norm_back(grad_norm, normed, factor):
    return factor * (
        grad_norm
        - jnp.mean(grad_norm, -1, keepdims=True)
        - normed * jnp.mean(grad_norm * normed, -1, keepdims=True)
    )


def half_masks():
    lane = lax.broadcasted_iota(jnp.int32, (1, LANES), 1)
    low = jnp.where(lane < HEAD_DIM, 1.0, 0.0).astype(BF16)
    return (low, (1.0 - low).astype(BF16))


def whole(shape):
    return pl.BlockSpec(shape, lambda *_: (0,) * len(shape))


def kind_of(which, t):
    return pl.BlockSpec((1, t, D), lambda *_: (which, 0, 0), pipeline_mode=pl.Buffered(1))


def once(shape):
    return pl.BlockSpec(shape, lambda *_: (0,) * len(shape), pipeline_mode=pl.Buffered(1))


def cost(flops, moved):
    return pl.CostEstimate(
        flops=int(COST * flops), bytes_accessed=int(COST * moved), transcendentals=0
    )


def params(**more):
    return pltpu.CompilerParams(vmem_limit_bytes=VMEM_LIMIT, **more)


def attn_forward_kernel(
    len_ref, tok_ref, cot_ref, mod_ref, wqkv_ref, wout_ref,
    qkv_ref, lse_ref, attn_ref, rows_ref,
):
    item = pl.program_id(0)
    mod = mod_ref[0]
    x = tok_ref[...].astype(F32)
    normed, _ = normalize(x)
    h = (normed * (1.0 + mod[1:2]) + mod[0:1]).astype(BF16)
    rows_ref[H_ATTN] = h
    qkv_ref[...] = dot_nn(h, wqkv_ref[...]).astype(BF16)
    key_live = lax.broadcasted_iota(jnp.int32, (1, SEQ), 1) < len_ref[item]
    masks = half_masks()
    lane = lax.broadcasted_iota(jnp.int32, (SEQ, LANES), 1)
    lse_all = jnp.zeros((SEQ, LANES), F32)
    for pair in range(PAIRS):
        at = LANES * pair
        q2 = qkv_ref[:, at : at + LANES]
        k2 = qkv_ref[:, D + at : D + at + LANES]
        v2 = qkv_ref[:, 2 * D + at : 2 * D + at + LANES]
        outs = []
        for half in range(2):
            s = dot_nt(q2 * masks[half], k2) * (SCALE * LOG2E)
            s = jnp.where(key_live, s, MASKED * LOG2E)
            peak = jnp.max(s, -1, keepdims=True)
            e = jnp.exp2(s - peak)
            total = jnp.sum(e, -1, keepdims=True)
            probs = (e * (1.0 / total)).astype(BF16)
            outs.append(dot_nn(probs, v2))
            lse = peak + jnp.log(total) * LOG2E
            lse_all = jnp.where(lane == 2 * pair + half, lse, lse_all)
        rows_ref[HEADS_OUT, :, at : at + LANES] = jnp.where(
            lane < HEAD_DIM, outs[0], outs[1]
        ).astype(BF16)
    lse_ref[...] = lse_all
    attn = dot_nn(rows_ref[HEADS_OUT], wout_ref[...])
    attn_ref[...] = attn
    x_mid = x + mod[2:3] * attn
    normed_mlp, _ = normalize(x_mid)
    rows_ref[H_MLP] = (normed_mlp * (1.0 + mod[4:5]) + mod[3:4]).astype(BF16)
    rows_ref[G_SHARED] = (mod[5:6] * cot_ref[...].astype(F32)).astype(BF16)


def attn_forward(lengths, tokens, cot, mod, wqkv, wout):
    t = tokens.shape[0]
    items = t // SEQ
    row = lambda w: pl.BlockSpec((SEQ, w), lambda i, _: (i, 0))
    return pl.pallas_call(
        attn_forward_kernel,
        name="attn_forward",
        grid_spec=pltpu.PrefetchScalarGridSpec(
            num_scalar_prefetch=1,
            grid=(items,),
            in_specs=[
                row(D), row(D), pl.BlockSpec((1, 6, D), lambda i, _: (i, 0, 0)),
                once((D, 3 * D)), once((D, D)),
            ],
            out_specs=[
                row(3 * D), row(LANES), row(D), pl.BlockSpec((4, SEQ, D), lambda i, _: (0, i, 0)),
            ],
        ),
        out_shape=[
            jax.ShapeDtypeStruct((t, 3 * D), BF16),
            jax.ShapeDtypeStruct((t, LANES), F32),
            jax.ShapeDtypeStruct((t, D), F32),
            jax.ShapeDtypeStruct((4, t, D), BF16),
        ],
        compiler_params=params(),
        cost_estimate=cost(int(8.1e9), int(24e6)),
    )(lengths, tokens, cot, mod, wqkv, wout)


def live_of(len_ref, items, shape, dim):
    tok = lax.broadcasted_iota(jnp.int32, shape, dim)
    limit = jnp.zeros(shape, jnp.int32)
    for i in range(items):
        limit = jnp.where(tok >= i * SEQ, i * SEQ + len_ref[i], limit)
    return tok < limit


def route_kernel(len_ref, h_ref, rw_ref, rcol_ref, rrow_ref, info_ref, pos_ref):
    t = h_ref.shape[1]
    items = t // SEQ
    lane = lax.broadcasted_iota(jnp.int32, (t, LANES), 1)
    r0 = rcol_ref[:, 0:1]
    r1 = rcol_ref[:, 1:2]
    live = live_of(len_ref, items, (t, 1), 0)
    is0 = lane == r0
    is1 = lane == r1
    hot = jnp.where((is0 | is1) & live, 1.0, 0.0)
    before = (
        lax.broadcasted_iota(jnp.int32, (t, t), 1) < lax.broadcasted_iota(jnp.int32, (t, t), 0)
    )
    tri = jnp.where(before, 1.0, 0.0).astype(BF16)
    count = dot_nn(tri, hot.astype(BF16))
    p0 = jnp.sum(jnp.where(is0, count, 0.0), -1, keepdims=True)
    p1 = jnp.sum(jnp.where(is1, count, 0.0), -1, keepdims=True)
    slot0 = jnp.where(live & (p0 < CAP), r0.astype(F32) * CAP + p0, -1.0)
    slot1 = jnp.where(live & (p1 < CAP), r1.astype(F32) * CAP + p1, -1.0)
    logits = dot_nn(h_ref[0], rw_ref[...])
    l0 = jnp.sum(jnp.where(is0, logits, 0.0), -1, keepdims=True)
    l1 = jnp.sum(jnp.where(is1, logits, 0.0), -1, keepdims=True)
    top = jnp.maximum(l0, l1)
    e0 = jnp.exp(l0 - top)
    e1 = jnp.exp(l1 - top)
    total = e0 + e1
    info = jnp.zeros((t, LANES), F32)
    for k, column in enumerate(
        (e0 / total, e1 / total, slot0, slot1, r0.astype(F32), r1.astype(F32))
    ):
        info = jnp.where(lane == k, column, info)
    info_ref[...] = info
    expert = lax.broadcasted_iota(jnp.int32, (EXPERTS, t), 0)
    live_row = live_of(len_ref, items, (1, t), 1)
    hot_row = ((expert == rrow_ref[0:1, :]) | (expert == rrow_ref[1:2, :])) & live_row
    count_row = dot_nt(jnp.where(hot_row, 1.0, 0.0).astype(BF16), tri)
    pos_ref[...] = jnp.where(hot_row, count_row, -1.0)


def route(lengths, rows, rw_pad, routes, routes_t):
    t = rows.shape[1]
    return pl.pallas_call(
        route_kernel,
        name="route",
        grid=(1,),
        in_specs=[
            pl.BlockSpec(memory_space=pltpu.SMEM), kind_of(H_MLP, t), whole(rw_pad.shape),
            whole(routes.shape), whole(routes_t.shape),
        ],
        out_specs=[whole((t, LANES)), whole((EXPERTS, t))],
        out_shape=[
            jax.ShapeDtypeStruct((t, LANES), F32),
            jax.ShapeDtypeStruct((EXPERTS, t), F32),
        ],
        compiler_params=params(),
        cost_estimate=cost(int(1e9), int(3e6)),
    )(lengths, rows, rw_pad, routes, routes_t)


def dispatch_kernel(local, first, h_ref, cot_ref, mod_ref, info_ref, pos_ref, out_ref, grad_scr):
    group = pl.program_id(0)
    t = h_ref.shape[1]
    items = t // SEQ
    expert = group * local + first

    @pl.when(group == 0)
    def _():
        for i in range(items):
            rows = slice(i * SEQ, (i + 1) * SEQ)
            grad_scr[rows] = mod_ref[i, 5:6, :] * cot_ref[rows].astype(F32)

    pos = pos_ref[pl.ds(expert, 1), :]
    slot = lax.broadcasted_iota(jnp.int32, (CAP, t), 0).astype(F32)
    hot = jnp.where(slot == pos, 1.0, 0.0).astype(BF16)
    out_ref[0, 0] = dot_nn(hot, h_ref[0]).astype(BF16)
    name = expert.astype(F32)
    weight = jnp.where(
        info_ref[:, 4:5] == name, info_ref[:, 0:1],
        jnp.where(info_ref[:, 5:6] == name, info_ref[:, 1:2], 0.0),
    )
    rows = (weight * grad_scr[...]).astype(BF16)
    out_ref[0, 1] = dot_nn(hot, rows).astype(BF16)


def dispatch(first, local, rows, cot, mod, info, pos):
    t = rows.shape[1]
    groups = EXPERTS // local
    return pl.pallas_call(
        functools.partial(dispatch_kernel, local, first),
        name="dispatch",
        grid=(groups,),
        in_specs=[
            kind_of(H_MLP, t), once((t, D)), once(mod.shape), once((t, LANES)), once((EXPERTS, t)),
        ],
        out_specs=pl.BlockSpec((1, 2, CAP, D), lambda g: (g, 0, 0, 0)),
        out_shape=jax.ShapeDtypeStruct((groups, 2, CAP, D), BF16),
        scratch_shapes=[pltpu.VMEM((t, D), F32)],
        compiler_params=params(),
        cost_estimate=cost(int(3.3e9), int(8e6)),
    )(rows, cot, mod, info, pos)


def gelu_pair(v):
    square = v * v
    gate = 0.5 * jnp.tanh(v * (GELU_C * GELU_A * square + GELU_C)) + 0.5
    act = v * gate
    slope = gate + act * (1.0 - gate) * (6.0 * GELU_C * GELU_A * square + 2.0 * GELU_C)
    return act, slope


def ffn_main_kernel(where_ref, x_ref, g_ref, w1_ref, w2_ref, *rest, paired, halved):
    if paired:
        out_ref, act_ref, gpre_ref = rest
        x, g = x_ref[0, 0], x_ref[0, 1]
    else:
        y_ref, gx_ref, act_ref, *gpre_refs, gpre_ref = rest
        x, g = x_ref[0], g_ref[0]
    for f in range(4):
        cols = slice(f * (FF // 4), (f + 1) * (FF // 4))
        act, slope = gelu_pair(dot_nn(x, w1_ref[0, :, cols]))
        act_ref[:, cols] = act.astype(BF16)
        gpre_ref[:, cols] = (dot_nt(g, w2_ref[0, cols, :]) * slope).astype(BF16)
    y = dot_nn(act_ref[...], w2_ref[0])
    gx = dot_nt(gpre_ref[...], w1_ref[0])
    if paired:
        out_ref[0, 0] = y.astype(BF16)
        out_ref[0, 1] = gx.astype(BF16)
    else:
        y_ref[...] = y
        gx_ref[...] = gx
    if halved:
        first = where_ref[0] == 0
        width = FF // 4
        for x_at in range(2):
            low = gpre_ref[:, 2 * x_at * width : (2 * x_at + 1) * width]
            high = gpre_ref[:, (2 * x_at + 1) * width : (2 * x_at + 2) * width]
            cols = slice(x_at * width, (x_at + 1) * width)
            gpre_refs[0][:, cols] = jnp.where(first, low, high)
            gpre_refs[1][:, cols] = jnp.where(first, high, low)


def ffn_main(x, w1, w2, which, where=None):
    paired = x.ndim == 4
    halved = where is not None
    rows = x.shape[0] * CAP if paired else x.shape[1]
    chunk = lambda w: pl.BlockSpec((CAP, w), lambda s, *_: (s, 0))
    scratch = []
    if paired:
        first = [pl.BlockSpec((1, 2, CAP, D), lambda s, *_: (s, 0, 0, 0)), once((8, D))]
        args = (x, jnp.zeros((8, D), BF16))
        outs, out_specs = [jax.ShapeDtypeStruct(x.shape, BF16)], first[:1]
    else:
        kind = lambda k: pl.BlockSpec((1, CAP, D), lambda s, *_: (k, s, 0))
        first = [kind(H_MLP), kind(G_SHARED)]
        args = (x, x)
        outs, out_specs = [jax.ShapeDtypeStruct((rows, D), F32)] * 2, [chunk(D)] * 2
    outs = outs + [jax.ShapeDtypeStruct((rows, FF), BF16)]
    out_specs = out_specs + [chunk(FF)]
    if halved:
        outs = outs + [jax.ShapeDtypeStruct((rows, FF // 2), BF16)] * 2
        out_specs = out_specs + [chunk(FF // 2)] * 2
        scratch = [pltpu.VMEM((CAP, FF), BF16)]
    else:
        where = jnp.zeros((1,), jnp.int32)
        outs = outs + [jax.ShapeDtypeStruct((rows, FF), BF16)]
        out_specs = out_specs + [chunk(FF)]
    weight = lambda r, c: pl.BlockSpec(
        (1, r, c), lambda s, *_: (which, 0, 0), pipeline_mode=pl.Buffered(1)
    )
    return pl.pallas_call(
        functools.partial(ffn_main_kernel, paired=paired, halved=halved),
        name="ffn_main_pairs" if paired else "ffn_main_shared",
        grid_spec=pltpu.PrefetchScalarGridSpec(
            num_scalar_prefetch=1,
            grid=(rows // CAP,),
            in_specs=first + [weight(D, FF), weight(FF, D)],
            out_specs=out_specs,
            scratch_shapes=scratch,
        ),
        out_shape=outs,
        compiler_params=params(),
        cost_estimate=cost(8 * rows * D * FF, int(30e6)),
    )(where, *args, w1, w2)


def weight_grad_kernel(mode, where_ref, a_ref, b_ref, *outs):
    a = a_ref[...].reshape(-1, D)
    part = dot_tn(a, b_ref[...]).astype(BF16)
    if mode == "plain":
        outs[0][...] = part
        return
    first = where_ref[0] == 0
    keep_ref, send_ref = outs
    if mode == "in":
        for z in range(4):
            low = part[192 * z : 192 * z + 96]
            high = part[192 * z + 96 : 192 * z + 192]
            at = (z % 2) ^ where_ref[1], (z // 2) ^ where_ref[2]
            keep_ref[at] = jnp.where(first, low, high)
            send_ref[at] = jnp.where(first, high, low)
    else:
        low, high = part[:, :384], part[:, 384:]
        mine = jnp.where(first, low, high)
        other = jnp.where(first, high, low)
        for k in range(8):
            cols = slice(k * 384, k * 384 + 384)
            keep_ref[0, 0, :, cols] = mine[k * 96 : k * 96 + 96]
            send_ref[0, 0, :, cols] = other[k * 96 : k * 96 + 96]


def weight_grad(mode, mine, a, kind, b):
    rows = b.shape[0]
    tile = FF // 4
    tile_of = lambda s, m: s
    if mode == "out":
        tile_of = lambda s, m: ((s % 2) ^ m[2]) * 2 + ((s // 2) ^ m[1])
    if a.ndim == 3:
        a_spec = kind_of(kind, rows)
    else:
        a_spec = pl.BlockSpec(
            (a.shape[0], 1, CAP, D), lambda s, m: (0, kind, 0, 0), pipeline_mode=pl.Buffered(1)
        )
    if mode == "plain":
        outs = [jax.ShapeDtypeStruct((D, FF), BF16)]
        specs = [pl.BlockSpec((D, tile), lambda s, m: (0, s))]
    else:
        outs = [jax.ShapeDtypeStruct((2, 2, 96, FF), BF16)] * 2
        if mode == "in":
            specs = [pl.BlockSpec((2, 2, 96, tile), lambda s, m: (0, 0, 0, s))] * 2
        else:
            specs = [pl.BlockSpec((1, 1, 96, FF), lambda s, m: (s // 2, s % 2, 0, 0))] * 2
    return pl.pallas_call(
        functools.partial(weight_grad_kernel, mode),
        name="weight_grad_" + mode,
        grid_spec=pltpu.PrefetchScalarGridSpec(
            num_scalar_prefetch=1,
            grid=(FF // tile,),
            in_specs=[a_spec, pl.BlockSpec((rows, tile), lambda s, m: (0, tile_of(s, m)))],
            out_specs=specs,
        ),
        out_shape=outs,
        compiler_params=params(),
        cost_estimate=cost(2 * rows * D * FF, int(13e6)),
    )(mine, a, b)


def batch_at(where_ref, b, y_last):
    z = b // 2
    y = (b % 2) ^ where_ref[2]
    near, far = (z % 2) ^ where_ref[3], (z // 2) ^ where_ref[4]
    return (near, far, y) if y_last else (y, near, far)


def own_columns(where_ref, v, width):
    low = jnp.concatenate([v[:, :width], v[:, 2 * width : 3 * width]], 1)
    high = jnp.concatenate([v[:, width : 2 * width], v[:, 3 * width :]], 1)
    return jnp.where(where_ref[0] == 0, low, high)


def shared_grad_kernel(
    where_ref, mine_ref, peer_ref, gpre_ref, gpre_peer_ref, act_ref, act_peer_ref,
    keep_ref, send_ref, g_scr,
):
    step = pl.program_id(0)
    side = step // 2
    rows = act_ref.shape[0]

    @pl.when(step == 0)
    def _():
        g_scr[:rows] = own_columns(where_ref, mine_ref[G_SHARED], D // 4)
        g_scr[rows:] = own_columns(where_ref, peer_ref[G_SHARED], D // 4)

    part = (
        dot_tn(mine_ref[H_MLP], gpre_ref[...]) + dot_tn(peer_ref[H_MLP], gpre_peer_ref[...])
    ).astype(BF16)
    for half in range(2):
        for s, ref in ((0, keep_ref), (1, send_ref)):
            @pl.when((step % 2 == half) & (side == s))
            def _():
                for b in range(8):
                    ref[(*batch_at(where_ref, b, False), 0, slice(None), slice(half * 384, half * 384 + 384))] = part[b * 96 : b * 96 + 96]

    both = (dot_tn(g_scr[:rows], act_ref[...]) + dot_tn(g_scr[rows:], act_peer_ref[...])).astype(BF16)
    first = where_ref[1] == 0
    low, high = both[:192], both[192:]
    for ref, v in ((keep_ref, jnp.where(first, low, high)), (send_ref, jnp.where(first, high, low))):
        for h in range(2):
            for y in range(2):
                at = batch_at(where_ref, 2 * step + y, False)
                ref[(*at, 1, slice(None), slice(h * 384, h * 384 + 384))] = v[
                    h * 96 : h * 96 + 96, y * 384 : y * 384 + 384
                ]


def shared_grad(where, mine, peer, gpre, gpre_peer, act, act_peer):
    rows = act.shape[0]
    gpre_spec = pl.BlockSpec((rows, FF // 8), lambda s, m: (0, ((s // 2) ^ m[1]) * 2 + s % 2))
    act_spec = pl.BlockSpec((rows, FF // 4), lambda s, m: (0, s))
    stack = pl.BlockSpec((2, rows, D), lambda s, m: (0, 0, 0), pipeline_mode=pl.Buffered(1))
    shape = (2, 2, 2, 2, 96, D)
    return pl.pallas_call(
        shared_grad_kernel,
        name="shared_grad",
        grid_spec=pltpu.PrefetchScalarGridSpec(
            num_scalar_prefetch=1,
            grid=(4,),
            in_specs=[stack, stack, gpre_spec, gpre_spec, act_spec, act_spec],
            out_specs=[once(shape)] * 2,
            scratch_shapes=[pltpu.VMEM((2 * rows, D // 2), BF16)],
        ),
        out_shape=[jax.ShapeDtypeStruct(shape, BF16)] * 2,
        compiler_params=params(),
        cost_estimate=cost(4 * rows * D * FF, int(25e6)),
    )(where, mine, peer, gpre, gpre_peer, act, act_peer)


def backward_kernel(
    local, fast, first_item, len_ref, where_ref, tok_ref, cot_ref, mod_ref, attn_ref, qkv_ref, lse_ref,
    sres_ref, gsh_ref, info_ref, wqkv_ref, wout_ref, rwt_ref, *rest,
):
    back = rest[:local]
    if fast:
        out_ref, gtok_ref, gmod_ref, own_ref, other_ref, gq_ref, yr_ref, gr_ref = rest[-8:]
    else:
        out_ref, gtok_ref, gmod_ref, own_ref, gq_ref, yr_ref, gr_ref = rest[-7:]
    item = pl.program_id(0) + first_item
    slots = yr_ref.shape[0]

    @pl.when(pl.program_id(0) == 0)
    def _():
        for j in range(local):
            for g in range(EXPERTS // local):
                rows = slice((g * local + j) * CAP, (g * local + j + 1) * CAP)
                yr_ref[rows] = back[j][g, 0]
                gr_ref[rows] = back[j][g, 1]

    mod = mod_ref[0]
    x = tok_ref[...].astype(F32)
    cot = cot_ref[...].astype(F32)
    attn = attn_ref[...]
    x_mid = x + mod[2:3] * attn
    normed_mlp, factor_mlp = normalize(x_mid)
    gw0, gw1 = info_ref[:, 0:1], info_ref[:, 1:2]
    slot = lax.broadcasted_iota(jnp.int32, (SEQ, slots), 1).astype(F32)
    hot0 = jnp.where(slot == info_ref[:, 2:3], 1.0, 0.0).astype(BF16)
    hot1 = jnp.where(slot == info_ref[:, 3:4], 1.0, 0.0).astype(BF16)
    row0 = dot_nn(hot0, yr_ref[...])
    row1 = dot_nn(hot1, yr_ref[...])
    mlp_out = sres_ref[...] + (gw0 * row0 + gw1 * row1)
    out_ref[...] = (x_mid + mod[5:6] * mlp_out).astype(BF16)
    gmod_ref[0, 5:6, :] = jnp.sum(cot * mlp_out, 0, keepdims=True)
    grad_mlp = mod[5:6] * cot
    gate0 = jnp.sum(grad_mlp * row0, -1, keepdims=True)
    gate1 = jnp.sum(grad_mlp * row1, -1, keepdims=True)
    weighted = gw0 * gate0 + gw1 * gate1
    sel0 = gw0 * (gate0 - weighted)
    sel1 = gw1 * (gate1 - weighted)
    high0 = sel0.astype(BF16).astype(F32)
    high1 = sel1.astype(BF16).astype(F32)
    lane = lax.broadcasted_iota(jnp.int32, (SEQ, LANES), 1)
    lane_f = lane.astype(F32)
    r0, r1 = info_ref[:, 4:5], info_ref[:, 5:6]
    g_logits = (
        jnp.where(lane_f == r0, high0, 0.0)
        + jnp.where(lane_f == r1, high1, 0.0)
        + jnp.where(lane_f == r0 + EXPERTS, sel0 - high0, 0.0)
        + jnp.where(lane_f == r1 + EXPERTS, sel1 - high1, 0.0)
    ).astype(BF16)
    grad_h = gsh_ref[...] + dot_nn(hot0 + hot1, gr_ref[...]) + dot_nn(g_logits, rwt_ref[...])
    gmod_ref[0, 3:4, :] = jnp.sum(grad_h, 0, keepdims=True)
    gmod_ref[0, 4:5, :] = jnp.sum(grad_h * normed_mlp, 0, keepdims=True)
    grad_mid = cot + norm_back(grad_h * (1.0 + mod[4:5]), normed_mlp, factor_mlp)
    gmod_ref[0, 2:3, :] = jnp.sum(grad_mid * attn, 0, keepdims=True)
    g_attn = (mod[2:3] * grad_mid).astype(BF16)
    g_heads = dot_nt(g_attn, wout_ref[...]).astype(BF16)
    key_live = lax.broadcasted_iota(jnp.int32, (1, SEQ), 1) < len_ref[item]
    masks = half_masks()
    low_half = lane < HEAD_DIM
    for pair in range(PAIRS):
        at = LANES * pair
        q2 = qkv_ref[:, at : at + LANES]
        k2 = qkv_ref[:, D + at : D + at + LANES]
        v2 = qkv_ref[:, 2 * D + at : 2 * D + at + LANES]
        gh2 = g_heads[:, at : at + LANES]
        dq, dk, dv = [], [], []
        for half in range(2):
            head = 2 * pair + half
            s = dot_nt(q2 * masks[half], k2) * (SCALE * LOG2E)
            s = jnp.where(key_live, s, MASKED * LOG2E)
            probs = jnp.exp2(s - lse_ref[:, head : head + 1])
            g_probs = dot_nt(gh2 * masks[half], v2)
            spread = jnp.sum(probs * g_probs, -1, keepdims=True)
            g_scores = (probs * (g_probs - spread)).astype(BF16)
            dq.append(dot_nn(g_scores, k2))
            dk.append(dot_tn(g_scores, q2))
            dv.append(dot_tn(probs.astype(BF16), gh2))
        gq_ref[:, at : at + LANES] = (jnp.where(low_half, dq[0], dq[1]) * SCALE).astype(BF16)
        gq_ref[:, D + at : D + at + LANES] = (
            jnp.where(low_half, dk[0], dk[1]) * SCALE
        ).astype(BF16)
        gq_ref[:, 2 * D + at : 2 * D + at + LANES] = jnp.where(low_half, dv[0], dv[1]).astype(BF16)
    g_qkv = gq_ref[...]
    g_h = dot_nt(g_qkv, wqkv_ref[...])
    normed, factor = normalize(x)
    gmod_ref[0, 0:1, :] = jnp.sum(g_h, 0, keepdims=True)
    gmod_ref[0, 1:2, :] = jnp.sum(g_h * normed, 0, keepdims=True)
    gmod_ref[0, 6:8, :] = jnp.zeros((2, D), F32)
    gtok_ref[...] = grad_mid + norm_back(g_h * (1.0 + mod[1:2]), normed, factor)
    if fast:
        sides = [
            jnp.concatenate(
                [
                    g_qkv[:, 576 * c : 576 * c + 576],
                    g_qkv[:, 1152 + 576 * c : 1728 + 576 * c],
                    g_attn[:, 192 * c : 192 * c + 192],
                    g_attn[:, 384 + 192 * c : 576 + 192 * c],
                ], 1
            )
            for c in range(2)
        ]
        first = where_ref[0] == 0
        own_ref[:, : 2 * D] = jnp.where(first, sides[0], sides[1])
        own_ref[:, 2 * D :] = g_logits
        other_ref[:, : 2 * D] = jnp.where(first, sides[1], sides[0])
        other_ref[:, 2 * D :] = g_logits
    else:
        own_ref[:, : 3 * D] = g_qkv
        own_ref[:, 3 * D : 4 * D] = g_attn
        own_ref[:, 4 * D :] = g_logits


def backward(
    fast, where, first_item, count, so_far, lengths, tokens, cot, mod, attn, qkv, lse, sres, gsh,
    info, back, wqkv, wout, rwt,
):
    t = tokens.shape[0]
    row = lambda w: pl.BlockSpec((SEQ, w), lambda i, *_: (i + first_item, 0))
    new = lambda w: pl.BlockSpec((SEQ, w), lambda i, *_: (i, 0))
    local = len(back)
    item_block = lambda r: pl.BlockSpec((1, r, D), lambda i, *_: (i + first_item, 0, 0))
    known = 14 + local
    widths = [2 * D + LANES] * 2 if fast else [4 * D + LANES]
    outs = pl.pallas_call(
        functools.partial(backward_kernel, local, fast, first_item),
        name="backward",
        grid_spec=pltpu.PrefetchScalarGridSpec(
            num_scalar_prefetch=2,
            grid=(count,),
            in_specs=[
                row(D), row(D), item_block(6),
                row(D), row(3 * D), row(LANES), row(D), row(D), row(LANES),
                once((D, 3 * D)), once((D, D)), once((LANES, D)),
            ] + [once(b.shape) for b in back]
            + [pl.BlockSpec(memory_space=pl.ANY)] * len(so_far),
            out_specs=[row(D), row(D), item_block(8)] + [new(w) for w in widths],
            scratch_shapes=[
                pltpu.VMEM((SEQ, 3 * D), BF16),
                pltpu.VMEM((EXPERTS * CAP, D), BF16),
                pltpu.VMEM((EXPERTS * CAP, D), BF16),
            ],
        ),
        out_shape=[
            jax.ShapeDtypeStruct((t, D), BF16),
            jax.ShapeDtypeStruct((t, D), F32),
            jax.ShapeDtypeStruct((t // SEQ, 8, D), F32),
        ] + [jax.ShapeDtypeStruct((count * SEQ, w), BF16) for w in widths],
        input_output_aliases={known + i: i for i in range(len(so_far))},
        compiler_params=params(),
        cost_estimate=cost(int(5e9) * count, int(7e6) * count),
    )(
        lengths, where, tokens, cot, mod, attn, qkv, lse, sres, gsh, info, wqkv, wout, rwt,
        *back, *so_far,
    )
    return (outs[:3], *outs[3:])


def tail_grad_kernel(fast, many, where_ref, *refs):
    stacks, grads, outs = refs[:many], refs[many:-2 if fast else -3], refs[-2 if fast else -3:]
    width = 3 * D // 2 if fast else 3 * D
    part = grads[0].shape[0]
    each = len(grads) // many

    def total(kind, start, size):
        value = None
        for i, g in enumerate(grads):
            at = (i % each) * part
            term = dot_tn(stacks[i // each][kind, at : at + part], g[:, start : start + size])
            value = term if value is None else value + term
        return value

    d_qkv = total(H_ATTN, 0, width).astype(BF16)
    d_out = total(HEADS_OUT, width, width // 3).astype(BF16)
    d_router = total(H_MLP, width + width // 3, LANES)
    d_router = (d_router + pltpu.roll(d_router, LANES - EXPERTS, 1)).astype(BF16)
    if not fast:
        outs[0][...], outs[1][...], outs[2][...] = d_qkv, d_out, d_router
        return
    first = where_ref[1] == 0
    low, high = [
        jnp.concatenate(
            [d_qkv[:, 576 * x : 576 * x + 576], d_out[:, 192 * x : 192 * x + 192], d_router], 1
        )
        for x in range(2)
    ]
    for ref, v in ((outs[0], jnp.where(first, low, high)), (outs[1], jnp.where(first, high, low))):
        for b in range(8):
            ref[batch_at(where_ref, b, True)] = v[b * 96 : b * 96 + 96]


def tail_grad(fast, where, stacks, grads):
    if fast:
        outs = [jax.ShapeDtypeStruct((2, 2, 2, 96, D + LANES), BF16)] * 2
    else:
        outs = [
            jax.ShapeDtypeStruct((D, 3 * D), BF16),
            jax.ShapeDtypeStruct((D, D), BF16),
            jax.ShapeDtypeStruct((D, LANES), BF16),
        ]
    vmem = pl.BlockSpec(memory_space=pltpu.VMEM)
    return pl.pallas_call(
        functools.partial(tail_grad_kernel, fast, len(stacks)),
        name="tail_grad",
        in_specs=[pl.BlockSpec(memory_space=pltpu.SMEM)] + [vmem] * (len(stacks) + len(grads)),
        out_specs=[vmem] * len(outs),
        out_shape=outs,
        compiler_params=params(),
        cost_estimate=cost(int(5e9), int(20e6)),
    )(where, *stacks, *grads)


def after(value, *others):
    if not others:
        return value
    return lax.optimization_barrier((value,) + tuple(others))[0]


def group_sum(blocks, axis, groups):
    width = len(groups[0])
    if width == 1:
        return blocks[0].astype(F32)
    low = blocks.astype(BF16)
    if width == 2:
        place = jnp.zeros((), jnp.int32)
        index = lax.axis_index(axis)
        for g in groups:
            place = jnp.where(index == g[1], 1, place)
        sent = lax.dynamic_index_in_dim(low, 1 - place, 0, keepdims=False)
        kept = lax.dynamic_index_in_dim(low, place, 0, keepdims=False)
        return pair_sum(kept, sent, axis, groups)
    got = lax.all_to_all(low, axis, 0, 0, tiled=True, axis_index_groups=groups)
    return jnp.sum(got.astype(F32), 0)


def pair_sum(kept, sent, axis, groups):
    pairs = [(g[0], g[1]) for g in groups] + [(g[1], g[0]) for g in groups]
    got = lax.ppermute(sent, axis, pairs)
    return kept.astype(F32) + got.astype(F32)


def swap(value, axis, bit):
    size = lax.axis_size(axis)
    return lax.ppermute(value.astype(BF16), axis, [(i, i ^ bit) for i in range(size)])


class Chain:
    def __init__(self, keep, send, stages):
        self.terms, self.send, self.stages = [keep], send, list(stages)

    def total(self):
        value = self.terms[0].astype(F32)
        for term in self.terms[1:]:
            value = value + term.astype(F32)
        return value

    def step(self, send_after=(), take_after=()):
        axis, bit = self.stages.pop(0)
        got = swap(after(self.send, *send_after), axis, bit)
        self.terms.append(after(got, *take_after))
        if self.stages:
            terms = self.terms
            self.terms = [v[1] for v in terms]
            self.send = self.total().astype(BF16)
            self.terms = [v[0] for v in terms]
        else:
            self.send = None
        return self


def inner_groups(outer, inner):
    return [[o * inner + i for i in range(inner)] for o in range(outer)]


def outer_groups(outer, inner):
    return [[o * inner + i for o in range(outer)] for i in range(inner)]


def batch_split(size):
    inner = 2 if size <= 8 else 8
    return (size // inner, inner)


def reduce_batch(blocks):
    outer, inner = batch_split(lax.axis_size("batch"))
    v = jnp.moveaxis(blocks.reshape((outer, inner) + blocks.shape[1:]), 1, 0)
    v = group_sum(v, "batch", inner_groups(outer, inner))
    return group_sum(v, "batch", outer_groups(outer, inner))


def reduce_expert(blocks):
    outer, inner = lax.axis_size("expert") // 2, 2
    v = jnp.moveaxis(blocks.reshape((outer, inner) + blocks.shape[1:]), 1, 0)
    v = group_sum(v, "expert", inner_groups(outer, inner))
    return group_sum(v, "expert", outer_groups(outer, inner))


def reduce_dense(grad):
    nb, ne = lax.axis_size("batch"), lax.axis_size("expert")
    r, c = grad.shape
    v = jnp.transpose(grad.reshape(r, ne, c // ne), (1, 0, 2))
    v = reduce_expert(v)
    return reduce_batch(v.reshape(nb, r // nb, c // ne))


def reduce_local(grad):
    nb = lax.axis_size("batch")
    r, c = grad.shape
    return reduce_batch(grad.reshape(nb, r // nb, c))


def all_pairs(parts):
    nb, ne = parts.shape[:2]
    return lax.all_to_all(
        parts.reshape((nb * ne,) + parts.shape[2:]), ("batch", "expert"), 0, 0, tiled=True
    )


def per_device(
    tokens, condition, lengths, routes, cotangent, ada_weight, qkv_weight, out_weight,
    router_weight, shared_in, shared_out, expert_in, expert_out,
):
    nb, ne = lax.axis_size("batch"), lax.axis_size("expert")
    local = expert_in.shape[0]
    items = lengths.shape[0]
    t = tokens.shape[0]
    fast = nb == 8 and ne == 4 and local == 2
    batch, expert = lax.axis_index("batch"), lax.axis_index("expert")
    z_at = batch // 2
    where = jnp.stack([expert % 2, expert // 2, batch % 2, z_at % 2, z_at // 2]).astype(jnp.int32)
    y_at = jnp.stack([batch % 2, z_at % 2, z_at // 2]).astype(jnp.int32)

    act = jax.nn.silu(condition.astype(F32)).astype(BF16)
    mod = dot_nn(act, ada_weight).reshape(items, 6, D)
    rw_pad = jnp.pad(router_weight, ((0, 0), (0, LANES - EXPERTS)))
    rw_t = router_weight.T
    rwt_pad = jnp.pad(jnp.concatenate([rw_t, rw_t], 0), ((0, LANES - 2 * EXPERTS), (0, 0)))

    qkv, lse, attn, rows = attn_forward(lengths, tokens, cotangent, mod, qkv_weight, out_weight)
    if fast:
        peer_rows = swap(rows, "expert", 1)
    info, pos = route(lengths, rows, rw_pad, routes, routes.T)
    sent, received = [], []
    rows_now = rows
    for j in range(local):
        sent.append(dispatch(j, local, rows_now, cotangent, mod, info, pos))
        rows_now = after(rows, sent[j])
    sres, gsh, s_act, *s_gpre = ffn_main(
        rows_now, shared_in[None], shared_out[None], 0, where if fast else None
    )
    if fast:
        peer_act = swap(s_act, "expert", 1)
        peer_gpre = swap(s_gpre[1], "expert", 1)
    for j in range(local):
        part = after(sent[j], sres) if j else sent[j]
        received.append(lax.all_to_all(part, "expert", 0, 0, tiled=True))
    back, expert_grads = [], []
    last = sres
    for j in range(local):
        rows_in = after(received[j], last)
        y, act_e, gpre_e = ffn_main(rows_in, expert_in, expert_out, j)
        back.append(lax.all_to_all(y, "expert", 0, 0, tiled=True))
        grad_rows = after(rows_in, back[j - 1]) if j else rows_in
        d2 = weight_grad("out" if fast else "plain", y_at, grad_rows, 1, act_e)
        d1 = weight_grad("in" if fast else "plain", y_at, after(rows_in, d2[0]), 0, gpre_e)
        last = d1[0]
        expert_grads.append((d1, d2))
    rows_now = after(rows, last)
    if fast:
        expert_stages = [("batch", 1), ("batch", 2), ("batch", 4)]
        shared_stages = [("expert", 2), ("batch", 1), ("batch", 2), ("batch", 4)]
        tail_stages = [("expert", 2), ("batch", 2), ("batch", 4), ("batch", 1)]
        in0, out0 = [Chain(*g, expert_stages) for g in expert_grads[0]]
        in1, out1 = [Chain(*g, expert_stages) for g in expert_grads[1]]
        out0.step()
        rows_now = after(rows_now, out0.send)
        shared_grads = shared_grad(where, rows_now, peer_rows, s_gpre[0], peer_gpre, s_act, peer_act)
        shared_sum = Chain(*shared_grads, shared_stages)
    else:
        shared_grads = (
            weight_grad("plain", y_at, rows_now, H_MLP, s_gpre[0])[0],
            weight_grad("plain", y_at, rows_now, G_SHARED, s_act)[0],
        )
    pieces = items if fast else 2
    per = items // pieces
    tok = after(tokens, shared_grads[0])
    outs, own, other = [], [], []
    for piece in range(pieces):
        outs, first, *second = backward(
            fast, where, piece * per, per, outs, lengths, tok, cotangent, mod, attn, qkv, lse,
            sres, gsh, info, back, qkv_weight, out_weight, rwt_pad,
        )
        own.append(first)
        now = (outs[0],)
        tok = after(tokens, *now)
        if fast:
            other.append(swap(second[0], "expert", 1))
            if piece == 0:
                in0.step(take_after=now)
                out0.step(take_after=now)
                tok = after(tok, in0.send, out0.send)
            elif piece == 2:
                in0.step(take_after=now)
                out0.step(take_after=now)
                tok = after(tok, in0.send, out0.terms[-1])
            elif piece == 3:
                out1.step(take_after=now)
                in0.step(take_after=now)
                shared_sum.step(take_after=now)
                where_now = after(where, out1.send, shared_sum.send, in0.terms[-1])
    result, grad_tokens, grad_mod = outs
    stacks = [rows, peer_rows] if fast else [rows]
    if not fast:
        where_now = where
    tail = tail_grad(fast, where_now, stacks, own + other)

    cols, ada_rows = 6 * D // ne, D // nb
    mod_parts = jnp.transpose(grad_mod[:, :6].reshape(items, ne, cols), (1, 0, 2))
    act_parts = jnp.transpose(act.astype(F32).reshape(items, nb, ada_rows), (1, 0, 2))
    act_parts = jnp.pad(act_parts, ((0, 0), (0, 0), (0, -ada_rows % LANES)))
    width = act_parts.shape[-1]
    parts = jnp.concatenate(
        [
            jnp.broadcast_to(mod_parts[None], (nb, ne, items, cols)),
            jnp.broadcast_to(act_parts[:, None], (nb, ne, items, width)),
        ],
        -1,
    )
    got = all_pairs(parts)

    if fast:
        def unfold(v):
            return v.reshape(96, 8, 384).transpose(2, 1, 0).reshape(384, D)

        tail_sum = Chain(*tail, tail_stages)
        token = tail[0]
        order = (
            in1, out1, tail_sum, in1, out1, shared_sum, in1,
            tail_sum, shared_sum, tail_sum, shared_sum, tail_sum,
        )
        for chain in order:
            chain.step(take_after=(token,))
            token = chain.send if chain.stages else token
        got = after(got, token)
        assert not any(c.stages for c in (in0, in1, out0, out1, shared_sum, tail_sum))
        sh, tl = shared_sum.total(), tail_sum.total()
        g_sh1 = sh[0]
        g_sh2 = sh[1].reshape(96, 2, 384).transpose(2, 1, 0).reshape(384, 192)
        g_e1 = jnp.stack([in0.total(), in1.total()])
        g_e2 = jnp.stack([unfold(out0.total()), unfold(out1.total())])
        g_qkv = tl[:, :576]
        g_out = tl[:, 576:768]
        g_rt = lax.dynamic_slice_in_dim(tl[:, 768:776], 2 * expert, 2, 1)
    else:
        def flipped(grad):
            r, c = grad.shape
            return jnp.transpose(reduce_dense_t(grad))

        def reduce_dense_t(grad):
            r, c = grad.shape
            v = reduce_expert(grad.reshape(ne, r // ne, c))
            v = jnp.transpose(v.reshape(r // ne, nb, c // nb), (1, 0, 2))
            return reduce_batch(v)

        g_sh1 = reduce_dense(shared_grads[0])
        g_sh2 = flipped(shared_grads[1])
        g_e1 = jnp.stack([reduce_local(g[0][0]) for g in expert_grads])
        g_e2 = jnp.stack([
            jnp.transpose(reduce_batch(jnp.transpose(g[1][0].reshape(D, nb, FF // nb), (1, 0, 2))))
            for g in expert_grads
        ])
        g_qkv = reduce_dense(tail[0])
        g_out = reduce_dense(tail[1])
        g_rt = reduce_dense(tail[2][:, :EXPERTS])
    got = got.reshape(nb * ne * items, cols + width)
    grad_ada = jnp.dot(
        got[:, cols : cols + ada_rows].T, got[:, :cols], precision=lax.Precision.HIGHEST
    )
    return (
        result, grad_tokens, grad_ada, g_qkv, g_out, g_rt, g_sh1, g_sh2, g_e1, g_e2
    )


def solution(mesh):
    placed = (
        P(("batch", "expert"), None),
        P(("batch", "expert"), None),
        P(("batch", "expert")),
        P(("batch", "expert"), None),
        P(("batch", "expert"), None),
        P(),
        P(),
        P(),
        P(),
        P(),
        P(),
        P("expert", None, None),
        P("expert", None, None),
    )
    return jax.shard_map(
        per_device,
        mesh=mesh,
        in_specs=placed,
        out_specs=(
            P(("batch", "expert"), None),
            P(("batch", "expert"), None),
            P("batch", "expert"),
            P("batch", "expert"),
            P("batch", "expert"),
            P("batch", "expert"),
            P("batch", "expert"),
            P("batch", "expert"),
            P("expert", "batch", None),
            P("expert", "batch", None),
        ),
        check_vma=False,
    )
```

time: 1210 us -> 508 us (0.42)
  Pallas kernels: 0 us -> 277 us
  local copies, waits for them, and re-layouts: 282 us -> 18.3 us
  matrix products: 251 us -> 5.39 us
  blocking collectives: 158 us -> 0 us
  other arithmetic: 182 us -> 42.3 us
  waiting for transfers between devices: 240 us -> 106 us
  starting transfers between devices: 66.4 us -> 49.7 us
  between operations: 16.3 us -> 1.31 us
    pallas_call x0 -> x17, Pallas kernels: none -> 277 us  [the longest x3 80.8 us: ffn_main(): pl.pallas_call(functools.partial(ffn_main_kernel, paired=paired, halved=h...]
    dot_general x28 -> x2, matrix products: 247 us -> 5.39 us  [the longest x1 4.05 us: dot_nn(): return jnp.dot(a, b, preferred_element_type=F32)]
    all_gather x2 -> x0, blocking collectives: 152 us -> none  [the longest x1 120 us: per_device(): act_all = lax.all_gather(cond_act, ('batch', 'expert'), axis=0, tiled=True)]
    reduce_sum x19 -> x0, other arithmetic: 80 us -> none  [the longest x1 38 us: per_device(): g_gate = jnp.sum(grad_mlp[:, None, :] * pair_rows, -1)]
    unnamed x2 -> x0, waiting for transfers between devices: 60.1 us -> none
    convert_element_type x16 -> x0, local copies, waits for them, and re-layouts: 56.5 us -> none  [the longest x5 10.3 us: group_sum(): low = blocks.astype(jnp.bfloat16)]
    gather x4 -> x0, local copies, waits for them, and re-layouts: 49.7 us -> none  [the longest x1 12.6 us: per_device(): g_row[slot_pair] * filled_low]
    all_to_all x11 -> x5, waiting for transfers between devices: 54.4 us -> 9.9 us  [the longest x2 9.9 us: per_device(): received.append(lax.all_to_all(part, 'expert', 0, 0, tiled=True))]
  transfers between devices with their start and end apart: 26 -> 32, of which waited for: 8 -> 10; matrix products, arithmetic and copies ran while one was open for 42% -> 10% of each run, Pallas kernels for 0% -> 49%
where the time goes in v2:
time: 508 us; the launch traced here: 500 us
  Pallas kernels  277 us (55%)
  waiting for transfers between devices  106 us (21%)
  starting transfers between devices  49.7 us (10%)
  other arithmetic  42.3 us (8%)
  local copies, waits for them, and re-layouts  18.3 us (4%)
  matrix products  5.39 us (1%)
    ppermute x27, waiting for transfers between devices, swap(): lax.ppermute(value.astype(BF16), axis, [(i, i ^ bit) for i in range(size)])  96.1 us
    pallas_call x3, Pallas kernels, ffn_main(): pl.pallas_call(functools.partial(ffn_main_kernel, paired=paired, halved=h...  80.8 us
    pallas_call x4, Pallas kernels, backward(): pl.pallas_call(functools.partial(backward_kernel, local, fast, first_item...  74.6 us
    pallas_call x4, Pallas kernels, weight_grad(): pl.pallas_call(functools.partial(weight_grad_kernel, mode), name='weight_...  39.6 us
    convert_element_type x14, other arithmetic, step(): self.send = self.total().astype(BF16)  29.3 us
    ppermute x27, starting transfers between devices, swap(): lax.ppermute(value.astype(BF16), axis, [(i, i ^ bit) for i in range(size)])  27.6 us
    pallas_call x1, Pallas kernels, shared_grad(): pl.pallas_call(shared_grad_kernel, name='shared_grad', grid_spec=pltpu.Pr...  24.8 us
    pallas_call x1, Pallas kernels, attn_forward(): pl.pallas_call(attn_forward_kernel, name='attn_forward', grid_spec=pltpu....  20.8 us
  transfers between devices with their start and end apart: 32, of which 10 were waited for; matrix products, arithmetic and copies ran while one was open for 10% of the time, Pallas kernels for 49%

profile of v2, /device:TPU:0, one launch (start us, length us, event | category | flops | bytes accessed | tf_op | source)
XLA Modules:
  0.0 500.0 jit_solution(1053105537598271893)
XLA Ops:
  0.7 4.0 fusion.31
  7.3 20.8 %attn_forward.1 = (bf16[1024,2304]{1,0:T(8,128)(2,1)}, f32[1024,128]{1,0:T(8,128)}, f32[1024,768]{1,0:T(8,128)}, bf16[4,1024,768]{2,1,0:T(8,128)(2,1)}) custom-call(s32[4]{0:T(128)} %len_ref.11, bf16[1024,768]{1,0:T(8,128)(2,1)} %tok_ref.5, bf16[1024,768]{1,0:T(8,128)(2,1)} %cot_ref.13, f32[4,6,768]{2,1,0:T(8,128)} %reshape.221.mod_ref, ...), custom_call_target="tpu_custom_call" | custom-call | flops 4049999872 | bytes 12000000 | tf_op jit(solution)/shard_map/attn_forward/pallas_call | solution.py:136
  28.1 5.7 %route.1 = (f32[1024,128]{1,0:T(8,128)}, f32[8,1024]{1,0:T(8,128)}) custom-call(s32[4]{0:T(128)} %len_ref.11, bf16[4,1024,768]{2,1,0:T(8,128)(2,1)} %get-tuple-element.119.h_ref.x_ref.g_ref.mine_ref.refs_0_, bf16[768,128]{1,0:T(8,128)(2,1)} %pad.15.rw_ref, s32[1024,2]{1,0:T(8,128)} %copy.41.rcol_ref, s32[2,1024]{1,0:T(2,128)} %bitcast.139), custom_call_target="tpu_custom_call" | custom-call | flops 500000000 | bytes 1500000 | tf_op jit(solution)/shard_map/route/pallas_call | solution.py:210
  33.9 7.8 %dispatch.2 = bf16[4,2,256,768]{3,2,1,0:T(8,128)(2,1)} custom-call(bf16[4,1024,768]{2,1,0:T(8,128)(2,1)} %get-tuple-element.119.h_ref.x_ref.g_ref.mine_ref.refs_0_, bf16[1024,768]{1,0:T(8,128)(2,1)} %cot_ref.13, f32[4,6,768]{2,1,0:T(8,128)} %reshape.221.mod_ref, f32[1024,128]{1,0:T(8,128)} %get-tuple-element.97.info_ref, f32[8,1024]{1,0:T(8,128)} %get-tuple-element.98.pos_ref), custom_call_target="tpu_custom_call" | custom-call | flops 1650000000 | bytes 4000000 | tf_op jit(solution)/shard_map/dispatch/pallas_call | solution.py:256
  41.6 4.4 all-to-all-start.1
  46.1 7.9 %dispatch.3 = bf16[4,2,256,768]{3,2,1,0:T(8,128)(2,1)} custom-call(bf16[4,1024,768]{2,1,0:T(8,128)(2,1)} %get-tuple-element.119.h_ref.x_ref.g_ref.mine_ref.refs_0_, bf16[1024,768]{1,0:T(8,128)(2,1)} %cot_ref.13, f32[4,6,768]{2,1,0:T(8,128)} %reshape.221.mod_ref, f32[1024,128]{1,0:T(8,128)} %get-tuple-element.97.info_ref, f32[8,1024]{1,0:T(8,128)} %get-tuple-element.98.pos_ref), custom_call_target="tpu_custom_call" | custom-call | flops 1650000000 | bytes 4000000 | tf_op jit(solution)/shard_map/dispatch/pallas_call | solution.py:256
  54.6 27.9 %ffn_main_shared.1 = (f32[1024,768]{1,0:T(8,128)}, f32[1024,768]{1,0:T(8,128)}, bf16[1024,3072]{1,0:T(8,128)(2,1)}, bf16[1024,1536]{1,0:T(8,128)(2,1)}, bf16[1024,1536]{1,0:T(8,128)(2,1)}) custom-call(s32[5]{0:T(128)} %stack.41.where_ref, bf16[4,1024,768]{2,1,0:T(8,128)(2,1)} %get-tuple-element.119.h_ref.x_ref.g_ref.mine_ref.refs_0_, ...), custom_call_target="tpu_custom_call" | custom-call | flops 9663676416 | bytes 15000000 | tf_op jit(solution)/shard_map/ffn_main_shared/pallas_call | solution.py:338
  83.0 1.6 copy-done.1
  84.7 4.6 all-to-all-start
  90.5 26.5 %ffn_main_pairs.2 = (bf16[4,2,256,768]{3,2,1,0:T(8,128)(2,1)}, bf16[1024,3072]{1,0:T(8,128)(2,1)}, bf16[1024,3072]{1,0:T(8,128)(2,1)}) custom-call(s32[1]{0:T(128)} %constant.72.clone.1.where_ref, bf16[4,2,256,768]{3,2,1,0:T(8,128)(2,1)} %copy-done.1, bf16[8,768]{1,0:T(8,128)(2,1)} %broadcast_3_g_ref.2.g_ref, bf16[2,768,3072]{2,1,0:T(8,128)(2,1)} %w1_ref.3, ...), custom_call_target="tpu_custom_call" | custom-call | flops 9663676416 | bytes 15000000 | tf_op jit(solution)/shard_map/ffn_main_pairs/pallas_call | solution.py:338
  117.0 9.3 %all-to-all-done.x_ref.a_ref = bf16[4,2,256,768]{3,2,1,0:T(8,128)(2,1)} async-done(((bf16[4,2,256,768]{3,2,1,0:T(8,128)(2,1)}), bf16[4,2,256,768]{3,2,1,0:T(8,128)(2,1)}, u32[]{:S(2)}, u32[]{:S(2)}) %all-to-all-start) | async-done | bytes 3145760 | tf_op jit(solution)/shard_map/all_to_all | solution.py:842
  126.3 4.1 all-to-all-start.2
  131.0 9.9 %weight_grad_out.2 = (bf16[2,2,96,3072]{3,2,1,0:T(8,128)(2,1)}, bf16[2,2,96,3072]{3,2,1,0:T(8,128)(2,1)}) custom-call(s32[3]{0:T(128)} %pad_add_fusion.where_ref, bf16[4,2,256,768]{3,2,1,0:T(8,128)(2,1)} %copy-done.1, bf16[1024,3072]{1,0:T(8,128)(2,1)} %get-tuple-element.104.b_ref), custom_call_target="tpu_custom_call" | custom-call | flops 2415919104 | bytes 6500000 | tf_op jit(solution)/shard_map/weight_grad_out/pallas_call | solution.py:400
  140.9 2.3 collective-permute-start
  143.5 9.9 %weight_grad_in.2 = (bf16[2,2,96,3072]{3,2,1,0:T(8,128)(2,1)}, bf16[2,2,96,3072]{3,2,1,0:T(8,128)(2,1)}) custom-call(s32[3]{0:T(128)} %pad_add_fusion.where_ref, bf16[4,2,256,768]{3,2,1,0:T(8,128)(2,1)} %copy-done.1, bf16[1024,3072]{1,0:T(8,128)(2,1)} %get-tuple-element.107.b_ref), custom_call_target="tpu_custom_call" | custom-call | flops 2415919104 | bytes 6500000 | tf_op jit(solution)/shard_map/weight_grad_in/pallas_call | solution.py:400
  153.4 26.5 %ffn_main_pairs.3 = (bf16[4,2,256,768]{3,2,1,0:T(8,128)(2,1)}, bf16[1024,3072]{1,0:T(8,128)(2,1)}, bf16[1024,3072]{1,0:T(8,128)(2,1)}) custom-call(s32[1]{0:T(128)} %constant.72.clone.1.where_ref, bf16[4,2,256,768]{3,2,1,0:T(8,128)(2,1)} %all-to-all-done.x_ref.a_ref, bf16[8,768]{1,0:T(8,128)(2,1)} %broadcast_3_g_ref.2.g_ref, bf16[2,768,3072]{2,1,0:T(8,128)(2,1)} %w1_ref.3, ...), custom_call_target="tpu_custom_call" | custom-call | flops 9663676416 | bytes 15000000 | tf_op jit(solution)/shard_map/ffn_main_pairs/pallas_call | solution.py:338
  179.9 1.7 copy-done
  181.5 4.7 all-to-all-start.3
  186.6 9.1 %collective-permute-done = bf16[2,2,96,3072]{3,2,1,0:T(8,128)(2,1)} collective-permute-done((bf16[2,2,96,3072]{3,2,1,0:T(8,128)(2,1)}, bf16[2,2,96,3072]{3,2,1,0:T(8,128)(2,1)}, u32[]{:S(2)}, u32[]{:S(2)}) %collective-permute-start) | collective-permute-done | bytes 2359328 | tf_op jit(solution)/shard_map/ppermute | solution.py:730
  195.7 2.0 fusion
  197.7 2.1 collective-permute-start.5
  200.5 9.9 %weight_grad_out.3 = (bf16[2,2,96,3072]{3,2,1,0:T(8,128)(2,1)}, bf16[2,2,96,3072]{3,2,1,0:T(8,128)(2,1)}) custom-call(s32[3]{0:T(128)} %pad_add_fusion.where_ref, bf16[4,2,256,768]{3,2,1,0:T(8,128)(2,1)} %all-to-all-done.x_ref.a_ref, bf16[1024,3072]{1,0:T(8,128)(2,1)} %get-tuple-element.112.b_ref), custom_call_target="tpu_custom_call" | custom-call | flops 2415919104 | bytes 6500000 | tf_op jit(solution)/shard_map/weight_grad_out/pallas_call | solution.py:400
  210.4 9.9 %weight_grad_in.3 = (bf16[2,2,96,3072]{3,2,1,0:T(8,128)(2,1)}, bf16[2,2,96,3072]{3,2,1,0:T(8,128)(2,1)}) custom-call(s32[3]{0:T(128)} %pad_add_fusion.where_ref, bf16[4,2,256,768]{3,2,1,0:T(8,128)(2,1)} %all-to-all-done.x_ref.a_ref, bf16[1024,3072]{1,0:T(8,128)(2,1)} %get-tuple-element.115.b_ref), custom_call_target="tpu_custom_call" | custom-call | flops 2415919104 | bytes 6500000 | tf_op jit(solution)/shard_map/weight_grad_in/pallas_call | solution.py:400
  220.3 1.5 collective-permute-start.8
  221.8 24.8 %shared_grad.1 = (bf16[2,2,2,2,96,768]{5,4,3,2,1,0:T(8,128)(2,1)}, bf16[2,2,2,2,96,768]{5,4,3,2,1,0:T(8,128)(2,1)}) custom-call(s32[5]{0:T(128)} %stack.41.where_ref, bf16[4,1024,768]{2,1,0:T(8,128)(2,1)} %get-tuple-element.119.h_ref.x_ref.g_ref.mine_ref.refs_0_, bf16[4,1024,768]{2,1,0:T(8,128)(2,1)} %collective-permute-done.1.peer_ref.refs_1_, ...), custom_call_target="tpu_custom_call" | custom-call | flops 4831838208 | bytes 12500000 | tf_op jit(solution)/shard_map/shared_grad/pallas_call | solution.py:469
  246.6 18.5 %backward.4 = (bf16[1024,768]{1,0:T(8,128)(2,1)}, f32[1024,768]{1,0:T(8,128)}, f32[4,8,768]{2,1,0:T(8,128)}, bf16[256,1664]{1,0:T(8,128)(2,1)}, bf16[256,1664]{1,0:T(8,128)(2,1)}) custom-call(s32[4]{0:T(128)} %len_ref.11, s32[5]{0:T(128)} %stack.41.where_ref, bf16[1024,768]{1,0:T(8,128)(2,1)} %tok_ref.5, bf16[1024,768]{1,0:T(8,128)(2,1)} %cot_ref.13, ...), custom_call_target="tpu_custom_call" | custom-call | flops 2500000000 | bytes 3500000 | tf_op jit(solution)/shard_map/backward/pallas_call | solution.py:611
  265.2 2.7 fusion.1
  268.4 2.5 fusion.15
  270.8 2.6 collective-permute-start.7
  273.4 1.9 collective-permute-start.9
  276.0 18.8 %backward.5 = (bf16[1024,768]{1,0:T(8,128)(2,1)}, f32[1024,768]{1,0:T(8,128)}, f32[4,8,768]{2,1,0:T(8,128)}, bf16[256,1664]{1,0:T(8,128)(2,1)}, bf16[256,1664]{1,0:T(8,128)(2,1)}) custom-call(s32[4]{0:T(128)} %len_ref.11, s32[5]{0:T(128)} %stack.41.where_ref, ...), custom_call_target="tpu_custom_call", output_to_operand_aliasing={{0}: (16, {}), {1}: (17, {}), {2}: (18, {})} | custom-call | flops 2500000000 | bytes 3500000 | tf_op jit(solution)/shard_map/backward/pallas_call | solution.py:611
  294.8 18.7 %backward.6 = (bf16[1024,768]{1,0:T(8,128)(2,1)}, f32[1024,768]{1,0:T(8,128)}, f32[4,8,768]{2,1,0:T(8,128)}, bf16[256,1664]{1,0:T(8,128)(2,1)}, bf16[256,1664]{1,0:T(8,128)(2,1)}) custom-call(s32[4]{0:T(128)} %len_ref.11, s32[5]{0:T(128)} %stack.41.where_ref, ...), custom_call_target="tpu_custom_call", output_to_operand_aliasing={{0}: (16, {}), {1}: (17, {}), {2}: (18, {})} | custom-call | flops 2500000000 | bytes 3500000 | tf_op jit(solution)/shard_map/backward/pallas_call | solution.py:611
  313.6 2.5 fusion.14
  316.2 1.9 fusion.6
  318.2 18.6 %backward.7 = (bf16[1024,768]{1,0:T(8,128)(2,1)}, f32[1024,768]{1,0:T(8,128)}, f32[4,8,768]{2,1,0:T(8,128)}, bf16[256,1664]{1,0:T(8,128)(2,1)}, bf16[256,1664]{1,0:T(8,128)(2,1)}) custom-call(s32[4]{0:T(128)} %len_ref.11, s32[5]{0:T(128)} %stack.41.where_ref, ...), custom_call_target="tpu_custom_call", output_to_operand_aliasing={{0}: (16, {}), {1}: (17, {}), {2}: (18, {})} | custom-call | flops 2500000000 | bytes 3500000 | tf_op jit(solution)/shard_map/backward/pallas_call | solution.py:611
  337.3 1.6 reshape.222
  339.8 5.9 %collective-permute-done.10 = bf16[96,3072]{1,0:T(8,128)(2,1)} collective-permute-done((bf16[96,3072]{1,0:T(8,128)(2,1)}, bf16[96,3072]{1,0:T(8,128)(2,1)}, u32[]{:S(2)}, u32[]{:S(2)}) %collective-permute-start.10) | collective-permute-done | bytes 589856 | tf_op jit(solution)/shard_map/ppermute | solution.py:730
  346.2 2.9 fusion.2
  349.1 2.6 fusion.3
  352.9 15.0 %tail_grad.1 = (bf16[2,2,2,96,896]{4,3,2,1,0:T(8,128)(2,1)}, bf16[2,2,2,96,896]{4,3,2,1,0:T(8,128)(2,1)}) custom-call(s32[5]{0:T(128)} %stack.41.where_ref, bf16[4,1024,768]{2,1,0:T(8,128)(2,1)} %get-tuple-element.119.h_ref.x_ref.g_ref.mine_ref.refs_0_, bf16[4,1024,768]{2,1,0:T(8,128)(2,1)} %collective-permute-done.1.peer_ref.refs_1_, ...), custom_call_target="tpu_custom_call" | custom-call | flops 2500000000 | bytes 10000000 | tf_op jit(solution)/shard_map/tail_grad/pallas_call | solution.py:688
  368.0 2.7 fusion.4
  370.7 2.0 collective-permute-start.20
  373.8 4.3 all-to-all-start.4
  378.1 1.9 collective-permute-start.19
  380.8 1.6 fusion.13
  382.5 1.7 collective-permute-start.26
  384.2 18.8 %collective-permute-done.15 = bf16[2,2,2,96,896]{4,3,2,1,0:T(8,128)(2,1)} collective-permute-done((bf16[2,2,2,96,896]{4,3,2,1,0:T(8,128)(2,1)}, bf16[2,2,2,96,896]{4,3,2,1,0:T(8,128)(2,1)}, u32[]{:S(2)}, u32[]{:S(2)}) %collective-permute-start.15) | collective-permute-done | bytes 1376288 | tf_op jit(solution)/shard_map/ppermute | solution.py:730
  403.0 2.1 fusion.16
  405.1 1.7 collective-permute-start.18
  406.8 18.9 %collective-permute-done.20 = bf16[2,96,3072]{2,1,0:T(8,128)(2,1)} collective-permute-done((bf16[2,96,3072]{2,1,0:T(8,128)(2,1)}, bf16[2,96,3072]{2,1,0:T(8,128)(2,1)}, u32[]{:S(2)}, u32[]{:S(2)}) %collective-permute-start.20) | collective-permute-done | bytes 1179680 | tf_op jit(solution)/shard_map/ppermute | solution.py:730
  425.8 2.3 fusion.12
  428.1 1.7 fusion.5
  430.2 1.9 copy.48
  432.2 1.7 fusion.11
  433.9 1.8 collective-permute-start.22
  435.8 19.3 %collective-permute-done.25 = bf16[96,3072]{1,0:T(8,128)(2,1)} collective-permute-done((bf16[96,3072]{1,0:T(8,128)(2,1)}, bf16[96,3072]{1,0:T(8,128)(2,1)}, u32[]{:S(2)}, u32[]{:S(2)}) %collective-permute-start.25) | collective-permute-done | bytes 589856 | tf_op jit(solution)/shard_map/ppermute | solution.py:730
  455.1 2.8 fusion.8
  459.1 2.6 collective-permute-start.21
  461.7 13.0 %collective-permute-done.22 = bf16[2,2,96,768]{3,2,1,0:T(8,128)(2,1)S(1)} collective-permute-done((bf16[2,2,96,768]{3,2,1,0:T(8,128)(2,1)S(1)}, bf16[2,2,96,768]{3,2,1,0:T(8,128)(2,1)S(1)}, u32[]{:S(2)}, u32[]{:S(2)}) %collective-permute-start.22) | collective-permute-done | bytes 589856 | tf_op jit(solution)/shard_map/ppermute | solution.py:730
  476.3 1.6 pad_maximum_fusion
  478.9 1.6 collective-permute-start.23
  480.6 10.2 %collective-permute-done.24 = bf16[2,96,768]{2,1,0:T(8,128)(2,1)S(1)} collective-permute-done((bf16[2,96,768]{2,1,0:T(8,128)(2,1)S(1)}, bf16[2,96,768]{2,1,0:T(8,128)(2,1)S(1)}, u32[]{:S(2)}, u32[]{:S(2)}) %collective-permute-start.24) | collective-permute-done | bytes 294944 | tf_op jit(solution)/shard_map/ppermute | solution.py:730
  490.8 1.3 fusion.20
  495.1 1.3 fusion.18
  (99 shorter events, 23.8 us)
Async XLA Ops:
  0.6 4.8 copy-start.13
  0.7 5.8 %copy-start.12 = (bf16[768,8]{0,1:T(8,128)(2,1)S(1)}, bf16[768,8]{0,1:T(8,128)(2,1)}, u32[]{:S(2)}) copy-start(bf16[768,8]{0,1:T(8,128)(2,1)} %param.21) | copy-start | bytes 36868
  41.6 41.4 %all-to-all-start.1 = ((bf16[4,2,256,768]{3,2,1,0:T(8,128)(2,1)}), bf16[4,2,256,768]{3,2,1,0:T(8,128)(2,1)S(1)}, u32[]{:S(2)}, u32[]{:S(2)}) async-start(bf16[4,2,256,768]{3,2,1,0:T(8,128)(2,1)} %dispatch.2), calls=%async_computation.1 | async-start | bytes 6291456 | tf_op jit(solution)/shard_map/all_to_all | solution.py:842
  83.0 1.6 copy-start.1
  84.7 41.7 %all-to-all-start = ((bf16[4,2,256,768]{3,2,1,0:T(8,128)(2,1)}), bf16[4,2,256,768]{3,2,1,0:T(8,128)(2,1)}, u32[]{:S(2)}, u32[]{:S(2)}) async-start(bf16[4,2,256,768]{3,2,1,0:T(8,128)(2,1)} %dispatch.3), calls=%async_computation | async-start | bytes 6291456 | tf_op jit(solution)/shard_map/all_to_all | solution.py:842
  89.3 132.5 %collective-permute-start.3 = (bf16[1024,3072]{1,0:T(8,128)(2,1)}, bf16[1024,3072]{1,0:T(8,128)(2,1)}, u32[]{:S(2)}, u32[]{:S(2)}) collective-permute-start(bf16[1024,3072]{1,0:T(8,128)(2,1)} %get-tuple-element.122.act_ref), channel_id=1, source_target_pairs={{0,1},{1,0},{2,3},{3,2},{4,5},{5,4},{6,7},{7,6},{8,9},{9,8},{10,11... | collective-permute-start | bytes 18874376 | tf_op jit(solution)/shard_map/ppermute | solution.py:730
  89.8 132.0 %collective-permute-start.1 = (bf16[4,1024,768]{2,1,0:T(8,128)(2,1)}, bf16[4,1024,768]{2,1,0:T(8,128)(2,1)}, u32[]{:S(2)}, u32[]{:S(2)}) collective-permute-start(bf16[4,1024,768]{2,1,0:T(8,128)(2,1)} %get-tuple-element.119.h_ref.x_ref.g_ref.mine_ref.refs_0_), channel_id=1, source_target_pairs={{0,1},{1,0},{2,3},{3,2},{4,5},{5,4},{6,7},{7,6},{8,9},{9,8},{10,11... | collective-permute-start | bytes 18874376 | tf_op jit(solution)/shard_map/ppermute | solution.py:730
  126.3 53.5 %all-to-all-start.2 = ((bf16[4,2,256,768]{3,2,1,0:T(8,128)(2,1)}), bf16[4,2,256,768]{3,2,1,0:T(8,128)(2,1)S(1)}, u32[]{:S(2)}, u32[]{:S(2)}) async-start(bf16[4,2,256,768]{3,2,1,0:T(8,128)(2,1)} %get-tuple-element.110), calls=%async_computation.2 | async-start | bytes 6291456 | tf_op jit(solution)/shard_map/all_to_all | solution.py:848
  140.9 54.8 %collective-permute-start = (bf16[2,2,96,3072]{3,2,1,0:T(8,128)(2,1)}, bf16[2,2,96,3072]{3,2,1,0:T(8,128)(2,1)}, u32[]{:S(2)}, u32[]{:S(2)}) collective-permute-start(bf16[2,2,96,3072]{3,2,1,0:T(8,128)(2,1)} %get-tuple-element.118), channel_id=1, source_target_pairs={{0,4},{4,0},{8,12},{12,8},{16,20},{20,16},{24,28},{28,24},{1,5},{5... | collective-permute-start | bytes 7077896 | tf_op jit(solution)/shard_map/ppermute | solution.py:730
  143.3 77.0 %collective-permute-start.2 = (bf16[1024,1536]{1,0:T(8,128)(2,1)}, bf16[1024,1536]{1,0:T(8,128)(2,1)}, u32[]{:S(2)}, u32[]{:S(2)}) collective-permute-start(bf16[1024,1536]{1,0:T(8,128)(2,1)} %get-tuple-element.121), channel_id=1, source_target_pairs={{0,1},{1,0},{2,3},{3,2},{4,5},{5,4},{6,7},{7,6},{8,9},{9,8},{10,11... | collective-permute-start | bytes 9437192 | tf_op jit(solution)/shard_map/ppermute | solution.py:730
  179.8 1.7 copy-start
  181.5 65.1 %all-to-all-start.3 = ((bf16[4,2,256,768]{3,2,1,0:T(8,128)(2,1)}), bf16[4,2,256,768]{3,2,1,0:T(8,128)(2,1)}, u32[]{:S(2)}, u32[]{:S(2)}) async-start(bf16[4,2,256,768]{3,2,1,0:T(8,128)(2,1)} %get-tuple-element.129), calls=%async_computation.3 | async-start | bytes 6291456 | tf_op jit(solution)/shard_map/all_to_all | solution.py:848
  186.2 79.0 %collective-permute-start.4 = (bf16[2,2,96,3072]{3,2,1,0:T(8,128)(2,1)}, bf16[2,2,96,3072]{3,2,1,0:T(8,128)(2,1)}, u32[]{:S(2)}, u32[]{:S(2)}) collective-permute-start(bf16[2,2,96,3072]{3,2,1,0:T(8,128)(2,1)} %get-tuple-element.132), channel_id=1, source_target_pairs={{0,4},{4,0},{8,12},{12,8},{16,20},{20,16},{24,28},{28,24},{1,5},{5... | collective-permute-start | bytes 7077896 | tf_op jit(solution)/shard_map/ppermute | solution.py:730
  197.7 67.4 %collective-permute-start.5 = (bf16[2,96,3072]{2,1,0:T(8,128)(2,1)S(1)}, bf16[2,96,3072]{2,1,0:T(8,128)(2,1)}, u32[]{:S(2)}, u32[]{:S(2)}) collective-permute-start(bf16[2,96,3072]{2,1,0:T(8,128)(2,1)S(1)} %fusion), channel_id=1, source_target_pairs={{0,8},{4,12},{8,0},{12,4},{16,24},{20,28},{24,16},{28,20},{1,9},{5... | collective-permute-start | bytes 3538952 | tf_op jit(solution)/shard_map/ppermute | solution.py:730
  220.3 116.5 %collective-permute-start.8 = (bf16[2,2,96,3072]{3,2,1,0:T(8,128)(2,1)}, bf16[2,2,96,3072]{3,2,1,0:T(8,128)(2,1)}, u32[]{:S(2)}, u32[]{:S(2)}) collective-permute-start(bf16[2,2,96,3072]{3,2,1,0:T(8,128)(2,1)} %get-tuple-element.152), channel_id=1, source_target_pairs={{0,4},{4,0},{8,12},{12,8},{16,20},{20,16},{24,28},{28,24},{1,5},{5... | collective-permute-start | bytes 7077896 | tf_op jit(solution)/shard_map/ppermute | solution.py:730
  246.6 18.5 %copy-start.2 = (bf16[2,2,96,3072]{3,2,1,0:T(8,128)(2,1)S(1)}, bf16[2,2,96,3072]{3,2,1,0:T(8,128)(2,1)}, u32[]{:S(2)}) copy-start(bf16[2,2,96,3072]{3,2,1,0:T(8,128)(2,1)} %get-tuple-element.108) | copy-start | bytes 7077892
  267.9 7.4 %copy-start.14 = (bf16[4,768]{1,0:T(4,128)(2,1)S(1)}, bf16[4,768]{1,0:T(4,128)(2,1)}, u32[]{:S(2)}) copy-start(bf16[4,768]{1,0:T(4,128)(2,1)} %param.14) | copy-start | bytes 18436
  267.9 45.7 %collective-permute-start.6 = (bf16[2,96,3072]{2,1,0:T(8,128)(2,1)}, bf16[2,96,3072]{2,1,0:T(8,128)(2,1)S(1)}, u32[]{:S(2)}, u32[]{:S(2)}) collective-permute-start(bf16[2,96,3072]{2,1,0:T(8,128)(2,1)} %fusion.1), channel_id=1, source_target_pairs={{0,8},{4,12},{8,0},{12,4},{16,24},{20,28},{24,16},{28,20},{1,9},{5... | collective-permute-start | bytes 3538952 | tf_op jit(solution)/shard_map/ppermute | solution.py:730
  270.8 42.7 %collective-permute-start.7 = (bf16[96,3072]{1,0:T(8,128)(2,1)}, bf16[96,3072]{1,0:T(8,128)(2,1)}, u32[]{:S(2)}, u32[]{:S(2)}) collective-permute-start(bf16[96,3072]{1,0:T(8,128)(2,1)} %fusion.15), channel_id=1, source_target_pairs={{0,16},{4,20},{8,24},{12,28},{16,0},{20,4},{24,8},{28,12},{1,17},{... | collective-permute-start | bytes 1769480 | tf_op jit(solution)/shard_map/ppermute | solution.py:730
  273.4 72.3 %collective-permute-start.9 = (bf16[2,2,2,2,96,768]{5,4,3,2,1,0:T(8,128)(2,1)}, bf16[2,2,2,2,96,768]{5,4,3,2,1,0:T(8,128)(2,1)}, u32[]{:S(2)}, u32[]{:S(2)}) collective-permute-start(bf16[2,2,2,2,96,768]{5,4,3,2,1,0:T(8,128)(2,1)} %get-tuple-element.154), channel_id=1, source_target_pairs={{0,2},{1,3},{2,0},{3,1},{4,6},{5,7},{6,4},{7,5},{8,10},{9,11},{10,... | collective-permute-start | bytes 7077896 | tf_op jit(solution)/shard_map/ppermute | solution.py:730
  275.5 92.5 %collective-permute-start.17 = (bf16[2,2,96,3072]{3,2,1,0:T(8,128)(2,1)}, bf16[2,2,96,3072]{3,2,1,0:T(8,128)(2,1)}, u32[]{:S(2)}, u32[]{:S(2)}) collective-permute-start(bf16[2,2,96,3072]{3,2,1,0:T(8,128)(2,1)} %get-tuple-element.168), channel_id=1, source_target_pairs={{0,4},{4,0},{8,12},{12,8},{16,20},{20,16},{24,28},{28,24},{1,5},{5... | collective-permute-start | bytes 7077896 | tf_op jit(solution)/shard_map/ppermute | solution.py:730
  313.5 38.2 %collective-permute-start.13 = (bf16[256,1664]{1,0:T(8,128)(2,1)}, bf16[256,1664]{1,0:T(8,128)(2,1)}, u32[]{:S(2)}, u32[]{:S(2)}) collective-permute-start(bf16[256,1664]{1,0:T(8,128)(2,1)} %get-tuple-element.164), channel_id=1, source_target_pairs={{0,1},{1,0},{2,3},{3,2},{4,5},{5,4},{6,7},{7,6},{8,9},{9,8},{10,11... | collective-permute-start | bytes 2555912 | tf_op jit(solution)/shard_map/ppermute | solution.py:730
  313.6 4.4 copy-start.8
  316.1 29.5 %collective-permute-start.10 = (bf16[96,3072]{1,0:T(8,128)(2,1)}, bf16[96,3072]{1,0:T(8,128)(2,1)}, u32[]{:S(2)}, u32[]{:S(2)}) collective-permute-start(bf16[96,3072]{1,0:T(8,128)(2,1)} %fusion.14), channel_id=1, source_target_pairs={{0,16},{4,20},{8,24},{12,28},{16,0},{20,4},{24,8},{28,12},{1,17},{... | collective-permute-start | bytes 1769480 | tf_op jit(solution)/shard_map/ppermute | solution.py:730
  318.2 28.1 %copy-start.4 = (bf16[2,2,96,3072]{3,2,1,0:T(8,128)(2,1)S(1)}, bf16[2,2,96,3072]{3,2,1,0:T(8,128)(2,1)}, u32[]{:S(2)}) copy-start(bf16[2,2,96,3072]{3,2,1,0:T(8,128)(2,1)} %get-tuple-element.113) | copy-start | bytes 7077892
  336.8 14.9 %collective-permute-start.12 = (bf16[256,1664]{1,0:T(8,128)(2,1)}, bf16[256,1664]{1,0:T(8,128)(2,1)}, u32[]{:S(2)}, u32[]{:S(2)}) collective-permute-start(bf16[256,1664]{1,0:T(8,128)(2,1)} %get-tuple-element.163), channel_id=1, source_target_pairs={{0,1},{1,0},{2,3},{3,2},{4,5},{5,4},{6,7},{7,6},{8,9},{9,8},{10,11... | collective-permute-start | bytes 2555912 | tf_op jit(solution)/shard_map/ppermute | solution.py:730
  345.7 6.0 %collective-permute-start.11 = (bf16[256,1664]{1,0:T(8,128)(2,1)}, bf16[256,1664]{1,0:T(8,128)(2,1)S(1)}, u32[]{:S(2)}, u32[]{:S(2)}) collective-permute-start(bf16[256,1664]{1,0:T(8,128)(2,1)} %get-tuple-element.162), channel_id=1, source_target_pairs={{0,1},{1,0},{2,3},{3,2},{4,5},{5,4},{6,7},{7,6},{8,9},{9,8},{10,11... | collective-permute-start | bytes 2555912 | tf_op jit(solution)/shard_map/ppermute | solution.py:730
  345.7 3.4 copy-start.5
  345.7 6.0 %collective-permute-start.14 = (bf16[256,1664]{1,0:T(8,128)(2,1)}, bf16[256,1664]{1,0:T(8,128)(2,1)S(1)}, u32[]{:S(2)}, u32[]{:S(2)}) collective-permute-start(bf16[256,1664]{1,0:T(8,128)(2,1)} %get-tuple-element.165), channel_id=1, source_target_pairs={{0,1},{1,0},{2,3},{3,2},{4,5},{5,4},{6,7},{7,6},{8,9},{9,8},{10,11... | collective-permute-start | bytes 2555912 | tf_op jit(solution)/shard_map/ppermute | solution.py:730
  351.7 29.1 %collective-permute-start.16 = (bf16[2,96,3072]{2,1,0:T(8,128)(2,1)}, bf16[2,96,3072]{2,1,0:T(8,128)(2,1)}, u32[]{:S(2)}, u32[]{:S(2)}) collective-permute-start(bf16[2,96,3072]{2,1,0:T(8,128)(2,1)} %fusion.2), channel_id=1, source_target_pairs={{0,8},{4,12},{8,0},{12,4},{16,24},{20,28},{24,16},{28,20},{1,9},{5... | collective-permute-start | bytes 3538952 | tf_op jit(solution)/shard_map/ppermute | solution.py:730
  351.7 1.0 copy-start.10
  351.7 1.2 copy-start.11
  352.9 15.1 %copy-start.3 = (bf16[2,2,96,3072]{3,2,1,0:T(8,128)(2,1)S(1)}, bf16[2,2,96,3072]{3,2,1,0:T(8,128)(2,1)}, u32[]{:S(2)}) copy-start(bf16[2,2,96,3072]{3,2,1,0:T(8,128)(2,1)} %get-tuple-element.116) | copy-start | bytes 7077892
  367.9 35.1 %collective-permute-start.15 = (bf16[2,2,2,96,896]{4,3,2,1,0:T(8,128)(2,1)}, bf16[2,2,2,96,896]{4,3,2,1,0:T(8,128)(2,1)}, u32[]{:S(2)}, u32[]{:S(2)}) collective-permute-start(bf16[2,2,2,96,896]{4,3,2,1,0:T(8,128)(2,1)} %get-tuple-element.167), channel_id=1, source_target_pairs={{0,2},{1,3},{2,0},{3,1},{4,6},{5,7},{6,4},{7,5},{8,10},{9,11},{10,... | collective-permute-start | bytes 4128776 | tf_op jit(solution)/shard_map/ppermute | solution.py:730
  370.7 55.1 %collective-permute-start.20 = (bf16[2,96,3072]{2,1,0:T(8,128)(2,1)}, bf16[2,96,3072]{2,1,0:T(8,128)(2,1)}, u32[]{:S(2)}, u32[]{:S(2)}) collective-permute-start(bf16[2,96,3072]{2,1,0:T(8,128)(2,1)} %fusion.4), channel_id=1, source_target_pairs={{0,8},{4,12},{8,0},{12,4},{16,24},{20,28},{24,16},{28,20},{1,9},{5... | collective-permute-start | bytes 3538952 | tf_op jit(solution)/shard_map/ppermute | solution.py:730
  373.8 120.0 %all-to-all-start.4 = ((f32[32,4,1280]{2,1,0:T(4,128)}), f32[32,4,1280]{2,1,0:T(4,128)}, u32[]{:S(2)}, u32[]{:S(2)}) async-start(f32[32,4,1280]{2,1,0:T(4,128)} %bitcast.17), calls=%async_computation.4 | async-start | bytes 1310720 | tf_op jit(solution)/shard_map/all_to_all | solution.py:800
  378.1 24.9 %copy-start.6 = (bf16[2,2,2,96,896]{4,3,2,1,0:T(8,128)(2,1)S(1)}, bf16[2,2,2,96,896]{4,3,2,1,0:T(8,128)(2,1)}, u32[]{:S(2)}) copy-start(bf16[2,2,2,96,896]{4,3,2,1,0:T(8,128)(2,1)} %get-tuple-element.166) | copy-start | bytes 4128772
  378.1 54.0 %collective-permute-start.19 = (bf16[2,2,2,96,768]{4,3,2,1,0:T(8,128)(2,1)}, bf16[2,2,2,96,768]{4,3,2,1,0:T(8,128)(2,1)}, u32[]{:S(2)}, u32[]{:S(2)}) collective-permute-start(bf16[2,2,2,96,768]{4,3,2,1,0:T(8,128)(2,1)} %fusion.3), channel_id=1, source_target_pairs={{0,4},{4,0},{8,12},{12,8},{16,20},{20,16},{24,28},{28,24},{1,5},{5... | collective-permute-start | bytes 3538952 | tf_op jit(solution)/shard_map/ppermute | solution.py:730
  382.5 45.6 %collective-permute-start.26 = (bf16[96,3072]{1,0:T(8,128)(2,1)S(1)}, bf16[96,3072]{1,0:T(8,128)(2,1)S(1)}, u32[]{:S(2)}, u32[]{:S(2)}) collective-permute-start(bf16[96,3072]{1,0:T(8,128)(2,1)S(1)} %fusion.13), channel_id=1, source_target_pairs={{0,16},{4,20},{8,24},{12,28},{16,0},{20,4},{24,8},{28,12},{1,17},{... | collective-permute-start | bytes 1769480 | tf_op jit(solution)/shard_map/ppermute | solution.py:730
  405.1 52.8 %collective-permute-start.18 = (bf16[2,2,96,896]{3,2,1,0:T(8,128)(2,1)}, bf16[2,2,96,896]{3,2,1,0:T(8,128)(2,1)}, u32[]{:S(2)}, u32[]{:S(2)}) collective-permute-start(bf16[2,2,96,896]{3,2,1,0:T(8,128)(2,1)} %fusion.16), channel_id=1, source_target_pairs={{0,8},{4,12},{8,0},{12,4},{16,24},{20,28},{24,16},{28,20},{1,9},{5... | collective-permute-start | bytes 2064392 | tf_op jit(solution)/shard_map/ppermute | solution.py:730
  428.1 27.0 %collective-permute-start.25 = (bf16[96,3072]{1,0:T(8,128)(2,1)}, bf16[96,3072]{1,0:T(8,128)(2,1)}, u32[]{:S(2)}, u32[]{:S(2)}) collective-permute-start(bf16[96,3072]{1,0:T(8,128)(2,1)} %fusion.12), channel_id=1, source_target_pairs={{0,16},{4,20},{8,24},{12,28},{16,0},{20,4},{24,8},{28,12},{1,17},{... | collective-permute-start | bytes 1769480 | tf_op jit(solution)/shard_map/ppermute | solution.py:730
  432.2 22.9 %copy-start.9 = (bf16[2,96,3072]{2,1,0:T(8,128)(2,1)S(1)}, bf16[2,96,3072]{2,1,0:T(8,128)(2,1)}, u32[]{:S(2)}) copy-start(bf16[2,96,3072]{2,1,0:T(8,128)(2,1)} %copy-done.8) | copy-start | bytes 3538948
  433.9 24.0 %copy-start.7 = (bf16[2,2,2,96,896]{4,3,2,1,0:T(8,128)(2,1)S(1)}, bf16[2,2,2,96,896]{4,3,2,1,0:T(8,128)(2,1)}, u32[]{:S(2)}) copy-start(bf16[2,2,2,96,896]{4,3,2,1,0:T(8,128)(2,1)} %get-tuple-element.166) | copy-start | bytes 4128772
  433.9 40.8 %collective-permute-start.22 = (bf16[2,2,96,768]{3,2,1,0:T(8,128)(2,1)S(1)}, bf16[2,2,96,768]{3,2,1,0:T(8,128)(2,1)S(1)}, u32[]{:S(2)}, u32[]{:S(2)}) collective-permute-start(bf16[2,2,96,768]{3,2,1,0:T(8,128)(2,1)S(1)} %fusion.11), channel_id=1, source_target_pairs={{0,8},{4,12},{8,0},{12,4},{16,24},{20,28},{24,16},{28,20},{1,9},{5... | collective-permute-start | bytes 1769480 | tf_op jit(solution)/shard_map/ppermute | solution.py:730
  459.1 18.7 %collective-permute-start.21 = (bf16[2,96,896]{2,1,0:T(8,128)(2,1)S(1)}, bf16[2,96,896]{2,1,0:T(8,128)(2,1)S(1)}, u32[]{:S(2)}, u32[]{:S(2)}) collective-permute-start(bf16[2,96,896]{2,1,0:T(8,128)(2,1)S(1)} %fusion.17), channel_id=1, source_target_pairs={{0,16},{4,20},{8,24},{12,28},{16,0},{20,4},{24,8},{28,12},{1,17},{... | collective-permute-start | bytes 1032200 | tf_op jit(solution)/shard_map/ppermute | solution.py:730
  476.0 14.9 %collective-permute-start.24 = (bf16[2,96,768]{2,1,0:T(8,128)(2,1)S(1)}, bf16[2,96,768]{2,1,0:T(8,128)(2,1)S(1)}, u32[]{:S(2)}, u32[]{:S(2)}) collective-permute-start(bf16[2,96,768]{2,1,0:T(8,128)(2,1)S(1)} %fusion.21), channel_id=1, source_target_pairs={{0,16},{4,20},{8,24},{12,28},{16,0},{20,4},{24,8},{28,12},{1,17},{... | collective-permute-start | bytes 884744 | tf_op jit(solution)/shard_map/ppermute | solution.py:730
  478.9 17.5 %collective-permute-start.23 = (bf16[96,896]{1,0:T(8,128)(2,1)S(1)}, bf16[96,896]{1,0:T(8,128)(2,1)S(1)}, u32[]{:S(2)}, u32[]{:S(2)}) collective-permute-start(bf16[96,896]{1,0:T(8,128)(2,1)S(1)} %fusion.25), channel_id=1, source_target_pairs={{0,4},{4,0},{8,12},{12,8},{16,20},{20,16},{24,28},{28,24},{1,5},{5... | collective-permute-start | bytes 516104 | tf_op jit(solution)/shard_map/ppermute | solution.py:730

commit v3 on v2

--- a/solution.py
+++ b/solution.py
@@ -74,6 +74,28 @@
 
 def once(shape):
     return pl.BlockSpec(shape, lambda *_: (0,) * len(shape), pipeline_mode=pl.Buffered(1))
+
+
+ANY = pl.BlockSpec(memory_space=pl.ANY)
+
+
+class Fetch:
+    def __init__(self, pairs, sems):
+        self.step = pl.program_id(0)
+        self.copies = [
+            pltpu.make_async_copy(src, dst, sems.at[i]) for i, (src, dst) in enumerate(pairs)
+        ]
+
+        @pl.when(self.step == 0)
+        def _():
+            for copy in self.copies:
+                copy.start()
+
+    def need(self, *which):
+        @pl.when(self.step == 0)
+        def _():
+            for i in which:
+                self.copies[i].wait()
 
 
 def cost(flops, moved):
@@ -166,7 +188,7 @@
     return tok < limit
 
 
-def route_kernel(len_ref, h_ref, rw_ref, rcol_ref, rrow_ref, info_ref, pos_ref):
+def route_kernel(local, len_ref, h_ref, rw_ref, rcol_ref, rrow_ref, info_ref, pos_ref):
     t = h_ref.shape[1]
     items = t // SEQ
     lane = lax.broadcasted_iota(jnp.int32, (t, LANES), 1)
@@ -183,8 +205,11 @@
     count = dot_nn(tri, hot.astype(BF16))
     p0 = jnp.sum(jnp.where(is0, count, 0.0), -1, keepdims=True)
     p1 = jnp.sum(jnp.where(is1, count, 0.0), -1, keepdims=True)
-    slot0 = jnp.where(live & (p0 < CAP), r0.astype(F32) * CAP + p0, -1.0)
-    slot1 = jnp.where(live & (p1 < CAP), r1.astype(F32) * CAP + p1, -1.0)
+    groups = EXPERTS // local
+    block0 = (r0 % local) * groups + r0 // local
+    block1 = (r1 % local) * groups + r1 // local
+    slot0 = jnp.where(live & (p0 < CAP), block0.astype(F32) * CAP + p0, -1.0)
+    slot1 = jnp.where(live & (p1 < CAP), block1.astype(F32) * CAP + p1, -1.0)
     logits = dot_nn(h_ref[0], rw_ref[...])
     l0 = jnp.sum(jnp.where(is0, logits, 0.0), -1, keepdims=True)
     l1 = jnp.sum(jnp.where(is1, logits, 0.0), -1, keepdims=True)
@@ -205,10 +230,10 @@
     pos_ref[...] = jnp.where(hot_row, count_row, -1.0)
 
 
-def route(lengths, rows, rw_pad, routes, routes_t):
+def route(local, lengths, rows, rw_pad, routes, routes_t):
     t = rows.shape[1]
     return pl.pallas_call(
-        route_kernel,
+        functools.partial(route_kernel, local),
         name="route",
         grid=(1,),
         in_specs=[
@@ -276,26 +301,16 @@
     return act, slope
 
 
-def ffn_main_kernel(where_ref, x_ref, g_ref, w1_ref, w2_ref, *rest, paired, halved):
-    if paired:
-        out_ref, act_ref, gpre_ref = rest
-        x, g = x_ref[0, 0], x_ref[0, 1]
-    else:
-        y_ref, gx_ref, act_ref, *gpre_refs, gpre_ref = rest
-        x, g = x_ref[0], g_ref[0]
+def shared_main_kernel(halved, where_ref, x_ref, g_ref, w1_ref, w2_ref, *rest):
+    y_ref, gx_ref, act_ref, *gpre_refs, gpre_ref = rest
+    x, g = x_ref[0], g_ref[0]
     for f in range(4):
         cols = slice(f * (FF // 4), (f + 1) * (FF // 4))
-        act, slope = gelu_pair(dot_nn(x, w1_ref[0, :, cols]))
+        act, slope = gelu_pair(dot_nn(x, w1_ref[:, cols]))
         act_ref[:, cols] = act.astype(BF16)
-        gpre_ref[:, cols] = (dot_nt(g, w2_ref[0, cols, :]) * slope).astype(BF16)
-    y = dot_nn(act_ref[...], w2_ref[0])
-    gx = dot_nt(gpre_ref[...], w1_ref[0])
-    if paired:
-        out_ref[0, 0] = y.astype(BF16)
-        out_ref[0, 1] = gx.astype(BF16)
-    else:
-        y_ref[...] = y
-        gx_ref[...] = gx
+        gpre_ref[:, cols] = (dot_nt(g, w2_ref[cols, :]) * slope).astype(BF16)
+    y_ref[...] = dot_nn(act_ref[...], w2_ref[...])
+    gx_ref[...] = dot_nt(gpre_ref[...], w1_ref[...])
     if halved:
         first = where_ref[0] == 0
         width = FF // 4
@@ -307,116 +322,163 @@
             gpre_refs[1][:, cols] = jnp.where(first, high, low)
 
 
-def ffn_main(x, w1, w2, which, where=None):
-    paired = x.ndim == 4
-    halved = where is not None
-    rows = x.shape[0] * CAP if paired else x.shape[1]
-    chunk = lambda w: pl.BlockSpec((CAP, w), lambda s, *_: (s, 0))
-    scratch = []
-    if paired:
-        first = [pl.BlockSpec((1, 2, CAP, D), lambda s, *_: (s, 0, 0, 0)), once((8, D))]
-        args = (x, jnp.zeros((8, D), BF16))
-        outs, out_specs = [jax.ShapeDtypeStruct(x.shape, BF16)], first[:1]
-    else:
-        kind = lambda k: pl.BlockSpec((1, CAP, D), lambda s, *_: (k, s, 0))
-        first = [kind(H_MLP), kind(G_SHARED)]
-        args = (x, x)
-        outs, out_specs = [jax.ShapeDtypeStruct((rows, D), F32)] * 2, [chunk(D)] * 2
-    outs = outs + [jax.ShapeDtypeStruct((rows, FF), BF16)]
-    out_specs = out_specs + [chunk(FF)]
-    if halved:
-        outs = outs + [jax.ShapeDtypeStruct((rows, FF // 2), BF16)] * 2
-        out_specs = out_specs + [chunk(FF // 2)] * 2
-        scratch = [pltpu.VMEM((CAP, FF), BF16)]
-    else:
-        where = jnp.zeros((1,), jnp.int32)
-        outs = outs + [jax.ShapeDtypeStruct((rows, FF), BF16)]
-        out_specs = out_specs + [chunk(FF)]
-    weight = lambda r, c: pl.BlockSpec(
-        (1, r, c), lambda s, *_: (which, 0, 0), pipeline_mode=pl.Buffered(1)
-    )
+def shared_main(halved, where, rows, w1, w2):
+    t = rows.shape[1]
+    chunk = lambda w: pl.BlockSpec((SEQ, w), lambda s, m: (s, 0))
+    kind = lambda k: pl.BlockSpec((1, SEQ, D), lambda s, m: (k, s, 0))
+    widths = [FF // 2] * 2 if halved else [FF]
     return pl.pallas_call(
-        functools.partial(ffn_main_kernel, paired=paired, halved=halved),
-        name="ffn_main_pairs" if paired else "ffn_main_shared",
+        functools.partial(shared_main_kernel, halved),
+        name="shared_main",
         grid_spec=pltpu.PrefetchScalarGridSpec(
             num_scalar_prefetch=1,
-            grid=(rows // CAP,),
-            in_specs=first + [weight(D, FF), weight(FF, D)],
-            out_specs=out_specs,
-            scratch_shapes=scratch,
+            grid=(t // SEQ,),
+            in_specs=[kind(H_MLP), kind(G_SHARED), once((D, FF)), once((FF, D))],
+            out_specs=[chunk(D), chunk(D), chunk(FF)] + [chunk(w) for w in widths],
+            scratch_shapes=[pltpu.VMEM((SEQ, FF), BF16)] if halved else [],
         ),
-        out_shape=outs,
+        out_shape=[jax.ShapeDtypeStruct((t, D), F32)] * 2
+        + [jax.ShapeDtypeStruct((t, FF), BF16)]
+        + [jax.ShapeDtypeStruct((t, w), BF16) for w in widths],
         compiler_params=params(),
-        cost_estimate=cost(8 * rows * D * FF, int(30e6)),
-    )(where, *args, w1, w2)
-
-
-def weight_grad_kernel(mode, where_ref, a_ref, b_ref, *outs):
-    a = a_ref[...].reshape(-1, D)
-    part = dot_tn(a, b_ref[...]).astype(BF16)
-    if mode == "plain":
+        cost_estimate=cost(8 * t * D * FF, int(30e6)),
+    )(where, rows, rows, w1, w2)
+
+
+def store_out_grad(where_ref, part, keep_ref, send_ref):
+    first = where_ref[0] == 0
+    low, high = part[:, :384], part[:, 384:]
+    mine = jnp.where(first, low, high)
+    other = jnp.where(first, high, low)
+    for k in range(8):
+        cols = slice(k * 384, k * 384 + 384)
+        keep_ref[0, 0, :, cols] = mine[k * 96 : k * 96 + 96]
+        send_ref[0, 0, :, cols] = other[k * 96 : k * 96 + 96]
+
+
+def expert_first_kernel(fast, where_ref, rows_ref, w1_ref, act_ref, slope_ref, *outs):
+    x = rows_ref[:, 0].reshape(-1, D)
+    g = rows_ref[:, 1].reshape(-1, D)
+    act, slope = gelu_pair(dot_nn(x, w1_ref[0]))
+    act = act.astype(BF16)
+    act_ref[...] = act
+    slope_ref[...] = slope
+    part = dot_tn(g, act).astype(BF16)
+    if fast:
+        store_out_grad(where_ref, part, *outs)
+    else:
+        outs[0][...] = part
+
+
+def expert_first(fast, where, rows, w1, which):
+    count = rows.shape[0] * CAP
+    tile = FF // 4 if fast else FF // 8
+    tile_of = lambda s, m: ((s % 2) ^ m[2]) * 2 + ((s // 2) ^ m[1]) if fast else s
+    col = pl.BlockSpec((count, tile), lambda s, m: (0, tile_of(s, m)))
+    if fast:
+        grads = [jax.ShapeDtypeStruct((2, 2, 96, FF), BF16)] * 2
+        specs = [pl.BlockSpec((1, 1, 96, FF), lambda s, m: (s // 2, s % 2, 0, 0))] * 2
+    else:
+        grads = [jax.ShapeDtypeStruct((D, FF), BF16)]
+        specs = [pl.BlockSpec((D, tile), lambda s, m: (0, s))]
+    act, slope, *grads = pl.pallas_call(
+        functools.partial(expert_first_kernel, fast),
+        name="expert_first",
+        grid_spec=pltpu.PrefetchScalarGridSpec(
+            num_scalar_prefetch=1,
+            grid=(FF // tile,),
+            in_specs=[
+                once(rows.shape), pl.BlockSpec((1, D, tile), lambda s, m: (which, 0, tile_of(s, m))),
+            ],
+            out_specs=[col, col] + specs,
+        ),
+        out_shape=[
+            jax.ShapeDtypeStruct((count, FF), BF16), jax.ShapeDtypeStruct((count, FF), F32),
+        ] + grads,
+        compiler_params=params(),
+        cost_estimate=cost(4 * count * D * FF, int(30e6)),
+    )(where, rows, w1)
+    return act, slope, grads
+
+
+def expert_second_kernel(rows_ref, act_ref, slope_ref, w1_ref, w2_ref, out_ref, gpre_ref):
+    g = rows_ref[0, 1]
+    for f in range(4):
+        cols = slice(f * (FF // 4), (f + 1) * (FF // 4))
+        gpre_ref[:, cols] = (dot_nt(g, w2_ref[0, cols, :]) * slope_ref[:, cols]).astype(BF16)
+    out_ref[0, 0] = dot_nn(act_ref[...], w2_ref[0]).astype(BF16)
+    out_ref[0, 1] = dot_nt(gpre_ref[...], w1_ref[0]).astype(BF16)
+
+
+def expert_second(rows, act, slope, w1, w2, which):
+    count = rows.shape[0] * CAP
+    chunk = lambda w: pl.BlockSpec((CAP, w), lambda s: (s, 0))
+    pair = pl.BlockSpec((1, 2, CAP, D), lambda s: (s, 0, 0, 0))
+    weight = lambda r, c: pl.BlockSpec(
+        (1, r, c), lambda s: (which, 0, 0), pipeline_mode=pl.Buffered(1)
+    )
+    return pl.pallas_call(
+        expert_second_kernel,
+        name="expert_second",
+        grid=(rows.shape[0],),
+        in_specs=[pair, chunk(FF), chunk(FF), weight(D, FF), weight(FF, D)],
+        out_specs=[pair, chunk(FF)],
+        out_shape=[
+            jax.ShapeDtypeStruct(rows.shape, BF16), jax.ShapeDtypeStruct((count, FF), BF16),
+        ],
+        compiler_params=params(),
+        cost_estimate=cost(6 * count * D * FF, int(40e6)),
+    )(rows, act, slope, w1, w2)
+
+
+def weight_grad_kernel(fast, where_ref, a_ref, b_ref, *outs):
+    part = dot_tn(a_ref[...].reshape(-1, D), b_ref[...]).astype(BF16)
+    if not fast:
         outs[0][...] = part
         return
     first = where_ref[0] == 0
     keep_ref, send_ref = outs
-    if mode == "in":
-        for z in range(4):
-            low = part[192 * z : 192 * z + 96]
-            high = part[192 * z + 96 : 192 * z + 192]
-            at = (z % 2) ^ where_ref[1], (z // 2) ^ where_ref[2]
-            keep_ref[at] = jnp.where(first, low, high)
-            send_ref[at] = jnp.where(first, high, low)
-    else:
-        low, high = part[:, :384], part[:, 384:]
-        mine = jnp.where(first, low, high)
-        other = jnp.where(first, high, low)
-        for k in range(8):
-            cols = slice(k * 384, k * 384 + 384)
-            keep_ref[0, 0, :, cols] = mine[k * 96 : k * 96 + 96]
-            send_ref[0, 0, :, cols] = other[k * 96 : k * 96 + 96]
-
-
-def weight_grad(mode, mine, a, kind, b):
+    for z in range(4):
+        low = part[192 * z : 192 * z + 96]
+        high = part[192 * z + 96 : 192 * z + 192]
+        at = (z % 2) ^ where_ref[1], (z // 2) ^ where_ref[2]
+        keep_ref[at] = jnp.where(first, low, high)
+        send_ref[at] = jnp.where(first, high, low)
+
+
+def weight_grad(fast, where, a, kind, b):
     rows = b.shape[0]
     tile = FF // 4
-    tile_of = lambda s, m: s
-    if mode == "out":
-        tile_of = lambda s, m: ((s % 2) ^ m[2]) * 2 + ((s // 2) ^ m[1])
     if a.ndim == 3:
         a_spec = kind_of(kind, rows)
     else:
         a_spec = pl.BlockSpec(
             (a.shape[0], 1, CAP, D), lambda s, m: (0, kind, 0, 0), pipeline_mode=pl.Buffered(1)
         )
-    if mode == "plain":
+    if fast:
+        outs = [jax.ShapeDtypeStruct((2, 2, 96, FF), BF16)] * 2
+        specs = [pl.BlockSpec((2, 2, 96, tile), lambda s, m: (0, 0, 0, s))] * 2
+    else:
         outs = [jax.ShapeDtypeStruct((D, FF), BF16)]
         specs = [pl.BlockSpec((D, tile), lambda s, m: (0, s))]
-    else:
-        outs = [jax.ShapeDtypeStruct((2, 2, 96, FF), BF16)] * 2
-        if mode == "in":
-            specs = [pl.BlockSpec((2, 2, 96, tile), lambda s, m: (0, 0, 0, s))] * 2
-        else:
-            specs = [pl.BlockSpec((1, 1, 96, FF), lambda s, m: (s // 2, s % 2, 0, 0))] * 2
     return pl.pallas_call(
-        functools.partial(weight_grad_kernel, mode),
-        name="weight_grad_" + mode,
+        functools.partial(weight_grad_kernel, fast),
+        name="weight_grad",
         grid_spec=pltpu.PrefetchScalarGridSpec(
             num_scalar_prefetch=1,
             grid=(FF // tile,),
-            in_specs=[a_spec, pl.BlockSpec((rows, tile), lambda s, m: (0, tile_of(s, m)))],
+            in_specs=[a_spec, pl.BlockSpec((rows, tile), lambda s, m: (0, s))],
             out_specs=specs,
         ),
         out_shape=outs,
         compiler_params=params(),
         cost_estimate=cost(2 * rows * D * FF, int(13e6)),
-    )(mine, a, b)
-
-
-def batch_at(where_ref, b, y_last):
+    )(where, a, b)
+
+
+def batch_at(where_ref, b):
     z = b // 2
-    y = (b % 2) ^ where_ref[2]
-    near, far = (z % 2) ^ where_ref[3], (z // 2) ^ where_ref[4]
-    return (near, far, y) if y_last else (y, near, far)
+    return (b % 2) ^ where_ref[2], (z % 2) ^ where_ref[3], (z // 2) ^ where_ref[4]
 
 
 def own_columns(where_ref, v, width):
@@ -427,7 +489,7 @@
 
 def shared_grad_kernel(
     where_ref, mine_ref, peer_ref, gpre_ref, gpre_peer_ref, act_ref, act_peer_ref,
-    keep_ref, send_ref, g_scr,
+    keep_ref, send_ref, g_scr, part_scr,
 ):
     step = pl.program_id(0)
     side = step // 2
@@ -438,15 +500,17 @@
         g_scr[:rows] = own_columns(where_ref, mine_ref[G_SHARED], D // 4)
         g_scr[rows:] = own_columns(where_ref, peer_ref[G_SHARED], D // 4)
 
-    part = (
-        dot_tn(mine_ref[H_MLP], gpre_ref[...]) + dot_tn(peer_ref[H_MLP], gpre_peer_ref[...])
-    ).astype(BF16)
-    for half in range(2):
+    @pl.when(step % 2 == 0)
+    def _():
+        part = (
+            dot_tn(mine_ref[H_MLP], gpre_ref[...]) + dot_tn(peer_ref[H_MLP], gpre_peer_ref[...])
+        ).astype(BF16)
+        for b in range(8):
+            part_scr[batch_at(where_ref, b)] = part[b * 96 : b * 96 + 96]
         for s, ref in ((0, keep_ref), (1, send_ref)):
-            @pl.when((step % 2 == half) & (side == s))
+            @pl.when(side == s)
             def _():
-                for b in range(8):
-                    ref[(*batch_at(where_ref, b, False), 0, slice(None), slice(half * 384, half * 384 + 384))] = part[b * 96 : b * 96 + 96]
+                ref[:, :, :, 0] = part_scr[...]
 
     both = (dot_tn(g_scr[:rows], act_ref[...]) + dot_tn(g_scr[rows:], act_peer_ref[...])).astype(BF16)
     first = where_ref[1] == 0
@@ -454,7 +518,7 @@
     for ref, v in ((keep_ref, jnp.where(first, low, high)), (send_ref, jnp.where(first, high, low))):
         for h in range(2):
             for y in range(2):
-                at = batch_at(where_ref, 2 * step + y, False)
+                at = batch_at(where_ref, 2 * step + y)
                 ref[(*at, 1, slice(None), slice(h * 384, h * 384 + 384))] = v[
                     h * 96 : h * 96 + 96, y * 384 : y * 384 + 384
                 ]
@@ -462,7 +526,7 @@
 
 def shared_grad(where, mine, peer, gpre, gpre_peer, act, act_peer):
     rows = act.shape[0]
-    gpre_spec = pl.BlockSpec((rows, FF // 8), lambda s, m: (0, ((s // 2) ^ m[1]) * 2 + s % 2))
+    gpre_spec = pl.BlockSpec((rows, FF // 4), lambda s, m: (0, (s // 2) ^ m[1]))
     act_spec = pl.BlockSpec((rows, FF // 4), lambda s, m: (0, s))
     stack = pl.BlockSpec((2, rows, D), lambda s, m: (0, 0, 0), pipeline_mode=pl.Buffered(1))
     shape = (2, 2, 2, 2, 96, D)
@@ -474,7 +538,9 @@
             grid=(4,),
             in_specs=[stack, stack, gpre_spec, gpre_spec, act_spec, act_spec],
             out_specs=[once(shape)] * 2,
-            scratch_shapes=[pltpu.VMEM((2 * rows, D // 2), BF16)],
+            scratch_shapes=[
+                pltpu.VMEM((2 * rows, D // 2), BF16), pltpu.VMEM((2, 2, 2, 96, D), BF16),
+            ],
         ),
         out_shape=[jax.ShapeDtypeStruct(shape, BF16)] * 2,
         compiler_params=params(),
@@ -488,19 +554,20 @@
 ):
     back = rest[:local]
     if fast:
-        out_ref, gtok_ref, gmod_ref, own_ref, other_ref, gq_ref, yr_ref, gr_ref = rest[-8:]
+        out_ref, gtok_ref, gmod_ref, own_ref, other_ref, gq_ref = rest[-6:]
     else:
-        out_ref, gtok_ref, gmod_ref, own_ref, gq_ref, yr_ref, gr_ref = rest[-7:]
+        out_ref, gtok_ref, gmod_ref, own_ref, gq_ref = rest[-5:]
     item = pl.program_id(0) + first_item
-    slots = yr_ref.shape[0]
-
-    @pl.when(pl.program_id(0) == 0)
-    def _():
+    slots = EXPERTS * CAP
+    each = slots // local
+
+    def pick(hot, kind):
+        value = None
         for j in range(local):
-            for g in range(EXPERTS // local):
-                rows = slice((g * local + j) * CAP, (g * local + j + 1) * CAP)
-                yr_ref[rows] = back[j][g, 0]
-                gr_ref[rows] = back[j][g, 1]
+            rows = back[j][:, kind].reshape(each, D)
+            term = dot_nn(hot[:, j * each : (j + 1) * each], rows)
+            value = term if value is None else value + term
+        return value
 
     mod = mod_ref[0]
     x = tok_ref[...].astype(F32)
@@ -512,8 +579,8 @@
     slot = lax.broadcasted_iota(jnp.int32, (SEQ, slots), 1).astype(F32)
     hot0 = jnp.where(slot == info_ref[:, 2:3], 1.0, 0.0).astype(BF16)
     hot1 = jnp.where(slot == info_ref[:, 3:4], 1.0, 0.0).astype(BF16)
-    row0 = dot_nn(hot0, yr_ref[...])
-    row1 = dot_nn(hot1, yr_ref[...])
+    row0 = pick(hot0, 0)
+    row1 = pick(hot1, 0)
     mlp_out = sres_ref[...] + (gw0 * row0 + gw1 * row1)
     out_ref[...] = (x_mid + mod[5:6] * mlp_out).astype(BF16)
     gmod_ref[0, 5:6, :] = jnp.sum(cot * mlp_out, 0, keepdims=True)
@@ -534,7 +601,7 @@
         + jnp.where(lane_f == r0 + EXPERTS, sel0 - high0, 0.0)
         + jnp.where(lane_f == r1 + EXPERTS, sel1 - high1, 0.0)
     ).astype(BF16)
-    grad_h = gsh_ref[...] + dot_nn(hot0 + hot1, gr_ref[...]) + dot_nn(g_logits, rwt_ref[...])
+    grad_h = gsh_ref[...] + pick(hot0 + hot1, 1) + dot_nn(g_logits, rwt_ref[...])
     gmod_ref[0, 3:4, :] = jnp.sum(grad_h, 0, keepdims=True)
     gmod_ref[0, 4:5, :] = jnp.sum(grad_h * normed_mlp, 0, keepdims=True)
     grad_mid = cot + norm_back(grad_h * (1.0 + mod[4:5]), normed_mlp, factor_mlp)
@@ -623,8 +690,6 @@
             out_specs=[row(D), row(D), item_block(8)] + [new(w) for w in widths],
             scratch_shapes=[
                 pltpu.VMEM((SEQ, 3 * D), BF16),
-                pltpu.VMEM((EXPERTS * CAP, D), BF16),
-                pltpu.VMEM((EXPERTS * CAP, D), BF16),
             ],
         ),
         out_shape=[
@@ -643,22 +708,34 @@
 
 
 def tail_grad_kernel(fast, many, where_ref, *refs):
-    stacks, grads, outs = refs[:many], refs[many:-2 if fast else -3], refs[-2 if fast else -3:]
+    count = 2 if fast else 3
+    *refs, stack_ref, grad_ref, sems = refs
+    stacks, grads, outs = refs[:many], refs[many:-count], refs[-count:]
     width = 3 * D // 2 if fast else 3 * D
-    part = grads[0].shape[0]
     each = len(grads) // many
-
-    def total(kind, start, size):
-        value = None
-        for i, g in enumerate(grads):
-            at = (i % each) * part
-            term = dot_tn(stacks[i // each][kind, at : at + part], g[:, start : start + size])
-            value = term if value is None else value + term
-        return value
-
-    d_qkv = total(H_ATTN, 0, width).astype(BF16)
-    d_out = total(HEADS_OUT, width, width // 3).astype(BF16)
-    d_router = total(H_MLP, width + width // 3, LANES)
+    t = stacks[0].shape[1]
+    pairs = []
+    for i, stack in enumerate(stacks):
+        start = i * t
+        pairs.append((stack.at[G_SHARED + 1 :], stack_ref.at[i, : 4 - G_SHARED - 1]))
+        pairs.append((stack.at[H_MLP], stack_ref.at[i, 2]))
+        for g in grads[i * each : (i + 1) * each]:
+            pairs.append((g, grad_ref.at[pl.ds(start, g.shape[0])]))
+            start += g.shape[0]
+    fetch = Fetch(pairs, sems)
+    d_qkv = d_out = d_router = None
+    for i in range(many):
+        fetch.need(*range((2 + each) * i, (2 + each) * (i + 1)))
+        rows = slice(i * t, (i + 1) * t)
+        terms = (
+            dot_tn(stack_ref[i, 0], grad_ref[rows, :width]),
+            dot_tn(stack_ref[i, 1], grad_ref[rows, width : width + width // 3]),
+            dot_tn(stack_ref[i, 2], grad_ref[rows, width + width // 3 :]),
+        )
+        if i:
+            terms = (d_qkv + terms[0], d_out + terms[1], d_router + terms[2])
+        d_qkv, d_out, d_router = terms
+    d_qkv, d_out = d_qkv.astype(BF16), d_out.astype(BF16)
     d_router = (d_router + pltpu.roll(d_router, LANES - EXPERTS, 1)).astype(BF16)
     if not fast:
         outs[0][...], outs[1][...], outs[2][...] = d_qkv, d_out, d_router
@@ -672,7 +749,7 @@
     ]
     for ref, v in ((outs[0], jnp.where(first, low, high)), (outs[1], jnp.where(first, high, low))):
         for b in range(8):
-            ref[batch_at(where_ref, b, True)] = v[b * 96 : b * 96 + 96]
+            ref[batch_at(where_ref, b)] = v[b * 96 : b * 96 + 96]
 
 
 def tail_grad(fast, where, stacks, grads):
@@ -684,12 +761,22 @@
             jax.ShapeDtypeStruct((D, D), BF16),
             jax.ShapeDtypeStruct((D, LANES), BF16),
         ]
-    vmem = pl.BlockSpec(memory_space=pltpu.VMEM)
+    t, wide = stacks[0].shape[1], grads[0].shape[1]
+    many = len(stacks)
     return pl.pallas_call(
         functools.partial(tail_grad_kernel, fast, len(stacks)),
         name="tail_grad",
-        in_specs=[pl.BlockSpec(memory_space=pltpu.SMEM)] + [vmem] * (len(stacks) + len(grads)),
-        out_specs=[vmem] * len(outs),
+        grid_spec=pltpu.PrefetchScalarGridSpec(
+            num_scalar_prefetch=1,
+            grid=(1,),
+            in_specs=[ANY] * (len(stacks) + len(grads)),
+            out_specs=[once(o.shape) for o in outs],
+            scratch_shapes=[
+                pltpu.VMEM((many, 3, t, D), BF16),
+                pltpu.VMEM((many * t, wide), BF16),
+                pltpu.SemaphoreType.DMA((2 * many + len(grads),)),
+            ],
+        ),
         out_shape=outs,
         compiler_params=params(),
         cost_estimate=cost(int(5e9), int(20e6)),
@@ -825,75 +912,79 @@
     qkv, lse, attn, rows = attn_forward(lengths, tokens, cotangent, mod, qkv_weight, out_weight)
     if fast:
         peer_rows = swap(rows, "expert", 1)
-    info, pos = route(lengths, rows, rw_pad, routes, routes.T)
+    info, pos = route(local, lengths, rows, rw_pad, routes, routes.T)
     sent, received = [], []
     rows_now = rows
     for j in range(local):
         sent.append(dispatch(j, local, rows_now, cotangent, mod, info, pos))
         rows_now = after(rows, sent[j])
-    sres, gsh, s_act, *s_gpre = ffn_main(
-        rows_now, shared_in[None], shared_out[None], 0, where if fast else None
-    )
+    sres, gsh, s_act, *s_gpre = shared_main(fast, where, rows_now, shared_in, shared_out)
     if fast:
         peer_act = swap(s_act, "expert", 1)
         peer_gpre = swap(s_gpre[1], "expert", 1)
     for j in range(local):
         part = after(sent[j], sres) if j else sent[j]
         received.append(lax.all_to_all(part, "expert", 0, 0, tiled=True))
-    back, expert_grads = [], []
-    last = sres
+    expert_stages = [("batch", 1), ("batch", 2), ("batch", 4)]
+    dense_stages = [("expert", 2), ("batch", 1), ("batch", 2), ("batch", 4)]
+    back, expert_grads, chains = [], [], []
+    last = (sres,)
     for j in range(local):
-        rows_in = after(received[j], last)
-        y, act_e, gpre_e = ffn_main(rows_in, expert_in, expert_out, j)
+        rows_in = after(received[j], *last)
+        act_e, slope_e, d2 = expert_first(fast, y_at, rows_in, expert_in, j)
+        waits = [d2[0], *back]
+        if fast:
+            chains.append(Chain(*d2, expert_stages))
+            if j == 1:
+                chains[0].step(take_after=d2[:1])
+                waits.append(chains[0].send)
+        rows_in = after(rows_in, *waits)
+        y, gpre_e = expert_second(rows_in, act_e, slope_e, expert_in, expert_out, j)
         back.append(lax.all_to_all(y, "expert", 0, 0, tiled=True))
-        grad_rows = after(rows_in, back[j - 1]) if j else rows_in
-        d2 = weight_grad("out" if fast else "plain", y_at, grad_rows, 1, act_e)
-        d1 = weight_grad("in" if fast else "plain", y_at, after(rows_in, d2[0]), 0, gpre_e)
-        last = d1[0]
+        d1 = weight_grad(fast, y_at, after(rows_in, y), 0, gpre_e)
+        last = (d1[0],)
+        if fast:
+            chains.append(Chain(*d1, expert_stages))
         expert_grads.append((d1, d2))
-    rows_now = after(rows, last)
     if fast:
-        expert_stages = [("batch", 1), ("batch", 2), ("batch", 4)]
-        shared_stages = [("expert", 2), ("batch", 1), ("batch", 2), ("batch", 4)]
-        tail_stages = [("expert", 2), ("batch", 2), ("batch", 4), ("batch", 1)]
-        in0, out0 = [Chain(*g, expert_stages) for g in expert_grads[0]]
-        in1, out1 = [Chain(*g, expert_stages) for g in expert_grads[1]]
-        out0.step()
-        rows_now = after(rows_now, out0.send)
+        out0, in0, out1, in1 = chains
+        now = last
+        out0.step(take_after=now)
+        in0.step(take_after=now)
+        rows_now = after(rows, *last, out0.send, in0.send)
         shared_grads = shared_grad(where, rows_now, peer_rows, s_gpre[0], peer_gpre, s_act, peer_act)
-        shared_sum = Chain(*shared_grads, shared_stages)
+        shared_sum = Chain(*shared_grads, dense_stages)
     else:
+        rows_now = after(rows, *last)
         shared_grads = (
-            weight_grad("plain", y_at, rows_now, H_MLP, s_gpre[0])[0],
-            weight_grad("plain", y_at, rows_now, G_SHARED, s_act)[0],
+            weight_grad(fast, y_at, rows_now, H_MLP, s_gpre[0])[0],
+            weight_grad(fast, y_at, rows_now, G_SHARED, s_act)[0],
         )
-    pieces = items if fast else 2
-    per = items // pieces
+    pieces = [items // 2, items - items // 2]
     tok = after(tokens, shared_grads[0])
     outs, own, other = [], [], []
-    for piece in range(pieces):
+    done = 0
+    for piece, per in enumerate(pieces):
         outs, first, *second = backward(
-            fast, where, piece * per, per, outs, lengths, tok, cotangent, mod, attn, qkv, lse,
+            fast, where, done, per, outs, lengths, tok, cotangent, mod, attn, qkv, lse,
             sres, gsh, info, back, qkv_weight, out_weight, rwt_pad,
         )
+        done += per
         own.append(first)
         now = (outs[0],)
         tok = after(tokens, *now)
         if fast:
             other.append(swap(second[0], "expert", 1))
             if piece == 0:
+                out0.step(take_after=now)
                 in0.step(take_after=now)
-                out0.step(take_after=now)
-                tok = after(tok, in0.send, out0.send)
-            elif piece == 2:
+                out1.step(take_after=now)
+                tok = after(tok, out0.terms[-1], in0.send, out1.send)
+            else:
+                in1.step(take_after=now)
                 in0.step(take_after=now)
-                out0.step(take_after=now)
-                tok = after(tok, in0.send, out0.terms[-1])
-            elif piece == 3:
                 out1.step(take_after=now)
-                in0.step(take_after=now)
-                shared_sum.step(take_after=now)
-                where_now = after(where, out1.send, shared_sum.send, in0.terms[-1])
+                where_now = after(where, in0.terms[-1], out1.send, in1.send)
     result, grad_tokens, grad_mod = outs
     stacks = [rows, peer_rows] if fast else [rows]
     if not fast:
@@ -901,8 +992,9 @@
     tail = tail_grad(fast, where_now, stacks, own + other)
 
     cols, ada_rows = 6 * D // ne, D // nb
-    mod_parts = jnp.transpose(grad_mod[:, :6].reshape(items, ne, cols), (1, 0, 2))
-    act_parts = jnp.transpose(act.astype(F32).reshape(items, nb, ada_rows), (1, 0, 2))
+    mod_parts = grad_mod[:, :6].reshape(items, ne, cols).astype(BF16)
+    mod_parts = jnp.transpose(mod_parts, (1, 0, 2))
+    act_parts = jnp.transpose(act.reshape(items, nb, ada_rows), (1, 0, 2))
     act_parts = jnp.pad(act_parts, ((0, 0), (0, 0), (0, -ada_rows % LANES)))
     width = act_parts.shape[-1]
     parts = jnp.concatenate(
@@ -912,24 +1004,24 @@
         ],
         -1,
     )
-    got = all_pairs(parts)
+    got = all_pairs(after(parts, tail[0]))
 
     if fast:
         def unfold(v):
             return v.reshape(96, 8, 384).transpose(2, 1, 0).reshape(384, D)
 
-        tail_sum = Chain(*tail, tail_stages)
+        tail_sum = Chain(*tail, dense_stages)
         token = tail[0]
-        order = (
-            in1, out1, tail_sum, in1, out1, shared_sum, in1,
-            tail_sum, shared_sum, tail_sum, shared_sum, tail_sum,
-        )
-        for chain in order:
+        for chain in (
+            shared_sum, out1, in1, shared_sum, tail_sum, in1, shared_sum, tail_sum, shared_sum,
+            tail_sum, tail_sum,
+        ):
             chain.step(take_after=(token,))
-            token = chain.send if chain.stages else token
+            token = chain.send if chain.stages else chain.terms[-1]
+        tl = tail_sum.total()
         got = after(got, token)
         assert not any(c.stages for c in (in0, in1, out0, out1, shared_sum, tail_sum))
-        sh, tl = shared_sum.total(), tail_sum.total()
+        sh = shared_sum.total()
         g_sh1 = sh[0]
         g_sh2 = sh[1].reshape(96, 2, 384).transpose(2, 1, 0).reshape(384, 192)
         g_e1 = jnp.stack([in0.total(), in1.total()])
@@ -958,7 +1050,7 @@
         g_qkv = reduce_dense(tail[0])
         g_out = reduce_dense(tail[1])
         g_rt = reduce_dense(tail[2][:, :EXPERTS])
-    got = got.reshape(nb * ne * items, cols + width)
+    got = got.reshape(nb * ne * items, cols + width).astype(F32)
     grad_ada = jnp.dot(
         got[:, cols : cols + ada_rows].T, got[:, :cols], precision=lax.Precision.HIGHEST
     )

time: 508 us -> 447 us (0.88)
  waiting for transfers between devices: 106 us -> 61.7 us
  Pallas kernels: 277 us -> 265 us
    ppermute x27 -> x25, waiting for transfers between devices: 96.1 us -> 56.8 us  [swap(): lax.ppermute(value.astype(BF16), axis, [(i, i ^ bit) for i in range(size)])]
    pallas_call x4 -> x2, Pallas kernels: 74.6 us -> 59.9 us  [backward(): pl.pallas_call(functools.partial(backward_kernel, local, fast, first_item...]
    all_to_all x2, waiting for transfers between devices: 9.9 us -> 0.61 us  [per_device(): received.append(lax.all_to_all(part, 'expert', 0, 0, tiled=True))]
    pallas_call x8, Pallas kernels: 126 us -> 133 us  [the longest x2 45.6 us: expert_second(): pl.pallas_call(expert_second_kernel, name='expert_second', grid=(rows.sha...]
    ppermute x27 -> x25, starting transfers between devices: 27.6 us -> 26.5 us  [swap(): lax.ppermute(value.astype(BF16), axis, [(i, i ^ bit) for i in range(size)])]
  transfers between devices with their start and end apart: 32 -> 30, of which waited for: 10 -> 12; matrix products, arithmetic and copies ran while one was open for 10% -> 12% of each run, Pallas kernels for 49% -> 52%
where the time goes in v3:
time: 447 us; the launch traced here: 439 us
  Pallas kernels  265 us (59%)
  waiting for transfers between devices  61.7 us (14%)
  starting transfers between devices  47.7 us (11%)
  other arithmetic  43.1 us (10%)
  local copies, waits for them, and re-layouts  15.2 us (3%)
  matrix products  5.06 us (1%)
    pallas_call x2, Pallas kernels, backward(): pl.pallas_call(functools.partial(backward_kernel, local, fast, first_item...  59.9 us
    ppermute x25, waiting for transfers between devices, swap(): lax.ppermute(value.astype(BF16), axis, [(i, i ^ bit) for i in range(size)])  56.8 us
    pallas_call x2, Pallas kernels, expert_second(): pl.pallas_call(expert_second_kernel, name='expert_second', grid=(rows.sha...  45.6 us
    pallas_call x2, Pallas kernels, expert_first(): pl.pallas_call(functools.partial(expert_first_kernel, fast), name='expert...  33.8 us
    convert_element_type x14, other arithmetic, step(): self.send = self.total().astype(BF16)  29.8 us
    pallas_call x1, Pallas kernels, shared_main(): pl.pallas_call(functools.partial(shared_main_kernel, halved), name='share...  27.9 us
    ppermute x25, starting transfers between devices, swap(): lax.ppermute(value.astype(BF16), axis, [(i, i ^ bit) for i in range(size)])  26.5 us
    pallas_call x1, Pallas kernels, shared_grad(): pl.pallas_call(shared_grad_kernel, name='shared_grad', grid_spec=pltpu.Pr...  20.8 us
  transfers between devices with their start and end apart: 30, of which 12 were waited for; matrix products, arithmetic and copies ran while one was open for 12% of the time, Pallas kernels for 52%

profile of v3, /device:TPU:0, one launch (start us, length us, event | category | flops | bytes accessed | tf_op | source)
XLA Modules:
  0.0 439.2 jit_solution(12238452889473379843)
XLA Ops:
  0.7 4.0 fusion.31
  7.3 20.8 %attn_forward.1 = (bf16[1024,2304]{1,0:T(8,128)(2,1)}, f32[1024,128]{1,0:T(8,128)}, f32[1024,768]{1,0:T(8,128)}, bf16[4,1024,768]{2,1,0:T(8,128)(2,1)}) custom-call(s32[4]{0:T(128)} %len_ref.7, bf16[1024,768]{1,0:T(8,128)(2,1)} %tok_ref.3, bf16[1024,768]{1,0:T(8,128)(2,1)} %cot_ref.9, f32[4,6,768]{2,1,0:T(8,128)} %reshape.219.mod_ref, ...), custom_call_target="tpu_custom_call" | custom-call | flops 4049999872 | bytes 12000000 | tf_op jit(solution)/shard_map/attn_forward/pallas_call | solution.py:158
  28.1 5.8 %route.1 = (f32[1024,128]{1,0:T(8,128)}, f32[8,1024]{1,0:T(8,128)}) custom-call(s32[4]{0:T(128)} %len_ref.7, bf16[4,1024,768]{2,1,0:T(8,128)(2,1)} %get-tuple-element.117.h_ref.x_ref.g_ref.mine_ref.refs_0_, bf16[768,128]{1,0:T(8,128)(2,1)} %pad.12.rw_ref, s32[1024,2]{1,0:T(8,128)} %copy.35.rcol_ref, s32[2,1024]{1,0:T(2,128)} %bitcast.136), custom_call_target="tpu_custom_call" | custom-call | flops 500000000 | bytes 1500000 | tf_op jit(solution)/shard_map/route/pallas_call | solution.py:235
  33.9 7.8 %dispatch.2 = bf16[4,2,256,768]{3,2,1,0:T(8,128)(2,1)} custom-call(bf16[4,1024,768]{2,1,0:T(8,128)(2,1)} %get-tuple-element.117.h_ref.x_ref.g_ref.mine_ref.refs_0_, bf16[1024,768]{1,0:T(8,128)(2,1)} %cot_ref.9, f32[4,6,768]{2,1,0:T(8,128)} %reshape.219.mod_ref, f32[1024,128]{1,0:T(8,128)} %get-tuple-element.88.info_ref, f32[8,1024]{1,0:T(8,128)} %get-tuple-element.89.pos_ref), custom_call_target="tpu_custom_call" | custom-call | flops 1650000000 | bytes 4000000 | tf_op jit(solution)/shard_map/dispatch/pallas_call | solution.py:281
  41.7 4.4 %all-to-all-start.1 = ((bf16[4,2,256,768]{3,2,1,0:T(8,128)(2,1)}), bf16[4,2,256,768]{3,2,1,0:T(8,128)(2,1)S(1)}, u32[]{:S(2)}, u32[]{:S(2)}) async-start(bf16[4,2,256,768]{3,2,1,0:T(8,128)(2,1)} %dispatch.2), calls=%async_computation.1 | async-start | bytes 6291456 | tf_op jit(solution)/shard_map/all_to_all | solution.py:927
  46.2 7.8 %dispatch.3 = bf16[4,2,256,768]{3,2,1,0:T(8,128)(2,1)} custom-call(bf16[4,1024,768]{2,1,0:T(8,128)(2,1)} %get-tuple-element.117.h_ref.x_ref.g_ref.mine_ref.refs_0_, bf16[1024,768]{1,0:T(8,128)(2,1)} %cot_ref.9, f32[4,6,768]{2,1,0:T(8,128)} %reshape.219.mod_ref, f32[1024,128]{1,0:T(8,128)} %get-tuple-element.88.info_ref, f32[8,1024]{1,0:T(8,128)} %get-tuple-element.89.pos_ref), custom_call_target="tpu_custom_call" | custom-call | flops 1650000000 | bytes 4000000 | tf_op jit(solution)/shard_map/dispatch/pallas_call | solution.py:281
  54.6 27.9 %shared_main.1 = (f32[1024,768]{1,0:T(8,128)}, f32[1024,768]{1,0:T(8,128)}, bf16[1024,3072]{1,0:T(8,128)(2,1)}, bf16[1024,1536]{1,0:T(8,128)(2,1)}, bf16[1024,1536]{1,0:T(8,128)(2,1)}) custom-call(s32[5]{0:T(128)} %stack.41.where_ref, bf16[4,1024,768]{2,1,0:T(8,128)(2,1)} %get-tuple-element.117.h_ref.x_ref.g_ref.mine_ref.refs_0_, ...), custom_call_target="tpu_custom_call" | custom-call | flops 9663676416 | bytes 15000000 | tf_op jit(solution)/shard_map/shared_main/pallas_call | solution.py:330
  83.1 1.9 copy-done.2
  85.0 4.9 %all-to-all-start = ((bf16[4,2,256,768]{3,2,1,0:T(8,128)(2,1)}), bf16[4,2,256,768]{3,2,1,0:T(8,128)(2,1)}, u32[]{:S(2)}, u32[]{:S(2)}) async-start(bf16[4,2,256,768]{3,2,1,0:T(8,128)(2,1)} %dispatch.3), calls=%async_computation | async-start | bytes 6291456 | tf_op jit(solution)/shard_map/all_to_all | solution.py:927
  91.1 16.9 %expert_first.2 = (bf16[1024,3072]{1,0:T(8,128)(2,1)}, f32[1024,3072]{1,0:T(8,128)}, bf16[2,2,96,3072]{3,2,1,0:T(8,128)(2,1)}, bf16[2,2,96,3072]{3,2,1,0:T(8,128)(2,1)}) custom-call(s32[3]{0:T(128)} %pad_add_fusion.where_ref, bf16[4,2,256,768]{3,2,1,0:T(8,128)(2,1)} %copy-done.2, bf16[2,768,3072]{2,1,0:T(8,128)(2,1)} %w1_ref.9), custom_call_target="tpu_custom_call" | custom-call | flops 4831838208 | bytes 15000000 | tf_op jit(solution)/shard_map/expert_first/pallas_call | solution.py:384
  108.0 2.3 collective-permute-start
  110.4 22.3 %expert_second.2 = (bf16[4,2,256,768]{3,2,1,0:T(8,128)(2,1)}, bf16[1024,3072]{1,0:T(8,128)(2,1)}) custom-call(bf16[4,2,256,768]{3,2,1,0:T(8,128)(2,1)} %copy-done.2, bf16[1024,3072]{1,0:T(8,128)(2,1)} %get-tuple-element.97.act_ref, f32[1024,3072]{1,0:T(8,128)} %get-tuple-element.98.slope_ref, bf16[2,768,3072]{2,1,0:T(8,128)(2,1)} %w1_ref.9, ...), custom_call_target="tpu_custom_call" | custom-call | flops 7247757312 | bytes 20000000 | tf_op jit(solution)/shard_map/expert_second/pallas_call | solution.py:420
  132.6 4.0 all-to-all-start.2
  137.2 9.9 %weight_grad.2 = (bf16[2,2,96,3072]{3,2,1,0:T(8,128)(2,1)}, bf16[2,2,96,3072]{3,2,1,0:T(8,128)(2,1)}) custom-call(s32[3]{0:T(128)} %pad_add_fusion.where_ref, bf16[4,2,256,768]{3,2,1,0:T(8,128)(2,1)} %copy-done.2, bf16[1024,3072]{1,0:T(8,128)(2,1)} %get-tuple-element.101.b_ref), custom_call_target="tpu_custom_call" | custom-call | flops 2415919104 | bytes 6500000 | tf_op jit(solution)/shard_map/weight_grad/pallas_call | solution.py:464
  147.1 16.9 %expert_first.3 = (bf16[1024,3072]{1,0:T(8,128)(2,1)}, f32[1024,3072]{1,0:T(8,128)}, bf16[2,2,96,3072]{3,2,1,0:T(8,128)(2,1)}, bf16[2,2,96,3072]{3,2,1,0:T(8,128)(2,1)}) custom-call(s32[3]{0:T(128)} %pad_add_fusion.where_ref, bf16[4,2,256,768]{3,2,1,0:T(8,128)(2,1)} %all-to-all-done.rows_ref.a_ref, bf16[2,768,3072]{2,1,0:T(8,128)(2,1)} %w1_ref.9), custom_call_target="tpu_custom_call" | custom-call | flops 4831838208 | bytes 15000000 | tf_op jit(solution)/shard_map/expert_first/pallas_call | solution.py:384
  164.0 3.0 fusion
  167.0 2.2 collective-permute-start.1
  169.2 4.3 all-to-all-done.2.rest_0_
  173.5 23.4 %expert_second.3 = (bf16[4,2,256,768]{3,2,1,0:T(8,128)(2,1)}, bf16[1024,3072]{1,0:T(8,128)(2,1)}) custom-call(bf16[4,2,256,768]{3,2,1,0:T(8,128)(2,1)} %all-to-all-done.rows_ref.a_ref, bf16[1024,3072]{1,0:T(8,128)(2,1)} %get-tuple-element.108.act_ref, f32[1024,3072]{1,0:T(8,128)} %get-tuple-element.109.slope_ref, bf16[2,768,3072]{2,1,0:T(8,128)(2,1)} %w1_ref.9, ...), custom_call_target="tpu_custom_call" | custom-call | flops 7247757312 | bytes 20000000 | tf_op jit(solution)/shard_map/expert_second/pallas_call | solution.py:420
  196.9 4.2 all-to-all-start.3
  202.0 9.9 %weight_grad.3 = (bf16[2,2,96,3072]{3,2,1,0:T(8,128)(2,1)}, bf16[2,2,96,3072]{3,2,1,0:T(8,128)(2,1)}) custom-call(s32[3]{0:T(128)} %pad_add_fusion.where_ref, bf16[4,2,256,768]{3,2,1,0:T(8,128)(2,1)} %all-to-all-done.rows_ref.a_ref, bf16[1024,3072]{1,0:T(8,128)(2,1)} %get-tuple-element.112.b_ref), custom_call_target="tpu_custom_call" | custom-call | flops 2415919104 | bytes 6500000 | tf_op jit(solution)/shard_map/weight_grad/pallas_call | solution.py:464
  211.9 1.2 collective-permute-done.2
  213.1 1.8 collective-permute-start.8
  214.8 3.1 fusion.1
  217.9 1.6 collective-permute-start.7
  219.6 2.5 fusion.15
  222.6 2.5 collective-permute-start.6
  225.1 20.8 %shared_grad.1 = (bf16[2,2,2,2,96,768]{5,4,3,2,1,0:T(8,128)(2,1)}, bf16[2,2,2,2,96,768]{5,4,3,2,1,0:T(8,128)(2,1)}) custom-call(s32[5]{0:T(128)} %stack.41.where_ref, bf16[4,1024,768]{2,1,0:T(8,128)(2,1)} %get-tuple-element.117.h_ref.x_ref.g_ref.mine_ref.refs_0_, bf16[4,1024,768]{2,1,0:T(8,128)(2,1)} %collective-permute-done.3.peer_ref.refs_1_, ...), custom_call_target="tpu_custom_call" | custom-call | flops 4831838208 | bytes 12500000 | tf_op jit(solution)/shard_map/shared_grad/pallas_call | solution.py:533
  245.9 1.7 collective-permute-start.15
  247.6 1.7 copy-done.1
  249.2 29.8 %backward.2 = (bf16[1024,768]{1,0:T(8,128)(2,1)}, f32[1024,768]{1,0:T(8,128)}, f32[4,8,768]{2,1,0:T(8,128)}, bf16[512,1664]{1,0:T(8,128)(2,1)}, bf16[512,1664]{1,0:T(8,128)(2,1)}) custom-call(s32[4]{0:T(128)} %len_ref.7, s32[5]{0:T(128)} %stack.41.where_ref, bf16[1024,768]{1,0:T(8,128)(2,1)} %tok_ref.3, bf16[1024,768]{1,0:T(8,128)(2,1)} %cot_ref.9, ...), custom_call_target="tpu_custom_call" | custom-call | flops 5000000000 | bytes 7000000 | tf_op jit(solution)/shard_map/backward/pallas_call | solution.py:678
  279.1 2.0 fusion.2
  281.6 2.5 fusion.14
  284.2 30.1 %backward.3 = (bf16[1024,768]{1,0:T(8,128)(2,1)}, f32[1024,768]{1,0:T(8,128)}, f32[4,8,768]{2,1,0:T(8,128)}, bf16[512,1664]{1,0:T(8,128)(2,1)}, bf16[512,1664]{1,0:T(8,128)(2,1)}) custom-call(s32[4]{0:T(128)} %len_ref.7, s32[5]{0:T(128)} %stack.41.where_ref, ...), custom_call_target="tpu_custom_call", output_to_operand_aliasing={{0}: (16, {}), {1}: (17, {}), {2}: (18, {})} | custom-call | flops 5000000000 | bytes 7000000 | tf_op jit(solution)/shard_map/backward/pallas_call | solution.py:678
  314.3 2.6 collective-permute-done.11
  318.4 2.0 fusion.6
  320.8 2.7 fusion.3
  323.5 2.4 fusion.13
  325.9 2.6 collective-permute-start.18
  329.6 1.6 collective-permute-start.17
  331.3 14.9 %tail_grad.1 = (bf16[2,2,2,96,896]{4,3,2,1,0:T(8,128)(2,1)}, bf16[2,2,2,96,896]{4,3,2,1,0:T(8,128)(2,1)}) custom-call(s32[5]{0:T(128)} %stack.41.where_ref, bf16[4,1024,768]{2,1,0:T(8,128)(2,1)} %get-tuple-element.117.h_ref.x_ref.g_ref.mine_ref.refs_0_, bf16[4,1024,768]{2,1,0:T(8,128)(2,1)} %collective-permute-done.3.peer_ref.refs_1_, ...), custom_call_target="tpu_custom_call" | custom-call | flops 2500000000 | bytes 10000000 | tf_op jit(solution)/shard_map/tail_grad/pallas_call | solution.py:766
  346.2 2.9 fusion.4
  349.1 1.5 collective-permute-start.16
  350.6 1.3 collective-permute-start.14
  352.0 3.6 all-to-all-start.4
  355.6 1.9 fusion.5
  357.6 15.5 %collective-permute-done.17 = bf16[2,96,3072]{2,1,0:T(8,128)(2,1)} collective-permute-done((bf16[2,96,3072]{2,1,0:T(8,128)(2,1)}, bf16[2,96,3072]{2,1,0:T(8,128)(2,1)}, u32[]{:S(2)}, u32[]{:S(2)}) %collective-permute-start.17) | collective-permute-done | bytes 1179680 | tf_op jit(solution)/shard_map/ppermute | solution.py:817
  373.1 2.3 fusion.12
  376.6 1.9 copy.42
  379.6 1.6 fusion.11
  381.2 1.5 collective-permute-start.20
  382.8 2.5 collective-permute-done.14
  385.3 1.3 fusion.16
  387.1 14.4 %collective-permute-done.21 = bf16[96,3072]{1,0:T(8,128)(2,1)} collective-permute-done((bf16[96,3072]{1,0:T(8,128)(2,1)}, bf16[96,3072]{1,0:T(8,128)(2,1)}, u32[]{:S(2)}, u32[]{:S(2)}) %collective-permute-start.21) | collective-permute-done | bytes 589856 | tf_op jit(solution)/shard_map/ppermute | solution.py:817
  401.5 3.0 fusion.8
  404.5 2.4 collective-permute-done.20
  406.9 1.3 fusion.19
  408.3 1.1 fusion.17
  409.4 1.2 collective-permute-start.22
  410.6 1.6 pad_maximum_fusion
  412.1 8.8 %collective-permute-done.23 = bf16[2,96,768]{2,1,0:T(8,128)(2,1)S(1)} collective-permute-done((bf16[2,96,768]{2,1,0:T(8,128)(2,1)S(1)}, bf16[2,96,768]{2,1,0:T(8,128)(2,1)S(1)}, u32[]{:S(2)}, u32[]{:S(2)}) %collective-permute-start.23) | collective-permute-done | bytes 294944 | tf_op jit(solution)/shard_map/ppermute | solution.py:817
  420.9 1.3 fusion.18
  422.3 1.1 collective-permute-done.22
  426.2 7.2 %collective-permute-done.24 = bf16[96,896]{1,0:T(8,128)(2,1)S(1)} collective-permute-done((bf16[96,896]{1,0:T(8,128)(2,1)S(1)}, bf16[96,896]{1,0:T(8,128)(2,1)S(1)}, u32[]{:S(2)}, u32[]{:S(2)}) %collective-permute-start.24) | collective-permute-done | bytes 172064 | tf_op jit(solution)/shard_map/ppermute | solution.py:817
  (79 shorter events, 21.5 us)
Async XLA Ops:
  0.6 4.8 %copy-start.6 = (s32[1024,2]{0,1:T(2,128)S(1)}, s32[1024,2]{0,1:T(2,128)}, u32[]{:S(2)}) copy-start(s32[1024,2]{0,1:T(2,128)} %param.16) | copy-start | bytes 24580
  0.7 5.8 %copy-start.5 = (bf16[768,8]{0,1:T(8,128)(2,1)S(1)}, bf16[768,8]{0,1:T(8,128)(2,1)}, u32[]{:S(2)}) copy-start(bf16[768,8]{0,1:T(8,128)(2,1)} %param.21) | copy-start | bytes 36868
  41.7 41.4 %all-to-all-start.1 = ((bf16[4,2,256,768]{3,2,1,0:T(8,128)(2,1)}), bf16[4,2,256,768]{3,2,1,0:T(8,128)(2,1)S(1)}, u32[]{:S(2)}, u32[]{:S(2)}) async-start(bf16[4,2,256,768]{3,2,1,0:T(8,128)(2,1)} %dispatch.2), calls=%async_computation.1 | async-start | bytes 6291456 | tf_op jit(solution)/shard_map/all_to_all | solution.py:927
  83.1 1.9 copy-start.2
  85.0 47.7 %all-to-all-start = ((bf16[4,2,256,768]{3,2,1,0:T(8,128)(2,1)}), bf16[4,2,256,768]{3,2,1,0:T(8,128)(2,1)}, u32[]{:S(2)}, u32[]{:S(2)}) async-start(bf16[4,2,256,768]{3,2,1,0:T(8,128)(2,1)} %dispatch.3), calls=%async_computation | async-start | bytes 6291456 | tf_op jit(solution)/shard_map/all_to_all | solution.py:927
  89.9 135.2 %collective-permute-start.3 = (bf16[4,1024,768]{2,1,0:T(8,128)(2,1)}, bf16[4,1024,768]{2,1,0:T(8,128)(2,1)}, u32[]{:S(2)}, u32[]{:S(2)}) collective-permute-start(bf16[4,1024,768]{2,1,0:T(8,128)(2,1)} %get-tuple-element.117.h_ref.x_ref.g_ref.mine_ref.refs_0_), channel_id=1, source_target_pairs={{0,1},{1,0},{2,3},{3,2},{4,5},{5,4},{6,7},{7,6},{8,9},{9,8},{10,11... | collective-permute-start | bytes 18874376 | tf_op jit(solution)/shard_map/ppermute | solution.py:817
  90.5 132.1 %collective-permute-start.5 = (bf16[1024,3072]{1,0:T(8,128)(2,1)}, bf16[1024,3072]{1,0:T(8,128)(2,1)}, u32[]{:S(2)}, u32[]{:S(2)}) collective-permute-start(bf16[1024,3072]{1,0:T(8,128)(2,1)} %get-tuple-element.120.act_ref), channel_id=1, source_target_pairs={{0,1},{1,0},{2,3},{3,2},{4,5},{5,4},{6,7},{7,6},{8,9},{9,8},{10,11... | collective-permute-start | bytes 18874376 | tf_op jit(solution)/shard_map/ppermute | solution.py:817
  108.0 56.0 %collective-permute-start = (bf16[2,2,96,3072]{3,2,1,0:T(8,128)(2,1)}, bf16[2,2,96,3072]{3,2,1,0:T(8,128)(2,1)}, u32[]{:S(2)}, u32[]{:S(2)}) collective-permute-start(bf16[2,2,96,3072]{3,2,1,0:T(8,128)(2,1)} %get-tuple-element.105), channel_id=1, source_target_pairs={{0,4},{4,0},{8,12},{12,8},{16,20},{20,16},{24,28},{28,24},{1,5},{5... | collective-permute-start | bytes 7077896 | tf_op jit(solution)/shard_map/ppermute | solution.py:817
  132.6 40.9 %all-to-all-start.2 = ((bf16[4,2,256,768]{3,2,1,0:T(8,128)(2,1)}), bf16[4,2,256,768]{3,2,1,0:T(8,128)(2,1)S(1)}, u32[]{:S(2)}, u32[]{:S(2)}) async-start(bf16[4,2,256,768]{3,2,1,0:T(8,128)(2,1)} %get-tuple-element.99), calls=%async_computation.2 | async-start | bytes 6291456 | tf_op jit(solution)/shard_map/all_to_all | solution.py:943
  136.6 85.4 %collective-permute-start.4 = (bf16[1024,1536]{1,0:T(8,128)(2,1)}, bf16[1024,1536]{1,0:T(8,128)(2,1)}, u32[]{:S(2)}, u32[]{:S(2)}) collective-permute-start(bf16[1024,1536]{1,0:T(8,128)(2,1)} %get-tuple-element.119), channel_id=1, source_target_pairs={{0,1},{1,0},{2,3},{3,2},{4,5},{5,4},{6,7},{7,6},{8,9},{9,8},{10,11... | collective-permute-start | bytes 9437192 | tf_op jit(solution)/shard_map/ppermute | solution.py:817
  147.1 66.0 %collective-permute-start.2 = (bf16[2,2,96,3072]{3,2,1,0:T(8,128)(2,1)}, bf16[2,2,96,3072]{3,2,1,0:T(8,128)(2,1)}, u32[]{:S(2)}, u32[]{:S(2)}) collective-permute-start(bf16[2,2,96,3072]{3,2,1,0:T(8,128)(2,1)} %get-tuple-element.115), channel_id=1, source_target_pairs={{0,4},{4,0},{8,12},{12,8},{16,20},{20,16},{24,28},{28,24},{1,5},{5... | collective-permute-start | bytes 7077896 | tf_op jit(solution)/shard_map/ppermute | solution.py:817
  167.0 50.9 %collective-permute-start.1 = (bf16[2,96,3072]{2,1,0:T(8,128)(2,1)}, bf16[2,96,3072]{2,1,0:T(8,128)(2,1)}, u32[]{:S(2)}, u32[]{:S(2)}) collective-permute-start(bf16[2,96,3072]{2,1,0:T(8,128)(2,1)} %fusion), channel_id=1, source_target_pairs={{0,8},{4,12},{8,0},{12,4},{16,24},{20,28},{24,16},{28,20},{1,9},{5... | collective-permute-start | bytes 3538952 | tf_op jit(solution)/shard_map/ppermute | solution.py:817
  173.5 23.4 %copy-start = (bf16[4,2,256,768]{3,2,1,0:T(8,128)(2,1)}, bf16[4,2,256,768]{3,2,1,0:T(8,128)(2,1)S(1)}, u32[]{:S(2)}) copy-start(bf16[4,2,256,768]{3,2,1,0:T(8,128)(2,1)S(1)} %all-to-all-done.2.rest_0_) | copy-start | bytes 9437188
  196.9 4.3 copy-start.7
  196.9 50.7 %all-to-all-start.3 = ((bf16[4,2,256,768]{3,2,1,0:T(8,128)(2,1)}), bf16[4,2,256,768]{3,2,1,0:T(8,128)(2,1)S(1)}, u32[]{:S(2)}, u32[]{:S(2)}) async-start(bf16[4,2,256,768]{3,2,1,0:T(8,128)(2,1)} %get-tuple-element.110), calls=%async_computation.3 | async-start | bytes 6291456 | tf_op jit(solution)/shard_map/all_to_all | solution.py:943
  213.1 66.0 %collective-permute-start.8 = (bf16[2,2,96,3072]{3,2,1,0:T(8,128)(2,1)}, bf16[2,2,96,3072]{3,2,1,0:T(8,128)(2,1)}, u32[]{:S(2)}, u32[]{:S(2)}) collective-permute-start(bf16[2,2,96,3072]{3,2,1,0:T(8,128)(2,1)} %get-tuple-element.131), channel_id=1, source_target_pairs={{0,4},{4,0},{8,12},{12,8},{16,20},{20,16},{24,28},{28,24},{1,5},{5... | collective-permute-start | bytes 7077896 | tf_op jit(solution)/shard_map/ppermute | solution.py:817
  217.9 61.1 %collective-permute-start.7 = (bf16[2,96,3072]{2,1,0:T(8,128)(2,1)}, bf16[2,96,3072]{2,1,0:T(8,128)(2,1)}, u32[]{:S(2)}, u32[]{:S(2)}) collective-permute-start(bf16[2,96,3072]{2,1,0:T(8,128)(2,1)} %fusion.1), channel_id=1, source_target_pairs={{0,8},{4,12},{8,0},{12,4},{16,24},{20,28},{24,16},{28,20},{1,9},{5... | collective-permute-start | bytes 3538952 | tf_op jit(solution)/shard_map/ppermute | solution.py:817
  222.1 94.9 %collective-permute-start.11 = (bf16[2,2,96,3072]{3,2,1,0:T(8,128)(2,1)}, bf16[2,2,96,3072]{3,2,1,0:T(8,128)(2,1)}, u32[]{:S(2)}, u32[]{:S(2)}) collective-permute-start(bf16[2,2,96,3072]{3,2,1,0:T(8,128)(2,1)} %get-tuple-element.141), channel_id=1, source_target_pairs={{0,4},{4,0},{8,12},{12,8},{16,20},{20,16},{24,28},{28,24},{1,5},{5... | collective-permute-start | bytes 7077896 | tf_op jit(solution)/shard_map/ppermute | solution.py:817
  222.6 56.5 %collective-permute-start.6 = (bf16[96,3072]{1,0:T(8,128)(2,1)}, bf16[96,3072]{1,0:T(8,128)(2,1)}, u32[]{:S(2)}, u32[]{:S(2)}) collective-permute-start(bf16[96,3072]{1,0:T(8,128)(2,1)} %fusion.15), channel_id=1, source_target_pairs={{0,16},{4,20},{8,24},{12,28},{16,0},{20,4},{24,8},{28,12},{1,17},{... | collective-permute-start | bytes 1769480 | tf_op jit(solution)/shard_map/ppermute | solution.py:817
  245.9 100.3 %collective-permute-start.15 = (bf16[2,2,2,2,96,768]{5,4,3,2,1,0:T(8,128)(2,1)}, bf16[2,2,2,2,96,768]{5,4,3,2,1,0:T(8,128)(2,1)}, u32[]{:S(2)}, u32[]{:S(2)}) collective-permute-start(bf16[2,2,2,2,96,768]{5,4,3,2,1,0:T(8,128)(2,1)} %get-tuple-element.151), channel_id=1, source_target_pairs={{0,2},{1,3},{2,0},{3,1},{4,6},{5,7},{6,4},{7,5},{8,10},{9,11},{10,... | collective-permute-start | bytes 7077896 | tf_op jit(solution)/shard_map/ppermute | solution.py:817
  247.6 1.7 copy-start.1
  281.1 42.4 %collective-permute-start.10 = (bf16[2,96,3072]{2,1,0:T(8,128)(2,1)S(1)}, bf16[2,96,3072]{2,1,0:T(8,128)(2,1)}, u32[]{:S(2)}, u32[]{:S(2)}) collective-permute-start(bf16[2,96,3072]{2,1,0:T(8,128)(2,1)S(1)} %fusion.2), channel_id=1, source_target_pairs={{0,8},{4,12},{8,0},{12,4},{16,24},{20,28},{24,16},{28,20},{1,9},{5... | collective-permute-start | bytes 3538952 | tf_op jit(solution)/shard_map/ppermute | solution.py:817
  284.1 45.5 %collective-permute-start.9 = (bf16[96,3072]{1,0:T(8,128)(2,1)}, bf16[96,3072]{1,0:T(8,128)(2,1)}, u32[]{:S(2)}, u32[]{:S(2)}) collective-permute-start(bf16[96,3072]{1,0:T(8,128)(2,1)} %fusion.14), channel_id=1, source_target_pairs={{0,16},{4,20},{8,24},{12,28},{16,0},{20,4},{24,8},{28,12},{1,17},{... | collective-permute-start | bytes 1769480 | tf_op jit(solution)/shard_map/ppermute | solution.py:817
  316.9 14.3 %collective-permute-start.13 = (bf16[512,1664]{1,0:T(8,128)(2,1)}, bf16[512,1664]{1,0:T(8,128)(2,1)}, u32[]{:S(2)}, u32[]{:S(2)}) collective-permute-start(bf16[512,1664]{1,0:T(8,128)(2,1)} %get-tuple-element.147), channel_id=1, source_target_pairs={{0,1},{1,0},{2,3},{3,2},{4,5},{5,4},{6,7},{7,6},{8,9},{9,8},{10,11... | collective-permute-start | bytes 5111816 | tf_op jit(solution)/shard_map/ppermute | solution.py:817
  317.0 14.3 %collective-permute-start.12 = (bf16[512,1664]{1,0:T(8,128)(2,1)}, bf16[512,1664]{1,0:T(8,128)(2,1)}, u32[]{:S(2)}, u32[]{:S(2)}) collective-permute-start(bf16[512,1664]{1,0:T(8,128)(2,1)} %get-tuple-element.146), channel_id=1, source_target_pairs={{0,1},{1,0},{2,3},{3,2},{4,5},{5,4},{6,7},{7,6},{8,9},{9,8},{10,11... | collective-permute-start | bytes 5111816 | tf_op jit(solution)/shard_map/ppermute | solution.py:817
  318.4 2.4 copy-start.3
  325.9 29.6 %collective-permute-start.18 = (bf16[96,3072]{1,0:T(8,128)(2,1)}, bf16[96,3072]{1,0:T(8,128)(2,1)}, u32[]{:S(2)}, u32[]{:S(2)}) collective-permute-start(bf16[96,3072]{1,0:T(8,128)(2,1)} %fusion.13), channel_id=1, source_target_pairs={{0,16},{4,20},{8,24},{12,28},{16,0},{20,4},{24,8},{28,12},{1,17},{... | collective-permute-start | bytes 1769480 | tf_op jit(solution)/shard_map/ppermute | solution.py:817
  329.6 43.5 %collective-permute-start.17 = (bf16[2,96,3072]{2,1,0:T(8,128)(2,1)}, bf16[2,96,3072]{2,1,0:T(8,128)(2,1)}, u32[]{:S(2)}, u32[]{:S(2)}) collective-permute-start(bf16[2,96,3072]{2,1,0:T(8,128)(2,1)} %fusion.3), channel_id=1, source_target_pairs={{0,8},{4,12},{8,0},{12,4},{16,24},{20,28},{24,16},{28,20},{1,9},{5... | collective-permute-start | bytes 3538952 | tf_op jit(solution)/shard_map/ppermute | solution.py:817
  349.1 30.5 %collective-permute-start.16 = (bf16[2,2,2,96,768]{4,3,2,1,0:T(8,128)(2,1)}, bf16[2,2,2,96,768]{4,3,2,1,0:T(8,128)(2,1)}, u32[]{:S(2)}, u32[]{:S(2)}) collective-permute-start(bf16[2,2,2,96,768]{4,3,2,1,0:T(8,128)(2,1)} %fusion.4), channel_id=1, source_target_pairs={{0,4},{4,0},{8,12},{12,8},{16,20},{20,16},{24,28},{28,24},{1,5},{5... | collective-permute-start | bytes 3538952 | tf_op jit(solution)/shard_map/ppermute | solution.py:817
  350.6 34.6 %collective-permute-start.14 = (bf16[2,2,2,96,896]{4,3,2,1,0:T(8,128)(2,1)}, bf16[2,2,2,96,896]{4,3,2,1,0:T(8,128)(2,1)}, u32[]{:S(2)}, u32[]{:S(2)}) collective-permute-start(bf16[2,2,2,96,896]{4,3,2,1,0:T(8,128)(2,1)} %get-tuple-element.150), channel_id=1, source_target_pairs={{0,2},{1,3},{2,0},{3,1},{4,6},{5,7},{6,4},{7,5},{8,10},{9,11},{10,... | collective-permute-start | bytes 4128776 | tf_op jit(solution)/shard_map/ppermute | solution.py:817
  352.0 84.7 %all-to-all-start.4 = ((bf16[32,4,1280]{2,1,0:T(4,128)(2,1)}), bf16[32,4,1280]{2,1,0:T(4,128)(2,1)}, u32[]{:S(2)}, u32[]{:S(2)}) async-start(bf16[32,4,1280]{2,1,0:T(4,128)(2,1)} %bitcast.131), calls=%async_computation.4 | async-start | bytes 655360 | tf_op jit(solution)/shard_map/all_to_all | solution.py:887
  375.4 26.0 %collective-permute-start.21 = (bf16[96,3072]{1,0:T(8,128)(2,1)}, bf16[96,3072]{1,0:T(8,128)(2,1)}, u32[]{:S(2)}, u32[]{:S(2)}) collective-permute-start(bf16[96,3072]{1,0:T(8,128)(2,1)} %fusion.12), channel_id=1, source_target_pairs={{0,16},{4,20},{8,24},{12,28},{16,0},{20,4},{24,8},{28,12},{1,17},{... | collective-permute-start | bytes 1769480 | tf_op jit(solution)/shard_map/ppermute | solution.py:817
  378.5 6.8 %copy-start.4 = (bf16[2,2,2,96,896]{4,3,2,1,0:T(8,128)(2,1)S(1)}, bf16[2,2,2,96,896]{4,3,2,1,0:T(8,128)(2,1)}, u32[]{:S(2)}) copy-start(bf16[2,2,2,96,896]{4,3,2,1,0:T(8,128)(2,1)} %get-tuple-element.148) | copy-start | bytes 4128772
  381.2 25.7 %collective-permute-start.20 = (bf16[2,2,96,768]{3,2,1,0:T(8,128)(2,1)S(1)}, bf16[2,2,96,768]{3,2,1,0:T(8,128)(2,1)S(1)}, u32[]{:S(2)}, u32[]{:S(2)}) collective-permute-start(bf16[2,2,96,768]{3,2,1,0:T(8,128)(2,1)S(1)} %fusion.11), channel_id=1, source_target_pairs={{0,8},{4,12},{8,0},{12,4},{16,24},{20,28},{24,16},{28,20},{1,9},{5... | collective-permute-start | bytes 1769480 | tf_op jit(solution)/shard_map/ppermute | solution.py:817
  386.5 21.7 %collective-permute-start.19 = (bf16[2,2,96,896]{3,2,1,0:T(8,128)(2,1)S(1)}, bf16[2,2,96,896]{3,2,1,0:T(8,128)(2,1)S(1)}, u32[]{:S(2)}, u32[]{:S(2)}) collective-permute-start(bf16[2,2,96,896]{3,2,1,0:T(8,128)(2,1)S(1)} %fusion.16), channel_id=1, source_target_pairs={{0,4},{4,0},{8,12},{12,8},{16,20},{20,16},{24,28},{28,24},{1,5},{5... | collective-permute-start | bytes 2064392 | tf_op jit(solution)/shard_map/ppermute | solution.py:817
  408.2 12.8 %collective-permute-start.23 = (bf16[2,96,768]{2,1,0:T(8,128)(2,1)S(1)}, bf16[2,96,768]{2,1,0:T(8,128)(2,1)S(1)}, u32[]{:S(2)}, u32[]{:S(2)}) collective-permute-start(bf16[2,96,768]{2,1,0:T(8,128)(2,1)S(1)} %fusion.19), channel_id=1, source_target_pairs={{0,16},{4,20},{8,24},{12,28},{16,0},{20,4},{24,8},{28,12},{1,17},{... | collective-permute-start | bytes 884744 | tf_op jit(solution)/shard_map/ppermute | solution.py:817
  409.4 14.0 %collective-permute-start.22 = (bf16[2,96,896]{2,1,0:T(8,128)(2,1)S(1)}, bf16[2,96,896]{2,1,0:T(8,128)(2,1)S(1)}, u32[]{:S(2)}, u32[]{:S(2)}) collective-permute-start(bf16[2,96,896]{2,1,0:T(8,128)(2,1)S(1)} %fusion.17), channel_id=1, source_target_pairs={{0,8},{4,12},{8,0},{12,4},{16,24},{20,28},{24,16},{28,20},{1,9},{5... | collective-permute-start | bytes 1032200 | tf_op jit(solution)/shard_map/ppermute | solution.py:817
  424.4 9.1 %collective-permute-start.24 = (bf16[96,896]{1,0:T(8,128)(2,1)S(1)}, bf16[96,896]{1,0:T(8,128)(2,1)S(1)}, u32[]{:S(2)}, u32[]{:S(2)}) collective-permute-start(bf16[96,896]{1,0:T(8,128)(2,1)S(1)} %fusion.23), channel_id=1, source_target_pairs={{0,16},{4,20},{8,24},{12,28},{16,0},{20,4},{24,8},{28,12},{1,17},{... | collective-permute-start | bytes 516104 | tf_op jit(solution)/shard_map/ppermute | solution.py:817

commit v4 on v3

--- a/solution.py
+++ b/solution.py
@@ -188,94 +188,93 @@
     return tok < limit
 
 
-def route_kernel(local, len_ref, h_ref, rw_ref, rcol_ref, rrow_ref, info_ref, pos_ref):
+def route_kernel(local, len_ref, h_ref, rw_ref, routes_ref, info_ref, line_ref, pos_ref):
     t = h_ref.shape[1]
     items = t // SEQ
-    lane = lax.broadcasted_iota(jnp.int32, (t, LANES), 1)
-    r0 = rcol_ref[:, 0:1]
-    r1 = rcol_ref[:, 1:2]
-    live = live_of(len_ref, items, (t, 1), 0)
-    is0 = lane == r0
-    is1 = lane == r1
-    hot = jnp.where((is0 | is1) & live, 1.0, 0.0)
+    r0, r1 = routes_ref[0:1, :], routes_ref[1:2, :]
+    expert = lax.broadcasted_iota(jnp.int32, (EXPERTS, t), 0)
+    is0, is1 = expert == r0, expert == r1
+    live = live_of(len_ref, items, (1, t), 1)
+    hot = (is0 | is1) & live
     before = (
         lax.broadcasted_iota(jnp.int32, (t, t), 1) < lax.broadcasted_iota(jnp.int32, (t, t), 0)
     )
     tri = jnp.where(before, 1.0, 0.0).astype(BF16)
-    count = dot_nn(tri, hot.astype(BF16))
-    p0 = jnp.sum(jnp.where(is0, count, 0.0), -1, keepdims=True)
-    p1 = jnp.sum(jnp.where(is1, count, 0.0), -1, keepdims=True)
+    count = dot_nt(jnp.where(hot, 1.0, 0.0).astype(BF16), tri)
+    pos_ref[...] = jnp.where(hot, count, -1.0)
+    pick = lambda where, v: jnp.sum(jnp.where(where, v, 0.0), 0, keepdims=True)
+    p0, p1 = pick(is0, count), pick(is1, count)
     groups = EXPERTS // local
     block0 = (r0 % local) * groups + r0 // local
     block1 = (r1 % local) * groups + r1 // local
     slot0 = jnp.where(live & (p0 < CAP), block0.astype(F32) * CAP + p0, -1.0)
     slot1 = jnp.where(live & (p1 < CAP), block1.astype(F32) * CAP + p1, -1.0)
-    logits = dot_nn(h_ref[0], rw_ref[...])
-    l0 = jnp.sum(jnp.where(is0, logits, 0.0), -1, keepdims=True)
-    l1 = jnp.sum(jnp.where(is1, logits, 0.0), -1, keepdims=True)
+    logits = dot_nt(rw_ref[...], h_ref[0])
+    l0, l1 = pick(is0, logits), pick(is1, logits)
     top = jnp.maximum(l0, l1)
     e0 = jnp.exp(l0 - top)
     e1 = jnp.exp(l1 - top)
     total = e0 + e1
-    info = jnp.zeros((t, LANES), F32)
-    for k, column in enumerate(
+    line = jnp.zeros((8, t), F32)
+    for k, value in enumerate(
         (e0 / total, e1 / total, slot0, slot1, r0.astype(F32), r1.astype(F32))
     ):
-        info = jnp.where(lane == k, column, info)
-    info_ref[...] = info
-    expert = lax.broadcasted_iota(jnp.int32, (EXPERTS, t), 0)
-    live_row = live_of(len_ref, items, (1, t), 1)
-    hot_row = ((expert == rrow_ref[0:1, :]) | (expert == rrow_ref[1:2, :])) & live_row
-    count_row = dot_nt(jnp.where(hot_row, 1.0, 0.0).astype(BF16), tri)
-    pos_ref[...] = jnp.where(hot_row, count_row, -1.0)
-
-
-def route(local, lengths, rows, rw_pad, routes, routes_t):
+        line = jnp.where(expert == k, value, line)
+    line_ref[...] = line
+    info_ref[:, 0:8] = line.T
+
+
+def route(local, lengths, rows, rw_t, routes_t):
     t = rows.shape[1]
     return pl.pallas_call(
         functools.partial(route_kernel, local),
         name="route",
         grid=(1,),
         in_specs=[
-            pl.BlockSpec(memory_space=pltpu.SMEM), kind_of(H_MLP, t), whole(rw_pad.shape),
-            whole(routes.shape), whole(routes_t.shape),
+            pl.BlockSpec(memory_space=pltpu.SMEM), kind_of(H_MLP, t), whole(rw_t.shape),
+            whole(routes_t.shape),
         ],
-        out_specs=[whole((t, LANES)), whole((EXPERTS, t))],
+        out_specs=[whole((t, LANES)), whole((8, t)), whole((EXPERTS, t))],
         out_shape=[
             jax.ShapeDtypeStruct((t, LANES), F32),
+            jax.ShapeDtypeStruct((8, t), F32),
             jax.ShapeDtypeStruct((EXPERTS, t), F32),
         ],
         compiler_params=params(),
         cost_estimate=cost(int(1e9), int(3e6)),
-    )(lengths, rows, rw_pad, routes, routes_t)
-
-
-def dispatch_kernel(local, first, h_ref, cot_ref, mod_ref, info_ref, pos_ref, out_ref, grad_scr):
-    group = pl.program_id(0)
+    )(lengths, rows, rw_t, routes_t)
+
+
+def dispatch_kernel(local, first, h_ref, cot_ref, mod_ref, line_ref, pos_ref, out_ref):
     t = h_ref.shape[1]
     items = t // SEQ
-    expert = group * local + first
-
-    @pl.when(group == 0)
-    def _():
-        for i in range(items):
-            rows = slice(i * SEQ, (i + 1) * SEQ)
-            grad_scr[rows] = mod_ref[i, 5:6, :] * cot_ref[rows].astype(F32)
-
+    expert = pl.program_id(0) * local + first
     pos = pos_ref[pl.ds(expert, 1), :]
     slot = lax.broadcasted_iota(jnp.int32, (CAP, t), 0).astype(F32)
     hot = jnp.where(slot == pos, 1.0, 0.0).astype(BF16)
     out_ref[0, 0] = dot_nn(hot, h_ref[0]).astype(BF16)
     name = expert.astype(F32)
     weight = jnp.where(
-        info_ref[:, 4:5] == name, info_ref[:, 0:1],
-        jnp.where(info_ref[:, 5:6] == name, info_ref[:, 1:2], 0.0),
-    )
-    rows = (weight * grad_scr[...]).astype(BF16)
-    out_ref[0, 1] = dot_nn(hot, rows).astype(BF16)
-
-
-def dispatch(first, local, rows, cot, mod, info, pos):
+        line_ref[4:5] == name, line_ref[0:1], jnp.where(line_ref[5:6] == name, line_ref[1:2], 0.0)
+    )
+    high = weight.astype(BF16).astype(F32)
+    middle = (weight - high).astype(BF16).astype(F32)
+    item = (lax.broadcasted_iota(jnp.int32, (1, t), 1) // SEQ).astype(F32)
+    lane = lax.broadcasted_iota(jnp.int32, (8, t), 0)
+    table = jnp.zeros((8, t), F32)
+    for k, value in enumerate((high, middle, weight - high - middle, item)):
+        table = jnp.where(lane == k, value, table)
+    values = dot_nt(hot, table.astype(BF16))
+    weight_col = values[:, 0:1] + values[:, 1:2] + values[:, 2:3]
+    item_col = values[:, 3:4]
+    gate = jnp.broadcast_to(mod_ref[0, 5:6, :], (CAP, D))
+    for i in range(1, items):
+        gate = jnp.where(item_col == i, mod_ref[i, 5:6, :], gate)
+    grad = gate * dot_nn(hot, cot_ref[...])
+    out_ref[0, 1] = (weight_col * grad).astype(BF16)
+
+
+def dispatch(first, local, rows, cot, mod, line, pos):
     t = rows.shape[1]
     groups = EXPERTS // local
     return pl.pallas_call(
@@ -283,14 +282,13 @@
         name="dispatch",
         grid=(groups,),
         in_specs=[
-            kind_of(H_MLP, t), once((t, D)), once(mod.shape), once((t, LANES)), once((EXPERTS, t)),
+            kind_of(H_MLP, t), once((t, D)), once(mod.shape), once((8, t)), once((EXPERTS, t)),
         ],
         out_specs=pl.BlockSpec((1, 2, CAP, D), lambda g: (g, 0, 0, 0)),
         out_shape=jax.ShapeDtypeStruct((groups, 2, CAP, D), BF16),
-        scratch_shapes=[pltpu.VMEM((t, D), F32)],
         compiler_params=params(),
         cost_estimate=cost(int(3.3e9), int(8e6)),
-    )(rows, cot, mod, info, pos)
+    )(rows, cot, mod, line, pos)
 
 
 def gelu_pair(v):
@@ -830,7 +828,8 @@
     def step(self, send_after=(), take_after=()):
         axis, bit = self.stages.pop(0)
         got = swap(after(self.send, *send_after), axis, bit)
-        self.terms.append(after(got, *take_after))
+        self.got = after(got, *take_after)
+        self.terms.append(self.got)
         if self.stages:
             terms = self.terms
             self.terms = [v[1] for v in terms]
@@ -905,18 +904,17 @@
 
     act = jax.nn.silu(condition.astype(F32)).astype(BF16)
     mod = dot_nn(act, ada_weight).reshape(items, 6, D)
-    rw_pad = jnp.pad(router_weight, ((0, 0), (0, LANES - EXPERTS)))
     rw_t = router_weight.T
     rwt_pad = jnp.pad(jnp.concatenate([rw_t, rw_t], 0), ((0, LANES - 2 * EXPERTS), (0, 0)))
 
     qkv, lse, attn, rows = attn_forward(lengths, tokens, cotangent, mod, qkv_weight, out_weight)
     if fast:
         peer_rows = swap(rows, "expert", 1)
-    info, pos = route(local, lengths, rows, rw_pad, routes, routes.T)
+    info, line, pos = route(local, lengths, rows, rw_t, routes.T)
     sent, received = [], []
     rows_now = rows
     for j in range(local):
-        sent.append(dispatch(j, local, rows_now, cotangent, mod, info, pos))
+        sent.append(dispatch(j, local, rows_now, cotangent, mod, line, pos))
         rows_now = after(rows, sent[j])
     sres, gsh, s_act, *s_gpre = shared_main(fast, where, rows_now, shared_in, shared_out)
     if fast:
@@ -984,7 +982,8 @@
                 in1.step(take_after=now)
                 in0.step(take_after=now)
                 out1.step(take_after=now)
-                where_now = after(where, in0.terms[-1], out1.send, in1.send)
+                shared_sum.step(take_after=now)
+                where_now = after(where, in0.got, out1.got, in1.send, shared_sum.got)
     result, grad_tokens, grad_mod = outs
     stacks = [rows, peer_rows] if fast else [rows]
     if not fast:
@@ -1013,8 +1012,8 @@
         tail_sum = Chain(*tail, dense_stages)
         token = tail[0]
         for chain in (
-            shared_sum, out1, in1, shared_sum, tail_sum, in1, shared_sum, tail_sum, shared_sum,
-            tail_sum, tail_sum,
+            out1, in1, shared_sum, tail_sum, in1, shared_sum, tail_sum, shared_sum, tail_sum,
+            tail_sum,
         ):
             chain.step(take_after=(token,))
             token = chain.send if chain.stages else chain.terms[-1]

time: 447 us -> 440 us (0.984)
  transfers between devices with their start and end apart: 30 -> 30, of which waited for: 12 -> 11; matrix products, arithmetic and copies ran while one was open for 12% -> 12% of each run, Pallas kernels for 52% -> 53%
where the time goes in v4:
time: 440 us; the launch traced here: 434 us
  Pallas kernels  262 us (60%)
  waiting for transfers between devices  59.9 us (14%)
  starting transfers between devices  50 us (11%)
  other arithmetic  42.9 us (10%)
  local copies, waits for them, and re-layouts  13.3 us (3%)
  matrix products  5.04 us (1%)
    pallas_call x2, Pallas kernels, backward(): pl.pallas_call(functools.partial(backward_kernel, local, fast, first_item...  59.9 us
    ppermute x25, waiting for transfers between devices, swap(): lax.ppermute(value.astype(BF16), axis, [(i, i ^ bit) for i in range(size)])  54.6 us
    pallas_call x2, Pallas kernels, expert_second(): pl.pallas_call(expert_second_kernel, name='expert_second', grid=(rows.sha...  45.6 us
    pallas_call x2, Pallas kernels, expert_first(): pl.pallas_call(functools.partial(expert_first_kernel, fast), name='expert...  33.8 us
    convert_element_type x14, other arithmetic, step(): self.send = self.total().astype(BF16)  29.6 us
    ppermute x25, starting transfers between devices, swap(): lax.ppermute(value.astype(BF16), axis, [(i, i ^ bit) for i in range(size)])  28.8 us
    pallas_call x1, Pallas kernels, shared_main(): pl.pallas_call(functools.partial(shared_main_kernel, halved), name='share...  27.9 us
    pallas_call x1, Pallas kernels, shared_grad(): pl.pallas_call(shared_grad_kernel, name='shared_grad', grid_spec=pltpu.Pr...  20.8 us
  transfers between devices with their start and end apart: 30, of which 11 were waited for; matrix products, arithmetic and copies ran while one was open for 12% of the time, Pallas kernels for 53%

profile of v4, /device:TPU:0, one launch (start us, length us, event | category | flops | bytes accessed | tf_op | source)
XLA Modules:
  0.0 434.2 jit_solution(16263759360899575624)
XLA Ops:
  0.6 4.0 fusion.31
  5.4 20.8 %attn_forward.1 = (bf16[1024,2304]{1,0:T(8,128)(2,1)}, f32[1024,128]{1,0:T(8,128)}, f32[1024,768]{1,0:T(8,128)}, bf16[4,1024,768]{2,1,0:T(8,128)(2,1)}) custom-call(s32[4]{0:T(128)} %len_ref.7, bf16[1024,768]{1,0:T(8,128)(2,1)} %tok_ref.3, bf16[1024,768]{1,0:T(8,128)(2,1)} %cot_ref.9, f32[4,6,768]{2,1,0:T(8,128)} %reshape.219.mod_ref, ...), custom_call_target="tpu_custom_call" | custom-call | flops 4049999872 | bytes 12000000 | tf_op jit(solution)/shard_map/attn_forward/pallas_call | solution.py:158
  26.2 3.3 route.1
  29.4 7.4 %dispatch.2 = bf16[4,2,256,768]{3,2,1,0:T(8,128)(2,1)} custom-call(bf16[4,1024,768]{2,1,0:T(8,128)(2,1)} %get-tuple-element.118.h_ref.x_ref.g_ref.mine_ref.refs_0_, bf16[1024,768]{1,0:T(8,128)(2,1)} %cot_ref.9, f32[4,6,768]{2,1,0:T(8,128)} %reshape.219.mod_ref, f32[8,1024]{1,0:T(8,128)} %get-tuple-element.89.line_ref, f32[8,1024]{1,0:T(8,128)} %get-tuple-element.90.pos_ref), custom_call_target="tpu_custom_call" | custom-call | flops 1650000000 | bytes 4000000 | tf_op jit(solution)/shard_map/dispatch/pallas_call | solution.py:280
  36.9 4.4 %all-to-all-start.1 = ((bf16[4,2,256,768]{3,2,1,0:T(8,128)(2,1)}), bf16[4,2,256,768]{3,2,1,0:T(8,128)(2,1)S(1)}, u32[]{:S(2)}, u32[]{:S(2)}) async-start(bf16[4,2,256,768]{3,2,1,0:T(8,128)(2,1)} %dispatch.2), calls=%async_computation.1 | async-start | bytes 6291456 | tf_op jit(solution)/shard_map/all_to_all | solution.py:925
  41.3 7.4 %dispatch.3 = bf16[4,2,256,768]{3,2,1,0:T(8,128)(2,1)} custom-call(bf16[4,1024,768]{2,1,0:T(8,128)(2,1)} %get-tuple-element.118.h_ref.x_ref.g_ref.mine_ref.refs_0_, bf16[1024,768]{1,0:T(8,128)(2,1)} %cot_ref.9, f32[4,6,768]{2,1,0:T(8,128)} %reshape.219.mod_ref, f32[8,1024]{1,0:T(8,128)} %get-tuple-element.89.line_ref, f32[8,1024]{1,0:T(8,128)} %get-tuple-element.90.pos_ref), custom_call_target="tpu_custom_call" | custom-call | flops 1650000000 | bytes 4000000 | tf_op jit(solution)/shard_map/dispatch/pallas_call | solution.py:280
  49.4 27.9 %shared_main.1 = (f32[1024,768]{1,0:T(8,128)}, f32[1024,768]{1,0:T(8,128)}, bf16[1024,3072]{1,0:T(8,128)(2,1)}, bf16[1024,1536]{1,0:T(8,128)(2,1)}, bf16[1024,1536]{1,0:T(8,128)(2,1)}) custom-call(s32[5]{0:T(128)} %stack.41.where_ref, bf16[4,1024,768]{2,1,0:T(8,128)(2,1)} %get-tuple-element.118.h_ref.x_ref.g_ref.mine_ref.refs_0_, ...), custom_call_target="tpu_custom_call" | custom-call | flops 9663676416 | bytes 15000000 | tf_op jit(solution)/shard_map/shared_main/pallas_call | solution.py:328
  77.2 1.0 all-to-all-done.1.rows_ref.a_ref
  78.3 1.9 copy-done.2
  80.1 4.9 %all-to-all-start = ((bf16[4,2,256,768]{3,2,1,0:T(8,128)(2,1)}), bf16[4,2,256,768]{3,2,1,0:T(8,128)(2,1)}, u32[]{:S(2)}, u32[]{:S(2)}) async-start(bf16[4,2,256,768]{3,2,1,0:T(8,128)(2,1)} %dispatch.3), calls=%async_computation | async-start | bytes 6291456 | tf_op jit(solution)/shard_map/all_to_all | solution.py:925
  86.3 16.9 %expert_first.2 = (bf16[1024,3072]{1,0:T(8,128)(2,1)}, f32[1024,3072]{1,0:T(8,128)}, bf16[2,2,96,3072]{3,2,1,0:T(8,128)(2,1)}, bf16[2,2,96,3072]{3,2,1,0:T(8,128)(2,1)}) custom-call(s32[3]{0:T(128)} %pad_add_fusion.where_ref, bf16[4,2,256,768]{3,2,1,0:T(8,128)(2,1)} %copy-done.2, bf16[2,768,3072]{2,1,0:T(8,128)(2,1)} %w1_ref.9), custom_call_target="tpu_custom_call" | custom-call | flops 4831838208 | bytes 15000000 | tf_op jit(solution)/shard_map/expert_first/pallas_call | solution.py:382
  103.2 2.3 collective-permute-start
  105.5 22.3 %expert_second.2 = (bf16[4,2,256,768]{3,2,1,0:T(8,128)(2,1)}, bf16[1024,3072]{1,0:T(8,128)(2,1)}) custom-call(bf16[4,2,256,768]{3,2,1,0:T(8,128)(2,1)} %copy-done.2, bf16[1024,3072]{1,0:T(8,128)(2,1)} %get-tuple-element.98.act_ref, f32[1024,3072]{1,0:T(8,128)} %get-tuple-element.99.slope_ref, bf16[2,768,3072]{2,1,0:T(8,128)(2,1)} %w1_ref.9, ...), custom_call_target="tpu_custom_call" | custom-call | flops 7247757312 | bytes 20000000 | tf_op jit(solution)/shard_map/expert_second/pallas_call | solution.py:418
  127.8 4.0 all-to-all-start.2
  132.3 9.9 %weight_grad.2 = (bf16[2,2,96,3072]{3,2,1,0:T(8,128)(2,1)}, bf16[2,2,96,3072]{3,2,1,0:T(8,128)(2,1)}) custom-call(s32[3]{0:T(128)} %pad_add_fusion.where_ref, bf16[4,2,256,768]{3,2,1,0:T(8,128)(2,1)} %copy-done.2, bf16[1024,3072]{1,0:T(8,128)(2,1)} %get-tuple-element.102.b_ref), custom_call_target="tpu_custom_call" | custom-call | flops 2415919104 | bytes 6500000 | tf_op jit(solution)/shard_map/weight_grad/pallas_call | solution.py:462
  142.3 16.9 %expert_first.3 = (bf16[1024,3072]{1,0:T(8,128)(2,1)}, f32[1024,3072]{1,0:T(8,128)}, bf16[2,2,96,3072]{3,2,1,0:T(8,128)(2,1)}, bf16[2,2,96,3072]{3,2,1,0:T(8,128)(2,1)}) custom-call(s32[3]{0:T(128)} %pad_add_fusion.where_ref, bf16[4,2,256,768]{3,2,1,0:T(8,128)(2,1)} %all-to-all-done.rows_ref.a_ref, bf16[2,768,3072]{2,1,0:T(8,128)(2,1)} %w1_ref.9), custom_call_target="tpu_custom_call" | custom-call | flops 4831838208 | bytes 15000000 | tf_op jit(solution)/shard_map/expert_first/pallas_call | solution.py:382
  159.2 3.0 fusion
  162.2 2.2 collective-permute-start.1
  164.4 4.2 all-to-all-done.2.rest_0_
  168.7 23.4 %expert_second.3 = (bf16[4,2,256,768]{3,2,1,0:T(8,128)(2,1)}, bf16[1024,3072]{1,0:T(8,128)(2,1)}) custom-call(bf16[4,2,256,768]{3,2,1,0:T(8,128)(2,1)} %all-to-all-done.rows_ref.a_ref, bf16[1024,3072]{1,0:T(8,128)(2,1)} %get-tuple-element.109.act_ref, f32[1024,3072]{1,0:T(8,128)} %get-tuple-element.110.slope_ref, bf16[2,768,3072]{2,1,0:T(8,128)(2,1)} %w1_ref.9, ...), custom_call_target="tpu_custom_call" | custom-call | flops 7247757312 | bytes 20000000 | tf_op jit(solution)/shard_map/expert_second/pallas_call | solution.py:418
  192.1 4.2 all-to-all-start.3
  197.2 9.9 %weight_grad.3 = (bf16[2,2,96,3072]{3,2,1,0:T(8,128)(2,1)}, bf16[2,2,96,3072]{3,2,1,0:T(8,128)(2,1)}) custom-call(s32[3]{0:T(128)} %pad_add_fusion.where_ref, bf16[4,2,256,768]{3,2,1,0:T(8,128)(2,1)} %all-to-all-done.rows_ref.a_ref, bf16[1024,3072]{1,0:T(8,128)(2,1)} %get-tuple-element.113.b_ref), custom_call_target="tpu_custom_call" | custom-call | flops 2415919104 | bytes 6500000 | tf_op jit(solution)/shard_map/weight_grad/pallas_call | solution.py:462
  207.1 1.1 collective-permute-done.2
  208.2 1.8 collective-permute-start.8
  210.0 3.1 fusion.1
  213.1 1.6 collective-permute-start.7
  214.8 2.5 fusion.15
  217.8 2.5 collective-permute-start.6
  220.3 20.8 %shared_grad.1 = (bf16[2,2,2,2,96,768]{5,4,3,2,1,0:T(8,128)(2,1)}, bf16[2,2,2,2,96,768]{5,4,3,2,1,0:T(8,128)(2,1)}) custom-call(s32[5]{0:T(128)} %stack.41.where_ref, bf16[4,1024,768]{2,1,0:T(8,128)(2,1)} %get-tuple-element.118.h_ref.x_ref.g_ref.mine_ref.refs_0_, bf16[4,1024,768]{2,1,0:T(8,128)(2,1)} %collective-permute-done.3.peer_ref.refs_1_, ...), custom_call_target="tpu_custom_call" | custom-call | flops 4831838208 | bytes 12500000 | tf_op jit(solution)/shard_map/shared_grad/pallas_call | solution.py:531
  241.1 1.6 collective-permute-start.12
  242.8 1.7 copy-done.1
  244.4 29.8 %backward.2 = (bf16[1024,768]{1,0:T(8,128)(2,1)}, f32[1024,768]{1,0:T(8,128)}, f32[4,8,768]{2,1,0:T(8,128)}, bf16[512,1664]{1,0:T(8,128)(2,1)}, bf16[512,1664]{1,0:T(8,128)(2,1)}) custom-call(s32[4]{0:T(128)} %len_ref.7, s32[5]{0:T(128)} %stack.41.where_ref, bf16[1024,768]{1,0:T(8,128)(2,1)} %tok_ref.3, bf16[1024,768]{1,0:T(8,128)(2,1)} %cot_ref.9, ...), custom_call_target="tpu_custom_call" | custom-call | flops 5000000000 | bytes 7000000 | tf_op jit(solution)/shard_map/backward/pallas_call | solution.py:676
  274.3 2.0 fusion.2
  276.8 2.5 fusion.14
  279.4 30.1 %backward.3 = (bf16[1024,768]{1,0:T(8,128)(2,1)}, f32[1024,768]{1,0:T(8,128)}, f32[4,8,768]{2,1,0:T(8,128)}, bf16[512,1664]{1,0:T(8,128)(2,1)}, bf16[512,1664]{1,0:T(8,128)(2,1)}) custom-call(s32[4]{0:T(128)} %len_ref.7, s32[5]{0:T(128)} %stack.41.where_ref, ...), custom_call_target="tpu_custom_call", output_to_operand_aliasing={{0}: (16, {}), {1}: (17, {}), {2}: (18, {})} | custom-call | flops 5000000000 | bytes 7000000 | tf_op jit(solution)/shard_map/backward/pallas_call | solution.py:676
  309.5 2.6 collective-permute-done.11
  313.6 2.0 fusion.6
  316.0 2.7 fusion.3
  318.7 2.5 fusion.13
  321.1 2.6 collective-permute-start.18
  324.9 1.6 collective-permute-start.17
  326.5 2.6 fusion.4
  329.1 1.5 collective-permute-start.16
  330.6 14.8 %tail_grad.1 = (bf16[2,2,2,96,896]{4,3,2,1,0:T(8,128)(2,1)}, bf16[2,2,2,96,896]{4,3,2,1,0:T(8,128)(2,1)}) custom-call(s32[5]{0:T(128)} %stack.41.where_ref, bf16[4,1024,768]{2,1,0:T(8,128)(2,1)} %get-tuple-element.118.h_ref.x_ref.g_ref.mine_ref.refs_0_, bf16[4,1024,768]{2,1,0:T(8,128)(2,1)} %collective-permute-done.3.peer_ref.refs_1_, ...), custom_call_target="tpu_custom_call" | custom-call | flops 2500000000 | bytes 10000000 | tf_op jit(solution)/shard_map/tail_grad/pallas_call | solution.py:764
  345.5 1.4 collective-permute-start.15
  346.9 3.6 all-to-all-start.4
  350.5 1.9 fusion.5
  352.5 15.8 %collective-permute-done.17 = bf16[2,96,3072]{2,1,0:T(8,128)(2,1)} collective-permute-done((bf16[2,96,3072]{2,1,0:T(8,128)(2,1)}, bf16[2,96,3072]{2,1,0:T(8,128)(2,1)}, u32[]{:S(2)}, u32[]{:S(2)}) %collective-permute-start.17) | collective-permute-done | bytes 1179680 | tf_op jit(solution)/shard_map/ppermute | solution.py:815
  368.3 2.3 fusion.12
  371.8 1.9 copy.38
  373.7 1.7 fusion.11
  375.4 2.5 collective-permute-start.20
  378.0 2.2 collective-permute-done.15
  380.2 1.3 fusion.16
  382.0 14.7 %collective-permute-done.21 = bf16[96,3072]{1,0:T(8,128)(2,1)} collective-permute-done((bf16[96,3072]{1,0:T(8,128)(2,1)}, bf16[96,3072]{1,0:T(8,128)(2,1)}, u32[]{:S(2)}, u32[]{:S(2)}) %collective-permute-start.21) | collective-permute-done | bytes 589856 | tf_op jit(solution)/shard_map/ppermute | solution.py:815
  396.7 3.0 fusion.8
  400.5 1.3 fusion.19
  401.9 1.1 fusion.17
  403.0 2.5 collective-permute-start.22
  405.5 1.6 pad_maximum_fusion
  407.1 9.1 %collective-permute-done.23 = bf16[2,96,768]{2,1,0:T(8,128)(2,1)S(1)} collective-permute-done((bf16[2,96,768]{2,1,0:T(8,128)(2,1)S(1)}, bf16[2,96,768]{2,1,0:T(8,128)(2,1)S(1)}, u32[]{:S(2)}, u32[]{:S(2)}) %collective-permute-start.23) | collective-permute-done | bytes 294944 | tf_op jit(solution)/shard_map/ppermute | solution.py:815
  416.2 1.3 fusion.18
  421.2 7.2 %collective-permute-done.24 = bf16[96,896]{1,0:T(8,128)(2,1)S(1)} collective-permute-done((bf16[96,896]{1,0:T(8,128)(2,1)S(1)}, bf16[96,896]{1,0:T(8,128)(2,1)S(1)}, u32[]{:S(2)}, u32[]{:S(2)}) %collective-permute-start.24) | collective-permute-done | bytes 172064 | tf_op jit(solution)/shard_map/ppermute | solution.py:815
  431.7 1.1 reshape.222
  (76 shorter events, 18.6 us)
Async XLA Ops:
  36.9 41.4 %all-to-all-start.1 = ((bf16[4,2,256,768]{3,2,1,0:T(8,128)(2,1)}), bf16[4,2,256,768]{3,2,1,0:T(8,128)(2,1)S(1)}, u32[]{:S(2)}, u32[]{:S(2)}) async-start(bf16[4,2,256,768]{3,2,1,0:T(8,128)(2,1)} %dispatch.2), calls=%async_computation.1 | async-start | bytes 6291456 | tf_op jit(solution)/shard_map/all_to_all | solution.py:925
  78.3 1.9 copy-start.2
  80.1 47.7 %all-to-all-start = ((bf16[4,2,256,768]{3,2,1,0:T(8,128)(2,1)}), bf16[4,2,256,768]{3,2,1,0:T(8,128)(2,1)}, u32[]{:S(2)}, u32[]{:S(2)}) async-start(bf16[4,2,256,768]{3,2,1,0:T(8,128)(2,1)} %dispatch.3), calls=%async_computation | async-start | bytes 6291456 | tf_op jit(solution)/shard_map/all_to_all | solution.py:925
  85.1 135.2 %collective-permute-start.3 = (bf16[4,1024,768]{2,1,0:T(8,128)(2,1)}, bf16[4,1024,768]{2,1,0:T(8,128)(2,1)}, u32[]{:S(2)}, u32[]{:S(2)}) collective-permute-start(bf16[4,1024,768]{2,1,0:T(8,128)(2,1)} %get-tuple-element.118.h_ref.x_ref.g_ref.mine_ref.refs_0_), channel_id=1, source_target_pairs={{0,1},{1,0},{2,3},{3,2},{4,5},{5,4},{6,7},{7,6},{8,9},{9,8},{10,11... | collective-permute-start | bytes 18874376 | tf_op jit(solution)/shard_map/ppermute | solution.py:815
  85.6 132.1 %collective-permute-start.5 = (bf16[1024,3072]{1,0:T(8,128)(2,1)}, bf16[1024,3072]{1,0:T(8,128)(2,1)}, u32[]{:S(2)}, u32[]{:S(2)}) collective-permute-start(bf16[1024,3072]{1,0:T(8,128)(2,1)} %get-tuple-element.121.act_ref), channel_id=1, source_target_pairs={{0,1},{1,0},{2,3},{3,2},{4,5},{5,4},{6,7},{7,6},{8,9},{9,8},{10,11... | collective-permute-start | bytes 18874376 | tf_op jit(solution)/shard_map/ppermute | solution.py:815
  103.2 56.0 %collective-permute-start = (bf16[2,2,96,3072]{3,2,1,0:T(8,128)(2,1)}, bf16[2,2,96,3072]{3,2,1,0:T(8,128)(2,1)}, u32[]{:S(2)}, u32[]{:S(2)}) collective-permute-start(bf16[2,2,96,3072]{3,2,1,0:T(8,128)(2,1)} %get-tuple-element.106), channel_id=1, source_target_pairs={{0,4},{4,0},{8,12},{12,8},{16,20},{20,16},{24,28},{28,24},{1,5},{5... | collective-permute-start | bytes 7077896 | tf_op jit(solution)/shard_map/ppermute | solution.py:815
  127.8 40.9 %all-to-all-start.2 = ((bf16[4,2,256,768]{3,2,1,0:T(8,128)(2,1)}), bf16[4,2,256,768]{3,2,1,0:T(8,128)(2,1)S(1)}, u32[]{:S(2)}, u32[]{:S(2)}) async-start(bf16[4,2,256,768]{3,2,1,0:T(8,128)(2,1)} %get-tuple-element.100), calls=%async_computation.2 | async-start | bytes 6291456 | tf_op jit(solution)/shard_map/all_to_all | solution.py:941
  131.8 85.4 %collective-permute-start.4 = (bf16[1024,1536]{1,0:T(8,128)(2,1)}, bf16[1024,1536]{1,0:T(8,128)(2,1)}, u32[]{:S(2)}, u32[]{:S(2)}) collective-permute-start(bf16[1024,1536]{1,0:T(8,128)(2,1)} %get-tuple-element.120), channel_id=1, source_target_pairs={{0,1},{1,0},{2,3},{3,2},{4,5},{5,4},{6,7},{7,6},{8,9},{9,8},{10,11... | collective-permute-start | bytes 9437192 | tf_op jit(solution)/shard_map/ppermute | solution.py:815
  142.2 66.0 %collective-permute-start.2 = (bf16[2,2,96,3072]{3,2,1,0:T(8,128)(2,1)}, bf16[2,2,96,3072]{3,2,1,0:T(8,128)(2,1)}, u32[]{:S(2)}, u32[]{:S(2)}) collective-permute-start(bf16[2,2,96,3072]{3,2,1,0:T(8,128)(2,1)} %get-tuple-element.116), channel_id=1, source_target_pairs={{0,4},{4,0},{8,12},{12,8},{16,20},{20,16},{24,28},{28,24},{1,5},{5... | collective-permute-start | bytes 7077896 | tf_op jit(solution)/shard_map/ppermute | solution.py:815
  162.2 50.9 %collective-permute-start.1 = (bf16[2,96,3072]{2,1,0:T(8,128)(2,1)}, bf16[2,96,3072]{2,1,0:T(8,128)(2,1)}, u32[]{:S(2)}, u32[]{:S(2)}) collective-permute-start(bf16[2,96,3072]{2,1,0:T(8,128)(2,1)} %fusion), channel_id=1, source_target_pairs={{0,8},{4,12},{8,0},{12,4},{16,24},{20,28},{24,16},{28,20},{1,9},{5... | collective-permute-start | bytes 3538952 | tf_op jit(solution)/shard_map/ppermute | solution.py:815
  168.7 23.4 %copy-start = (bf16[4,2,256,768]{3,2,1,0:T(8,128)(2,1)}, bf16[4,2,256,768]{3,2,1,0:T(8,128)(2,1)S(1)}, u32[]{:S(2)}) copy-start(bf16[4,2,256,768]{3,2,1,0:T(8,128)(2,1)S(1)} %all-to-all-done.2.rest_0_) | copy-start | bytes 9437188
  192.1 4.3 copy-start.7
  192.1 4.4 %copy-start.6 = (bf16[768,8]{0,1:T(8,128)(2,1)S(1)}, bf16[768,8]{0,1:T(8,128)(2,1)}, u32[]{:S(2)}) copy-start(bf16[768,8]{0,1:T(8,128)(2,1)} %param.21) | copy-start | bytes 36868
  192.1 50.6 %all-to-all-start.3 = ((bf16[4,2,256,768]{3,2,1,0:T(8,128)(2,1)}), bf16[4,2,256,768]{3,2,1,0:T(8,128)(2,1)S(1)}, u32[]{:S(2)}, u32[]{:S(2)}) async-start(bf16[4,2,256,768]{3,2,1,0:T(8,128)(2,1)} %get-tuple-element.111), calls=%async_computation.3 | async-start | bytes 6291456 | tf_op jit(solution)/shard_map/all_to_all | solution.py:941
  208.2 66.0 %collective-permute-start.8 = (bf16[2,2,96,3072]{3,2,1,0:T(8,128)(2,1)}, bf16[2,2,96,3072]{3,2,1,0:T(8,128)(2,1)}, u32[]{:S(2)}, u32[]{:S(2)}) collective-permute-start(bf16[2,2,96,3072]{3,2,1,0:T(8,128)(2,1)} %get-tuple-element.133), channel_id=1, source_target_pairs={{0,4},{4,0},{8,12},{12,8},{16,20},{20,16},{24,28},{28,24},{1,5},{5... | collective-permute-start | bytes 7077896 | tf_op jit(solution)/shard_map/ppermute | solution.py:815
  213.1 61.2 %collective-permute-start.7 = (bf16[2,96,3072]{2,1,0:T(8,128)(2,1)}, bf16[2,96,3072]{2,1,0:T(8,128)(2,1)}, u32[]{:S(2)}, u32[]{:S(2)}) collective-permute-start(bf16[2,96,3072]{2,1,0:T(8,128)(2,1)} %fusion.1), channel_id=1, source_target_pairs={{0,8},{4,12},{8,0},{12,4},{16,24},{20,28},{24,16},{28,20},{1,9},{5... | collective-permute-start | bytes 3538952 | tf_op jit(solution)/shard_map/ppermute | solution.py:815
  217.2 94.9 %collective-permute-start.11 = (bf16[2,2,96,3072]{3,2,1,0:T(8,128)(2,1)}, bf16[2,2,96,3072]{3,2,1,0:T(8,128)(2,1)}, u32[]{:S(2)}, u32[]{:S(2)}) collective-permute-start(bf16[2,2,96,3072]{3,2,1,0:T(8,128)(2,1)} %get-tuple-element.143), channel_id=1, source_target_pairs={{0,4},{4,0},{8,12},{12,8},{16,20},{20,16},{24,28},{28,24},{1,5},{5... | collective-permute-start | bytes 7077896 | tf_op jit(solution)/shard_map/ppermute | solution.py:815
  217.8 56.5 %collective-permute-start.6 = (bf16[96,3072]{1,0:T(8,128)(2,1)}, bf16[96,3072]{1,0:T(8,128)(2,1)}, u32[]{:S(2)}, u32[]{:S(2)}) collective-permute-start(bf16[96,3072]{1,0:T(8,128)(2,1)} %fusion.15), channel_id=1, source_target_pairs={{0,16},{4,20},{8,24},{12,28},{16,0},{20,4},{24,8},{28,12},{1,17},{... | collective-permute-start | bytes 1769480 | tf_op jit(solution)/shard_map/ppermute | solution.py:815
  241.1 85.4 %collective-permute-start.12 = (bf16[2,2,2,2,96,768]{5,4,3,2,1,0:T(8,128)(2,1)}, bf16[2,2,2,2,96,768]{5,4,3,2,1,0:T(8,128)(2,1)}, u32[]{:S(2)}, u32[]{:S(2)}) collective-permute-start(bf16[2,2,2,2,96,768]{5,4,3,2,1,0:T(8,128)(2,1)} %get-tuple-element.145), channel_id=1, source_target_pairs={{0,2},{1,3},{2,0},{3,1},{4,6},{5,7},{6,4},{7,5},{8,10},{9,11},{10,... | collective-permute-start | bytes 7077896 | tf_op jit(solution)/shard_map/ppermute | solution.py:815
  242.8 1.7 copy-start.1
  276.3 42.4 %collective-permute-start.10 = (bf16[2,96,3072]{2,1,0:T(8,128)(2,1)S(1)}, bf16[2,96,3072]{2,1,0:T(8,128)(2,1)}, u32[]{:S(2)}, u32[]{:S(2)}) collective-permute-start(bf16[2,96,3072]{2,1,0:T(8,128)(2,1)S(1)} %fusion.2), channel_id=1, source_target_pairs={{0,8},{4,12},{8,0},{12,4},{16,24},{20,28},{24,16},{28,20},{1,9},{5... | collective-permute-start | bytes 3538952 | tf_op jit(solution)/shard_map/ppermute | solution.py:815
  279.3 45.5 %collective-permute-start.9 = (bf16[96,3072]{1,0:T(8,128)(2,1)}, bf16[96,3072]{1,0:T(8,128)(2,1)}, u32[]{:S(2)}, u32[]{:S(2)}) collective-permute-start(bf16[96,3072]{1,0:T(8,128)(2,1)} %fusion.14), channel_id=1, source_target_pairs={{0,16},{4,20},{8,24},{12,28},{16,0},{20,4},{24,8},{28,12},{1,17},{... | collective-permute-start | bytes 1769480 | tf_op jit(solution)/shard_map/ppermute | solution.py:815
  312.1 18.5 %collective-permute-start.14 = (bf16[512,1664]{1,0:T(8,128)(2,1)}, bf16[512,1664]{1,0:T(8,128)(2,1)}, u32[]{:S(2)}, u32[]{:S(2)}) collective-permute-start(bf16[512,1664]{1,0:T(8,128)(2,1)} %get-tuple-element.151), channel_id=1, source_target_pairs={{0,1},{1,0},{2,3},{3,2},{4,5},{5,4},{6,7},{7,6},{8,9},{9,8},{10,11... | collective-permute-start | bytes 5111816 | tf_op jit(solution)/shard_map/ppermute | solution.py:815
  312.1 18.5 %collective-permute-start.13 = (bf16[512,1664]{1,0:T(8,128)(2,1)}, bf16[512,1664]{1,0:T(8,128)(2,1)}, u32[]{:S(2)}, u32[]{:S(2)}) collective-permute-start(bf16[512,1664]{1,0:T(8,128)(2,1)} %get-tuple-element.150), channel_id=1, source_target_pairs={{0,1},{1,0},{2,3},{3,2},{4,5},{5,4},{6,7},{7,6},{8,9},{9,8},{10,11... | collective-permute-start | bytes 5111816 | tf_op jit(solution)/shard_map/ppermute | solution.py:815
  313.6 2.4 copy-start.3
  321.1 29.3 %collective-permute-start.18 = (bf16[96,3072]{1,0:T(8,128)(2,1)}, bf16[96,3072]{1,0:T(8,128)(2,1)}, u32[]{:S(2)}, u32[]{:S(2)}) collective-permute-start(bf16[96,3072]{1,0:T(8,128)(2,1)} %fusion.13), channel_id=1, source_target_pairs={{0,16},{4,20},{8,24},{12,28},{16,0},{20,4},{24,8},{28,12},{1,17},{... | collective-permute-start | bytes 1769480 | tf_op jit(solution)/shard_map/ppermute | solution.py:815
  323.9 2.7 copy-start.4
  324.9 43.4 %collective-permute-start.17 = (bf16[2,96,3072]{2,1,0:T(8,128)(2,1)}, bf16[2,96,3072]{2,1,0:T(8,128)(2,1)}, u32[]{:S(2)}, u32[]{:S(2)}) collective-permute-start(bf16[2,96,3072]{2,1,0:T(8,128)(2,1)} %fusion.3), channel_id=1, source_target_pairs={{0,8},{4,12},{8,0},{12,4},{16,24},{20,28},{24,16},{28,20},{1,9},{5... | collective-permute-start | bytes 3538952 | tf_op jit(solution)/shard_map/ppermute | solution.py:815
  329.1 44.6 %collective-permute-start.16 = (bf16[2,2,2,96,768]{4,3,2,1,0:T(8,128)(2,1)}, bf16[2,2,2,96,768]{4,3,2,1,0:T(8,128)(2,1)}, u32[]{:S(2)}, u32[]{:S(2)}) collective-permute-start(bf16[2,2,2,96,768]{4,3,2,1,0:T(8,128)(2,1)} %fusion.4), channel_id=1, source_target_pairs={{0,4},{4,0},{8,12},{12,8},{16,20},{20,16},{24,28},{28,24},{1,5},{5... | collective-permute-start | bytes 3538952 | tf_op jit(solution)/shard_map/ppermute | solution.py:815
  345.5 34.7 %collective-permute-start.15 = (bf16[2,2,2,96,896]{4,3,2,1,0:T(8,128)(2,1)}, bf16[2,2,2,96,896]{4,3,2,1,0:T(8,128)(2,1)}, u32[]{:S(2)}, u32[]{:S(2)}) collective-permute-start(bf16[2,2,2,96,896]{4,3,2,1,0:T(8,128)(2,1)} %get-tuple-element.154), channel_id=1, source_target_pairs={{0,2},{1,3},{2,0},{3,1},{4,6},{5,7},{6,4},{7,5},{8,10},{9,11},{10,... | collective-permute-start | bytes 4128776 | tf_op jit(solution)/shard_map/ppermute | solution.py:815
  346.9 84.8 %all-to-all-start.4 = ((bf16[32,4,1280]{2,1,0:T(4,128)(2,1)}), bf16[32,4,1280]{2,1,0:T(4,128)(2,1)}, u32[]{:S(2)}, u32[]{:S(2)}) async-start(bf16[32,4,1280]{2,1,0:T(4,128)(2,1)} %bitcast.131), calls=%async_computation.4 | async-start | bytes 655360 | tf_op jit(solution)/shard_map/all_to_all | solution.py:886
  370.6 26.1 %collective-permute-start.21 = (bf16[96,3072]{1,0:T(8,128)(2,1)}, bf16[96,3072]{1,0:T(8,128)(2,1)}, u32[]{:S(2)}, u32[]{:S(2)}) collective-permute-start(bf16[96,3072]{1,0:T(8,128)(2,1)} %fusion.12), channel_id=1, source_target_pairs={{0,16},{4,20},{8,24},{12,28},{16,0},{20,4},{24,8},{28,12},{1,17},{... | collective-permute-start | bytes 1769480 | tf_op jit(solution)/shard_map/ppermute | solution.py:815
  373.7 6.5 %copy-start.5 = (bf16[2,2,2,96,896]{4,3,2,1,0:T(8,128)(2,1)S(1)}, bf16[2,2,2,96,896]{4,3,2,1,0:T(8,128)(2,1)}, u32[]{:S(2)}) copy-start(bf16[2,2,2,96,896]{4,3,2,1,0:T(8,128)(2,1)} %get-tuple-element.152) | copy-start | bytes 4128772
  375.4 25.0 %collective-permute-start.20 = (bf16[2,2,96,768]{3,2,1,0:T(8,128)(2,1)S(1)}, bf16[2,2,96,768]{3,2,1,0:T(8,128)(2,1)S(1)}, u32[]{:S(2)}, u32[]{:S(2)}) collective-permute-start(bf16[2,2,96,768]{3,2,1,0:T(8,128)(2,1)S(1)} %fusion.11), channel_id=1, source_target_pairs={{0,8},{4,12},{8,0},{12,4},{16,24},{20,28},{24,16},{28,20},{1,9},{5... | collective-permute-start | bytes 1769480 | tf_op jit(solution)/shard_map/ppermute | solution.py:815
  381.4 20.4 %collective-permute-start.19 = (bf16[2,2,96,896]{3,2,1,0:T(8,128)(2,1)S(1)}, bf16[2,2,96,896]{3,2,1,0:T(8,128)(2,1)S(1)}, u32[]{:S(2)}, u32[]{:S(2)}) collective-permute-start(bf16[2,2,96,896]{3,2,1,0:T(8,128)(2,1)S(1)} %fusion.16), channel_id=1, source_target_pairs={{0,4},{4,0},{8,12},{12,8},{16,20},{20,16},{24,28},{28,24},{1,5},{5... | collective-permute-start | bytes 2064392 | tf_op jit(solution)/shard_map/ppermute | solution.py:815
  401.8 14.4 %collective-permute-start.23 = (bf16[2,96,768]{2,1,0:T(8,128)(2,1)S(1)}, bf16[2,96,768]{2,1,0:T(8,128)(2,1)S(1)}, u32[]{:S(2)}, u32[]{:S(2)}) collective-permute-start(bf16[2,96,768]{2,1,0:T(8,128)(2,1)S(1)} %fusion.19), channel_id=1, source_target_pairs={{0,16},{4,20},{8,24},{12,28},{16,0},{20,4},{24,8},{28,12},{1,17},{... | collective-permute-start | bytes 884744 | tf_op jit(solution)/shard_map/ppermute | solution.py:815
  403.0 15.5 %collective-permute-start.22 = (bf16[2,96,896]{2,1,0:T(8,128)(2,1)S(1)}, bf16[2,96,896]{2,1,0:T(8,128)(2,1)S(1)}, u32[]{:S(2)}, u32[]{:S(2)}) collective-permute-start(bf16[2,96,896]{2,1,0:T(8,128)(2,1)S(1)} %fusion.17), channel_id=1, source_target_pairs={{0,8},{4,12},{8,0},{12,4},{16,24},{20,28},{24,16},{28,20},{1,9},{5... | collective-permute-start | bytes 1032200 | tf_op jit(solution)/shard_map/ppermute | solution.py:815
  419.5 9.0 %collective-permute-start.24 = (bf16[96,896]{1,0:T(8,128)(2,1)S(1)}, bf16[96,896]{1,0:T(8,128)(2,1)S(1)}, u32[]{:S(2)}, u32[]{:S(2)}) collective-permute-start(bf16[96,896]{1,0:T(8,128)(2,1)S(1)} %fusion.23), channel_id=1, source_target_pairs={{0,16},{4,20},{8,24},{12,28},{16,0},{20,4},{24,8},{28,12},{1,17},{... | collective-permute-start | bytes 516104 | tf_op jit(solution)/shard_map/ppermute | solution.py:815

commit v5 on v4

--- a/solution.py
+++ b/solution.py
@@ -706,7 +706,7 @@
 
 
 def tail_grad_kernel(fast, many, where_ref, *refs):
-    count = 2 if fast else 3
+    count = 3
     *refs, stack_ref, grad_ref, sems = refs
     stacks, grads, outs = refs[:many], refs[many:-count], refs[-count:]
     width = 3 * D // 2 if fast else 3 * D
@@ -731,17 +731,18 @@
             dot_tn(stack_ref[i, 2], grad_ref[rows, width + width // 3 :]),
         )
         if i:
-            terms = (d_qkv + terms[0], d_out + terms[1], d_router + terms[2])
+            terms = (d_qkv + terms[0], d_out + terms[1], d_router)
         d_qkv, d_out, d_router = terms
     d_qkv, d_out = d_qkv.astype(BF16), d_out.astype(BF16)
     d_router = (d_router + pltpu.roll(d_router, LANES - EXPERTS, 1)).astype(BF16)
     if not fast:
         outs[0][...], outs[1][...], outs[2][...] = d_qkv, d_out, d_router
         return
+    outs[2][...] = d_router
     first = where_ref[1] == 0
     low, high = [
         jnp.concatenate(
-            [d_qkv[:, 576 * x : 576 * x + 576], d_out[:, 192 * x : 192 * x + 192], d_router], 1
+            [d_qkv[:, 576 * x : 576 * x + 576], d_out[:, 192 * x : 192 * x + 192]], 1
         )
         for x in range(2)
     ]
@@ -752,7 +753,8 @@
 
 def tail_grad(fast, where, stacks, grads):
     if fast:
-        outs = [jax.ShapeDtypeStruct((2, 2, 2, 96, D + LANES), BF16)] * 2
+        outs = [jax.ShapeDtypeStruct((2, 2, 2, 96, D), BF16)] * 2
+        outs.append(jax.ShapeDtypeStruct((D, LANES), BF16))
     else:
         outs = [
             jax.ShapeDtypeStruct((D, 3 * D), BF16),
@@ -991,34 +993,46 @@
     tail = tail_grad(fast, where_now, stacks, own + other)
 
     cols, ada_rows = 6 * D // ne, D // nb
-    mod_parts = grad_mod[:, :6].reshape(items, ne, cols).astype(BF16)
-    mod_parts = jnp.transpose(mod_parts, (1, 0, 2))
-    act_parts = jnp.transpose(act.reshape(items, nb, ada_rows), (1, 0, 2))
-    act_parts = jnp.pad(act_parts, ((0, 0), (0, 0), (0, -ada_rows % LANES)))
-    width = act_parts.shape[-1]
-    parts = jnp.concatenate(
-        [
+    width = ada_rows + -ada_rows % LANES
+    each = ada_rows * EXPERTS // ne // items
+
+    def exchange(*others):
+        mod_parts = after(grad_mod, *others)[:, :6].reshape(items, ne, cols).astype(BF16)
+        mod_parts = jnp.transpose(mod_parts, (1, 0, 2))
+        act_parts = jnp.transpose(act.reshape(items, nb, ada_rows), (1, 0, 2))
+        act_parts = jnp.pad(act_parts, ((0, 0), (0, 0), (0, -ada_rows % LANES)))
+        pieces = [
             jnp.broadcast_to(mod_parts[None], (nb, ne, items, cols)),
             jnp.broadcast_to(act_parts[:, None], (nb, ne, items, width)),
-        ],
-        -1,
-    )
-    got = all_pairs(after(parts, tail[0]))
+        ]
+        if fast:
+            mine = after(tail[2], *others)[:, :EXPERTS].reshape(nb, ada_rows, ne, EXPERTS // ne)
+            mine = jnp.transpose(mine, (0, 2, 1, 3)).reshape(nb, ne, items, each)
+            pieces.append(jnp.pad(mine, ((0, 0), (0, 0), (0, 0), (0, -each % LANES))))
+        parts = jnp.concatenate(pieces, -1)
+        return all_pairs(parts)
+
+    if not fast:
+        got = exchange()
 
     if fast:
         def unfold(v):
             return v.reshape(96, 8, 384).transpose(2, 1, 0).reshape(384, D)
 
-        tail_sum = Chain(*tail, dense_stages)
+        tail_sum = Chain(*tail[:2], dense_stages)
         token = tail[0]
         for chain in (
-            out1, in1, shared_sum, tail_sum, in1, shared_sum, tail_sum, shared_sum, tail_sum,
+            out1, in1, shared_sum, tail_sum, shared_sum, in1, tail_sum, tail_sum, shared_sum,
             tail_sum,
         ):
             chain.step(take_after=(token,))
             token = chain.send if chain.stages else chain.terms[-1]
+            if chain is shared_sum and len(chain.stages) == 2:
+                got = exchange(token)
+            if chain is tail_sum and len(chain.stages) == 1:
+                late = token
         tl = tail_sum.total()
-        got = after(got, token)
+        got = after(got, late)
         assert not any(c.stages for c in (in0, in1, out0, out1, shared_sum, tail_sum))
         sh = shared_sum.total()
         g_sh1 = sh[0]
@@ -1027,7 +1041,8 @@
         g_e2 = jnp.stack([unfold(out0.total()), unfold(out1.total())])
         g_qkv = tl[:, :576]
         g_out = tl[:, 576:768]
-        g_rt = lax.dynamic_slice_in_dim(tl[:, 768:776], 2 * expert, 2, 1)
+        rt = got[..., cols + width : cols + width + each].astype(F32)
+        g_rt = jnp.sum(rt.reshape(nb * ne, ada_rows, EXPERTS // ne), 0)
     else:
         def flipped(grad):
             r, c = grad.shape
@@ -1049,7 +1064,7 @@
         g_qkv = reduce_dense(tail[0])
         g_out = reduce_dense(tail[1])
         g_rt = reduce_dense(tail[2][:, :EXPERTS])
-    got = got.reshape(nb * ne * items, cols + width).astype(F32)
+    got = got.reshape(nb * ne * items, -1).astype(F32)
     grad_ada = jnp.dot(
         got[:, cols : cols + ada_rows].T, got[:, :cols], precision=lax.Precision.HIGHEST
     )

time: 440 us -> 433 us (0.984)
  waiting for transfers between devices: 59.9 us -> 51.7 us
    ppermute x25, waiting for transfers between devices: 54.6 us -> 46.4 us  [swap(): lax.ppermute(value.astype(BF16), axis, [(i, i ^ bit) for i in range(size)])]
  transfers between devices with their start and end apart: 30 -> 30, of which waited for: 11 -> 10; matrix products, arithmetic and copies ran while one was open for 12% -> 12% of each run, Pallas kernels for 53% -> 54%
where the time goes in v5:
time: 433 us; the launch traced here: 427 us
  Pallas kernels  261 us (60%)
  waiting for transfers between devices  51.7 us (12%)
  starting transfers between devices  50.7 us (12%)
  other arithmetic  45.2 us (10%)
  local copies, waits for them, and re-layouts  11.7 us (3%)
  matrix products  5.04 us (1%)
    pallas_call x2, Pallas kernels, backward(): pl.pallas_call(functools.partial(backward_kernel, local, fast, first_item...  59.9 us
    ppermute x25, waiting for transfers between devices, swap(): lax.ppermute(value.astype(BF16), axis, [(i, i ^ bit) for i in range(size)])  46.4 us
    pallas_call x2, Pallas kernels, expert_second(): pl.pallas_call(expert_second_kernel, name='expert_second', grid=(rows.sha...  45.6 us
    pallas_call x2, Pallas kernels, expert_first(): pl.pallas_call(functools.partial(expert_first_kernel, fast), name='expert...  33.8 us
    convert_element_type x14, other arithmetic, step(): self.send = self.total().astype(BF16)  31.8 us
    ppermute x25, starting transfers between devices, swap(): lax.ppermute(value.astype(BF16), axis, [(i, i ^ bit) for i in range(size)])  29.4 us
    pallas_call x1, Pallas kernels, shared_main(): pl.pallas_call(functools.partial(shared_main_kernel, halved), name='share...  27.9 us
    pallas_call x1, Pallas kernels, shared_grad(): pl.pallas_call(shared_grad_kernel, name='shared_grad', grid_spec=pltpu.Pr...  20.8 us
  transfers between devices with their start and end apart: 30, of which 10 were waited for; matrix products, arithmetic and copies ran while one was open for 12% of the time, Pallas kernels for 54%

profile of v5, /device:TPU:0, one launch (start us, length us, event | category | flops | bytes accessed | tf_op | source)
XLA Modules:
  0.0 426.8 jit_solution(15301874325283673365)
XLA Ops:
  0.6 4.0 fusion.33
  5.4 20.8 %attn_forward.1 = (bf16[1024,2304]{1,0:T(8,128)(2,1)}, f32[1024,128]{1,0:T(8,128)}, f32[1024,768]{1,0:T(8,128)}, bf16[4,1024,768]{2,1,0:T(8,128)(2,1)}) custom-call(s32[4]{0:T(128)} %len_ref.7, bf16[1024,768]{1,0:T(8,128)(2,1)} %tok_ref.3, bf16[1024,768]{1,0:T(8,128)(2,1)} %cot_ref.9, f32[4,6,768]{2,1,0:T(8,128)} %reshape.227.mod_ref, ...), custom_call_target="tpu_custom_call" | custom-call | flops 4049999872 | bytes 12000000 | tf_op jit(solution)/shard_map/attn_forward/pallas_call | solution.py:158
  26.2 3.3 route.1
  29.4 7.4 %dispatch.2 = bf16[4,2,256,768]{3,2,1,0:T(8,128)(2,1)} custom-call(bf16[4,1024,768]{2,1,0:T(8,128)(2,1)} %get-tuple-element.120.h_ref.x_ref.g_ref.mine_ref.refs_0_, bf16[1024,768]{1,0:T(8,128)(2,1)} %cot_ref.9, f32[4,6,768]{2,1,0:T(8,128)} %reshape.227.mod_ref, f32[8,1024]{1,0:T(8,128)} %get-tuple-element.91.line_ref, f32[8,1024]{1,0:T(8,128)} %get-tuple-element.92.pos_ref), custom_call_target="tpu_custom_call" | custom-call | flops 1650000000 | bytes 4000000 | tf_op jit(solution)/shard_map/dispatch/pallas_call | solution.py:280
  36.9 4.4 %all-to-all-start.1 = ((bf16[4,2,256,768]{3,2,1,0:T(8,128)(2,1)}), bf16[4,2,256,768]{3,2,1,0:T(8,128)(2,1)S(1)}, u32[]{:S(2)}, u32[]{:S(2)}) async-start(bf16[4,2,256,768]{3,2,1,0:T(8,128)(2,1)} %dispatch.2), calls=%async_computation.1 | async-start | bytes 6291456 | tf_op jit(solution)/shard_map/all_to_all | solution.py:927
  41.3 7.4 %dispatch.3 = bf16[4,2,256,768]{3,2,1,0:T(8,128)(2,1)} custom-call(bf16[4,1024,768]{2,1,0:T(8,128)(2,1)} %get-tuple-element.120.h_ref.x_ref.g_ref.mine_ref.refs_0_, bf16[1024,768]{1,0:T(8,128)(2,1)} %cot_ref.9, f32[4,6,768]{2,1,0:T(8,128)} %reshape.227.mod_ref, f32[8,1024]{1,0:T(8,128)} %get-tuple-element.91.line_ref, f32[8,1024]{1,0:T(8,128)} %get-tuple-element.92.pos_ref), custom_call_target="tpu_custom_call" | custom-call | flops 1650000000 | bytes 4000000 | tf_op jit(solution)/shard_map/dispatch/pallas_call | solution.py:280
  49.4 27.9 %shared_main.1 = (f32[1024,768]{1,0:T(8,128)}, f32[1024,768]{1,0:T(8,128)}, bf16[1024,3072]{1,0:T(8,128)(2,1)}, bf16[1024,1536]{1,0:T(8,128)(2,1)}, bf16[1024,1536]{1,0:T(8,128)(2,1)}) custom-call(s32[5]{0:T(128)} %stack.41.where_ref, bf16[4,1024,768]{2,1,0:T(8,128)(2,1)} %get-tuple-element.120.h_ref.x_ref.g_ref.mine_ref.refs_0_, ...), custom_call_target="tpu_custom_call" | custom-call | flops 9663676416 | bytes 15000000 | tf_op jit(solution)/shard_map/shared_main/pallas_call | solution.py:328
  78.3 1.9 copy-done.2
  80.1 4.9 %all-to-all-start = ((bf16[4,2,256,768]{3,2,1,0:T(8,128)(2,1)}), bf16[4,2,256,768]{3,2,1,0:T(8,128)(2,1)}, u32[]{:S(2)}, u32[]{:S(2)}) async-start(bf16[4,2,256,768]{3,2,1,0:T(8,128)(2,1)} %dispatch.3), calls=%async_computation | async-start | bytes 6291456 | tf_op jit(solution)/shard_map/all_to_all | solution.py:927
  86.3 16.9 %expert_first.2 = (bf16[1024,3072]{1,0:T(8,128)(2,1)}, f32[1024,3072]{1,0:T(8,128)}, bf16[2,2,96,3072]{3,2,1,0:T(8,128)(2,1)}, bf16[2,2,96,3072]{3,2,1,0:T(8,128)(2,1)}) custom-call(s32[3]{0:T(128)} %pad_add_fusion.where_ref, bf16[4,2,256,768]{3,2,1,0:T(8,128)(2,1)} %copy-done.2, bf16[2,768,3072]{2,1,0:T(8,128)(2,1)} %w1_ref.9), custom_call_target="tpu_custom_call" | custom-call | flops 4831838208 | bytes 15000000 | tf_op jit(solution)/shard_map/expert_first/pallas_call | solution.py:382
  103.2 2.3 collective-permute-start
  105.5 22.3 %expert_second.2 = (bf16[4,2,256,768]{3,2,1,0:T(8,128)(2,1)}, bf16[1024,3072]{1,0:T(8,128)(2,1)}) custom-call(bf16[4,2,256,768]{3,2,1,0:T(8,128)(2,1)} %copy-done.2, bf16[1024,3072]{1,0:T(8,128)(2,1)} %get-tuple-element.100.act_ref, f32[1024,3072]{1,0:T(8,128)} %get-tuple-element.101.slope_ref, bf16[2,768,3072]{2,1,0:T(8,128)(2,1)} %w1_ref.9, ...), custom_call_target="tpu_custom_call" | custom-call | flops 7247757312 | bytes 20000000 | tf_op jit(solution)/shard_map/expert_second/pallas_call | solution.py:418
  127.8 4.0 all-to-all-start.2
  132.3 9.9 %weight_grad.2 = (bf16[2,2,96,3072]{3,2,1,0:T(8,128)(2,1)}, bf16[2,2,96,3072]{3,2,1,0:T(8,128)(2,1)}) custom-call(s32[3]{0:T(128)} %pad_add_fusion.where_ref, bf16[4,2,256,768]{3,2,1,0:T(8,128)(2,1)} %copy-done.2, bf16[1024,3072]{1,0:T(8,128)(2,1)} %get-tuple-element.104.b_ref), custom_call_target="tpu_custom_call" | custom-call | flops 2415919104 | bytes 6500000 | tf_op jit(solution)/shard_map/weight_grad/pallas_call | solution.py:462
  142.3 16.9 %expert_first.3 = (bf16[1024,3072]{1,0:T(8,128)(2,1)}, f32[1024,3072]{1,0:T(8,128)}, bf16[2,2,96,3072]{3,2,1,0:T(8,128)(2,1)}, bf16[2,2,96,3072]{3,2,1,0:T(8,128)(2,1)}) custom-call(s32[3]{0:T(128)} %pad_add_fusion.where_ref, bf16[4,2,256,768]{3,2,1,0:T(8,128)(2,1)} %all-to-all-done.rows_ref.a_ref, bf16[2,768,3072]{2,1,0:T(8,128)(2,1)} %w1_ref.9), custom_call_target="tpu_custom_call" | custom-call | flops 4831838208 | bytes 15000000 | tf_op jit(solution)/shard_map/expert_first/pallas_call | solution.py:382
  159.2 3.0 fusion
  162.2 2.2 collective-permute-start.1
  164.4 4.2 all-to-all-done.2.rest_0_
  168.7 23.4 %expert_second.3 = (bf16[4,2,256,768]{3,2,1,0:T(8,128)(2,1)}, bf16[1024,3072]{1,0:T(8,128)(2,1)}) custom-call(bf16[4,2,256,768]{3,2,1,0:T(8,128)(2,1)} %all-to-all-done.rows_ref.a_ref, bf16[1024,3072]{1,0:T(8,128)(2,1)} %get-tuple-element.111.act_ref, f32[1024,3072]{1,0:T(8,128)} %get-tuple-element.112.slope_ref, bf16[2,768,3072]{2,1,0:T(8,128)(2,1)} %w1_ref.9, ...), custom_call_target="tpu_custom_call" | custom-call | flops 7247757312 | bytes 20000000 | tf_op jit(solution)/shard_map/expert_second/pallas_call | solution.py:418
  192.1 4.2 all-to-all-start.3
  197.2 9.9 %weight_grad.3 = (bf16[2,2,96,3072]{3,2,1,0:T(8,128)(2,1)}, bf16[2,2,96,3072]{3,2,1,0:T(8,128)(2,1)}) custom-call(s32[3]{0:T(128)} %pad_add_fusion.where_ref, bf16[4,2,256,768]{3,2,1,0:T(8,128)(2,1)} %all-to-all-done.rows_ref.a_ref, bf16[1024,3072]{1,0:T(8,128)(2,1)} %get-tuple-element.115.b_ref), custom_call_target="tpu_custom_call" | custom-call | flops 2415919104 | bytes 6500000 | tf_op jit(solution)/shard_map/weight_grad/pallas_call | solution.py:462
  207.1 1.1 collective-permute-done.2
  208.2 1.8 collective-permute-start.8
  210.0 3.1 fusion.1
  213.1 1.6 collective-permute-start.7
  214.8 2.5 fusion.15
  217.8 2.5 collective-permute-start.6
  220.3 20.8 %shared_grad.1 = (bf16[2,2,2,2,96,768]{5,4,3,2,1,0:T(8,128)(2,1)}, bf16[2,2,2,2,96,768]{5,4,3,2,1,0:T(8,128)(2,1)}) custom-call(s32[5]{0:T(128)} %stack.41.where_ref, bf16[4,1024,768]{2,1,0:T(8,128)(2,1)} %get-tuple-element.120.h_ref.x_ref.g_ref.mine_ref.refs_0_, bf16[4,1024,768]{2,1,0:T(8,128)(2,1)} %collective-permute-done.3.peer_ref.refs_1_, ...), custom_call_target="tpu_custom_call" | custom-call | flops 4831838208 | bytes 12500000 | tf_op jit(solution)/shard_map/shared_grad/pallas_call | solution.py:531
  241.1 1.6 collective-permute-start.9
  242.8 1.7 copy-done.1
  244.4 29.8 %backward.2 = (bf16[1024,768]{1,0:T(8,128)(2,1)}, f32[1024,768]{1,0:T(8,128)}, f32[4,8,768]{2,1,0:T(8,128)}, bf16[512,1664]{1,0:T(8,128)(2,1)}, bf16[512,1664]{1,0:T(8,128)(2,1)}) custom-call(s32[4]{0:T(128)} %len_ref.7, s32[5]{0:T(128)} %stack.41.where_ref, bf16[1024,768]{1,0:T(8,128)(2,1)} %tok_ref.3, bf16[1024,768]{1,0:T(8,128)(2,1)} %cot_ref.9, ...), custom_call_target="tpu_custom_call" | custom-call | flops 5000000000 | bytes 7000000 | tf_op jit(solution)/shard_map/backward/pallas_call | solution.py:676
  274.3 2.0 fusion.2
  276.8 2.5 fusion.14
  279.4 30.1 %backward.3 = (bf16[1024,768]{1,0:T(8,128)(2,1)}, f32[1024,768]{1,0:T(8,128)}, f32[4,8,768]{2,1,0:T(8,128)}, bf16[512,1664]{1,0:T(8,128)(2,1)}, bf16[512,1664]{1,0:T(8,128)(2,1)}) custom-call(s32[4]{0:T(128)} %len_ref.7, s32[5]{0:T(128)} %stack.41.where_ref, ...), custom_call_target="tpu_custom_call", output_to_operand_aliasing={{0}: (16, {}), {1}: (17, {}), {2}: (18, {})} | custom-call | flops 5000000000 | bytes 7000000 | tf_op jit(solution)/shard_map/backward/pallas_call | solution.py:676
  309.5 2.6 collective-permute-done.11
  312.6 1.9 fusion.6
  314.9 2.7 fusion.13
  317.6 2.2 collective-permute-start.14
  319.8 2.7 fusion.4
  322.6 1.6 collective-permute-start.12
  324.2 2.6 fusion.3
  326.8 1.5 collective-permute-start.10
  328.4 14.2 %tail_grad.1 = (bf16[2,2,2,96,768]{4,3,2,1,0:T(8,128)(2,1)}, bf16[2,2,2,96,768]{4,3,2,1,0:T(8,128)(2,1)}, bf16[768,128]{1,0:T(8,128)(2,1)}) custom-call(s32[5]{0:T(128)} %stack.41.where_ref, bf16[4,1024,768]{2,1,0:T(8,128)(2,1)} %get-tuple-element.120.h_ref.x_ref.g_ref.mine_ref.refs_0_, bf16[4,1024,768]{2,1,0:T(8,128)(2,1)} %collective-permute-done.3.peer_ref.refs_1_, ...), custom_call_target="tpu_custom_call" | custom-call | flops 2500000000 | bytes 10000000 | tf_op jit(solution)/shard_map/tail_grad/pallas_call | solution.py:766
  342.5 1.4 collective-permute-start.18
  343.9 2.5 collective-permute-done.14
  346.4 1.9 fusion.5
  348.4 13.6 %collective-permute-done.12 = bf16[2,96,3072]{2,1,0:T(8,128)(2,1)} collective-permute-done((bf16[2,96,3072]{2,1,0:T(8,128)(2,1)}, bf16[2,96,3072]{2,1,0:T(8,128)(2,1)}, u32[]{:S(2)}, u32[]{:S(2)}) %collective-permute-start.12) | collective-permute-done | bytes 1179680 | tf_op jit(solution)/shard_map/ppermute | solution.py:817
  362.0 2.3 fusion.12
  364.9 2.4 fusion.11
  367.4 2.5 collective-permute-start.21
  370.2 2.0 copy.79
  373.7 3.7 all-to-all-start.4
  377.5 1.2 fusion.17
  378.7 1.9 collective-permute-start.19
  380.6 17.7 %collective-permute-done.21 = bf16[2,2,96,768]{3,2,1,0:T(8,128)(2,1)} collective-permute-done((bf16[2,2,96,768]{3,2,1,0:T(8,128)(2,1)}, bf16[2,2,96,768]{3,2,1,0:T(8,128)(2,1)}, u32[]{:S(2)}, u32[]{:S(2)}) %collective-permute-start.21) | collective-permute-done | bytes 589856 | tf_op jit(solution)/shard_map/ppermute | solution.py:817
  398.3 2.1 fusion.20
  400.4 3.0 fusion.8
  403.4 1.1 fusion.19
  404.5 2.4 collective-permute-start.22
  406.9 1.6 pad_maximum_fusion
  408.5 6.6 %collective-permute-done.22 = bf16[2,96,768]{2,1,0:T(8,128)(2,1)S(1)} collective-permute-done((bf16[2,96,768]{2,1,0:T(8,128)(2,1)S(1)}, bf16[2,96,768]{2,1,0:T(8,128)(2,1)S(1)}, u32[]{:S(2)}, u32[]{:S(2)}) %collective-permute-start.22) | collective-permute-done | bytes 294944 | tf_op jit(solution)/shard_map/ppermute | solution.py:817
  415.1 1.6 fusion.27
  417.0 1.4 fusion.18
  421.9 1.9 collective-permute-done.23
  (85 shorter events, 15.9 us)
Async XLA Ops:
  36.9 41.4 %all-to-all-start.1 = ((bf16[4,2,256,768]{3,2,1,0:T(8,128)(2,1)}), bf16[4,2,256,768]{3,2,1,0:T(8,128)(2,1)S(1)}, u32[]{:S(2)}, u32[]{:S(2)}) async-start(bf16[4,2,256,768]{3,2,1,0:T(8,128)(2,1)} %dispatch.2), calls=%async_computation.1 | async-start | bytes 6291456 | tf_op jit(solution)/shard_map/all_to_all | solution.py:927
  78.3 1.9 copy-start.2
  80.1 47.7 %all-to-all-start = ((bf16[4,2,256,768]{3,2,1,0:T(8,128)(2,1)}), bf16[4,2,256,768]{3,2,1,0:T(8,128)(2,1)}, u32[]{:S(2)}, u32[]{:S(2)}) async-start(bf16[4,2,256,768]{3,2,1,0:T(8,128)(2,1)} %dispatch.3), calls=%async_computation | async-start | bytes 6291456 | tf_op jit(solution)/shard_map/all_to_all | solution.py:927
  85.1 135.2 %collective-permute-start.3 = (bf16[4,1024,768]{2,1,0:T(8,128)(2,1)}, bf16[4,1024,768]{2,1,0:T(8,128)(2,1)}, u32[]{:S(2)}, u32[]{:S(2)}) collective-permute-start(bf16[4,1024,768]{2,1,0:T(8,128)(2,1)} %get-tuple-element.120.h_ref.x_ref.g_ref.mine_ref.refs_0_), channel_id=1, source_target_pairs={{0,1},{1,0},{2,3},{3,2},{4,5},{5,4},{6,7},{7,6},{8,9},{9,8},{10,11... | collective-permute-start | bytes 18874376 | tf_op jit(solution)/shard_map/ppermute | solution.py:817
  85.6 132.1 %collective-permute-start.5 = (bf16[1024,3072]{1,0:T(8,128)(2,1)}, bf16[1024,3072]{1,0:T(8,128)(2,1)}, u32[]{:S(2)}, u32[]{:S(2)}) collective-permute-start(bf16[1024,3072]{1,0:T(8,128)(2,1)} %get-tuple-element.123.act_ref), channel_id=1, source_target_pairs={{0,1},{1,0},{2,3},{3,2},{4,5},{5,4},{6,7},{7,6},{8,9},{9,8},{10,11... | collective-permute-start | bytes 18874376 | tf_op jit(solution)/shard_map/ppermute | solution.py:817
  103.2 56.0 %collective-permute-start = (bf16[2,2,96,3072]{3,2,1,0:T(8,128)(2,1)}, bf16[2,2,96,3072]{3,2,1,0:T(8,128)(2,1)}, u32[]{:S(2)}, u32[]{:S(2)}) collective-permute-start(bf16[2,2,96,3072]{3,2,1,0:T(8,128)(2,1)} %get-tuple-element.108), channel_id=1, source_target_pairs={{0,4},{4,0},{8,12},{12,8},{16,20},{20,16},{24,28},{28,24},{1,5},{5... | collective-permute-start | bytes 7077896 | tf_op jit(solution)/shard_map/ppermute | solution.py:817
  127.8 40.9 %all-to-all-start.2 = ((bf16[4,2,256,768]{3,2,1,0:T(8,128)(2,1)}), bf16[4,2,256,768]{3,2,1,0:T(8,128)(2,1)S(1)}, u32[]{:S(2)}, u32[]{:S(2)}) async-start(bf16[4,2,256,768]{3,2,1,0:T(8,128)(2,1)} %get-tuple-element.102), calls=%async_computation.2 | async-start | bytes 6291456 | tf_op jit(solution)/shard_map/all_to_all | solution.py:943
  131.8 85.4 %collective-permute-start.4 = (bf16[1024,1536]{1,0:T(8,128)(2,1)}, bf16[1024,1536]{1,0:T(8,128)(2,1)}, u32[]{:S(2)}, u32[]{:S(2)}) collective-permute-start(bf16[1024,1536]{1,0:T(8,128)(2,1)} %get-tuple-element.122), channel_id=1, source_target_pairs={{0,1},{1,0},{2,3},{3,2},{4,5},{5,4},{6,7},{7,6},{8,9},{9,8},{10,11... | collective-permute-start | bytes 9437192 | tf_op jit(solution)/shard_map/ppermute | solution.py:817
  142.2 66.0 %collective-permute-start.2 = (bf16[2,2,96,3072]{3,2,1,0:T(8,128)(2,1)}, bf16[2,2,96,3072]{3,2,1,0:T(8,128)(2,1)}, u32[]{:S(2)}, u32[]{:S(2)}) collective-permute-start(bf16[2,2,96,3072]{3,2,1,0:T(8,128)(2,1)} %get-tuple-element.118), channel_id=1, source_target_pairs={{0,4},{4,0},{8,12},{12,8},{16,20},{20,16},{24,28},{28,24},{1,5},{5... | collective-permute-start | bytes 7077896 | tf_op jit(solution)/shard_map/ppermute | solution.py:817
  162.2 50.9 %collective-permute-start.1 = (bf16[2,96,3072]{2,1,0:T(8,128)(2,1)}, bf16[2,96,3072]{2,1,0:T(8,128)(2,1)}, u32[]{:S(2)}, u32[]{:S(2)}) collective-permute-start(bf16[2,96,3072]{2,1,0:T(8,128)(2,1)} %fusion), channel_id=1, source_target_pairs={{0,8},{4,12},{8,0},{12,4},{16,24},{20,28},{24,16},{28,20},{1,9},{5... | collective-permute-start | bytes 3538952 | tf_op jit(solution)/shard_map/ppermute | solution.py:817
  168.7 23.4 %copy-start = (bf16[4,2,256,768]{3,2,1,0:T(8,128)(2,1)}, bf16[4,2,256,768]{3,2,1,0:T(8,128)(2,1)S(1)}, u32[]{:S(2)}) copy-start(bf16[4,2,256,768]{3,2,1,0:T(8,128)(2,1)S(1)} %all-to-all-done.2.rest_0_) | copy-start | bytes 9437188
  192.1 4.3 %copy-start.9 = (bf16[4,768]{1,0:T(4,128)(2,1)S(1)}, bf16[4,768]{1,0:T(4,128)(2,1)}, u32[]{:S(2)}) copy-start(bf16[4,768]{1,0:T(4,128)(2,1)} %param.14) | copy-start | bytes 18436
  192.1 4.4 %copy-start.8 = (bf16[768,8]{0,1:T(8,128)(2,1)S(1)}, bf16[768,8]{0,1:T(8,128)(2,1)}, u32[]{:S(2)}) copy-start(bf16[768,8]{0,1:T(8,128)(2,1)} %param.21) | copy-start | bytes 36868
  192.1 50.6 %all-to-all-start.3 = ((bf16[4,2,256,768]{3,2,1,0:T(8,128)(2,1)}), bf16[4,2,256,768]{3,2,1,0:T(8,128)(2,1)S(1)}, u32[]{:S(2)}, u32[]{:S(2)}) async-start(bf16[4,2,256,768]{3,2,1,0:T(8,128)(2,1)} %get-tuple-element.113), calls=%async_computation.3 | async-start | bytes 6291456 | tf_op jit(solution)/shard_map/all_to_all | solution.py:943
  208.2 66.0 %collective-permute-start.8 = (bf16[2,2,96,3072]{3,2,1,0:T(8,128)(2,1)}, bf16[2,2,96,3072]{3,2,1,0:T(8,128)(2,1)}, u32[]{:S(2)}, u32[]{:S(2)}) collective-permute-start(bf16[2,2,96,3072]{3,2,1,0:T(8,128)(2,1)} %get-tuple-element.135), channel_id=1, source_target_pairs={{0,4},{4,0},{8,12},{12,8},{16,20},{20,16},{24,28},{28,24},{1,5},{5... | collective-permute-start | bytes 7077896 | tf_op jit(solution)/shard_map/ppermute | solution.py:817
  213.1 61.2 %collective-permute-start.7 = (bf16[2,96,3072]{2,1,0:T(8,128)(2,1)}, bf16[2,96,3072]{2,1,0:T(8,128)(2,1)}, u32[]{:S(2)}, u32[]{:S(2)}) collective-permute-start(bf16[2,96,3072]{2,1,0:T(8,128)(2,1)} %fusion.1), channel_id=1, source_target_pairs={{0,8},{4,12},{8,0},{12,4},{16,24},{20,28},{24,16},{28,20},{1,9},{5... | collective-permute-start | bytes 3538952 | tf_op jit(solution)/shard_map/ppermute | solution.py:817
  217.2 94.9 %collective-permute-start.11 = (bf16[2,2,96,3072]{3,2,1,0:T(8,128)(2,1)}, bf16[2,2,96,3072]{3,2,1,0:T(8,128)(2,1)}, u32[]{:S(2)}, u32[]{:S(2)}) collective-permute-start(bf16[2,2,96,3072]{3,2,1,0:T(8,128)(2,1)} %get-tuple-element.145), channel_id=1, source_target_pairs={{0,4},{4,0},{8,12},{12,8},{16,20},{20,16},{24,28},{28,24},{1,5},{5... | collective-permute-start | bytes 7077896 | tf_op jit(solution)/shard_map/ppermute | solution.py:817
  217.8 56.5 %collective-permute-start.6 = (bf16[96,3072]{1,0:T(8,128)(2,1)}, bf16[96,3072]{1,0:T(8,128)(2,1)}, u32[]{:S(2)}, u32[]{:S(2)}) collective-permute-start(bf16[96,3072]{1,0:T(8,128)(2,1)} %fusion.15), channel_id=1, source_target_pairs={{0,16},{4,20},{8,24},{12,28},{16,0},{20,4},{24,8},{28,12},{1,17},{... | collective-permute-start | bytes 1769480 | tf_op jit(solution)/shard_map/ppermute | solution.py:817
  241.1 83.1 %collective-permute-start.9 = (bf16[2,2,2,2,96,768]{5,4,3,2,1,0:T(8,128)(2,1)}, bf16[2,2,2,2,96,768]{5,4,3,2,1,0:T(8,128)(2,1)}, u32[]{:S(2)}, u32[]{:S(2)}) collective-permute-start(bf16[2,2,2,2,96,768]{5,4,3,2,1,0:T(8,128)(2,1)} %get-tuple-element.143), channel_id=1, source_target_pairs={{0,2},{1,3},{2,0},{3,1},{4,6},{5,7},{6,4},{7,5},{8,10},{9,11},{10,... | collective-permute-start | bytes 7077896 | tf_op jit(solution)/shard_map/ppermute | solution.py:817
  242.8 1.7 copy-start.1
  276.3 38.6 %collective-permute-start.13 = (bf16[2,96,3072]{2,1,0:T(8,128)(2,1)S(1)}, bf16[2,96,3072]{2,1,0:T(8,128)(2,1)}, u32[]{:S(2)}, u32[]{:S(2)}) collective-permute-start(bf16[2,96,3072]{2,1,0:T(8,128)(2,1)S(1)} %fusion.2), channel_id=1, source_target_pairs={{0,8},{4,12},{8,0},{12,4},{16,24},{20,28},{24,16},{28,20},{1,9},{5... | collective-permute-start | bytes 3538952 | tf_op jit(solution)/shard_map/ppermute | solution.py:817
  279.3 43.3 %collective-permute-start.15 = (bf16[96,3072]{1,0:T(8,128)(2,1)}, bf16[96,3072]{1,0:T(8,128)(2,1)}, u32[]{:S(2)}, u32[]{:S(2)}) collective-permute-start(bf16[96,3072]{1,0:T(8,128)(2,1)} %fusion.14), channel_id=1, source_target_pairs={{0,16},{4,20},{8,24},{12,28},{16,0},{20,4},{24,8},{28,12},{1,17},{... | collective-permute-start | bytes 1769480 | tf_op jit(solution)/shard_map/ppermute | solution.py:817
  312.1 16.2 %collective-permute-start.17 = (bf16[512,1664]{1,0:T(8,128)(2,1)}, bf16[512,1664]{1,0:T(8,128)(2,1)}, u32[]{:S(2)}, u32[]{:S(2)}) collective-permute-start(bf16[512,1664]{1,0:T(8,128)(2,1)} %get-tuple-element.153), channel_id=1, source_target_pairs={{0,1},{1,0},{2,3},{3,2},{4,5},{5,4},{6,7},{7,6},{8,9},{9,8},{10,11... | collective-permute-start | bytes 5111816 | tf_op jit(solution)/shard_map/ppermute | solution.py:817
  312.1 16.2 %collective-permute-start.16 = (bf16[512,1664]{1,0:T(8,128)(2,1)}, bf16[512,1664]{1,0:T(8,128)(2,1)}, u32[]{:S(2)}, u32[]{:S(2)}) collective-permute-start(bf16[512,1664]{1,0:T(8,128)(2,1)} %get-tuple-element.152), channel_id=1, source_target_pairs={{0,1},{1,0},{2,3},{3,2},{4,5},{5,4},{6,7},{7,6},{8,9},{9,8},{10,11... | collective-permute-start | bytes 5111816 | tf_op jit(solution)/shard_map/ppermute | solution.py:817
  314.5 5.3 %copy-start.3 = (bf16[2,2,96,3072]{3,2,1,0:T(8,128)(2,1)S(1)}, bf16[2,2,96,3072]{3,2,1,0:T(8,128)(2,1)}, u32[]{:S(2)}) copy-start(bf16[2,2,96,3072]{3,2,1,0:T(8,128)(2,1)} %get-tuple-element.116) | copy-start | bytes 7077892
  317.6 28.8 %collective-permute-start.14 = (bf16[96,3072]{1,0:T(8,128)(2,1)}, bf16[96,3072]{1,0:T(8,128)(2,1)}, u32[]{:S(2)}, u32[]{:S(2)}) collective-permute-start(bf16[96,3072]{1,0:T(8,128)(2,1)} %fusion.13), channel_id=1, source_target_pairs={{0,16},{4,20},{8,24},{12,28},{16,0},{20,4},{24,8},{28,12},{1,17},{... | collective-permute-start | bytes 1769480 | tf_op jit(solution)/shard_map/ppermute | solution.py:817
  322.5 1.7 copy-start.4
  322.6 39.4 %collective-permute-start.12 = (bf16[2,96,3072]{2,1,0:T(8,128)(2,1)}, bf16[2,96,3072]{2,1,0:T(8,128)(2,1)}, u32[]{:S(2)}, u32[]{:S(2)}) collective-permute-start(bf16[2,96,3072]{2,1,0:T(8,128)(2,1)} %fusion.4), channel_id=1, source_target_pairs={{0,8},{4,12},{8,0},{12,4},{16,24},{20,28},{24,16},{28,20},{1,9},{5... | collective-permute-start | bytes 3538952 | tf_op jit(solution)/shard_map/ppermute | solution.py:817
  326.8 38.1 %collective-permute-start.10 = (bf16[2,2,2,96,768]{4,3,2,1,0:T(8,128)(2,1)}, bf16[2,2,2,96,768]{4,3,2,1,0:T(8,128)(2,1)}, u32[]{:S(2)}, u32[]{:S(2)}) collective-permute-start(bf16[2,2,2,96,768]{4,3,2,1,0:T(8,128)(2,1)} %fusion.3), channel_id=1, source_target_pairs={{0,4},{4,0},{8,12},{12,8},{16,20},{20,16},{24,28},{28,24},{1,5},{5... | collective-permute-start | bytes 3538952 | tf_op jit(solution)/shard_map/ppermute | solution.py:817
  342.5 34.9 %collective-permute-start.18 = (bf16[2,2,2,96,768]{4,3,2,1,0:T(8,128)(2,1)}, bf16[2,2,2,96,768]{4,3,2,1,0:T(8,128)(2,1)}, u32[]{:S(2)}, u32[]{:S(2)}) collective-permute-start(bf16[2,2,2,96,768]{4,3,2,1,0:T(8,128)(2,1)} %get-tuple-element.161), channel_id=1, source_target_pairs={{0,2},{1,3},{2,0},{3,1},{4,6},{5,7},{6,4},{7,5},{8,10},{9,11},{10,... | collective-permute-start | bytes 3538952 | tf_op jit(solution)/shard_map/ppermute | solution.py:817
  364.3 36.1 %collective-permute-start.20 = (bf16[96,3072]{1,0:T(8,128)(2,1)}, bf16[96,3072]{1,0:T(8,128)(2,1)}, u32[]{:S(2)}, u32[]{:S(2)}) collective-permute-start(bf16[96,3072]{1,0:T(8,128)(2,1)} %fusion.12), channel_id=1, source_target_pairs={{0,16},{4,20},{8,24},{12,28},{16,0},{20,4},{24,8},{28,12},{1,17},{... | collective-permute-start | bytes 1769480 | tf_op jit(solution)/shard_map/ppermute | solution.py:817
  367.4 30.9 %collective-permute-start.21 = (bf16[2,2,96,768]{3,2,1,0:T(8,128)(2,1)}, bf16[2,2,96,768]{3,2,1,0:T(8,128)(2,1)}, u32[]{:S(2)}, u32[]{:S(2)}) collective-permute-start(bf16[2,2,96,768]{3,2,1,0:T(8,128)(2,1)} %fusion.11), channel_id=1, source_target_pairs={{0,8},{4,12},{8,0},{12,4},{16,24},{20,28},{24,16},{28,20},{1,9},{5... | collective-permute-start | bytes 1769480 | tf_op jit(solution)/shard_map/ppermute | solution.py:817
  370.1 2.0 copy-start.6
  370.2 2.0 copy-start.7
  372.1 5.3 %copy-start.5 = (bf16[2,2,2,96,768]{4,3,2,1,0:T(8,128)(2,1)S(1)}, bf16[2,2,2,96,768]{4,3,2,1,0:T(8,128)(2,1)}, u32[]{:S(2)}) copy-start(bf16[2,2,2,96,768]{4,3,2,1,0:T(8,128)(2,1)} %get-tuple-element.154) | copy-start | bytes 3538948
  373.7 43.2 %all-to-all-start.4 = ((bf16[32,4,1408]{2,1,0:T(4,128)(2,1)}), bf16[32,4,1408]{2,1,0:T(4,128)(2,1)S(1)}, u32[]{:S(2)}, u32[]{:S(2)}) async-start(bf16[32,4,1408]{2,1,0:T(4,128)(2,1)} %bitcast.26), calls=%async_computation.4 | async-start | bytes 720896 | tf_op jit(solution)/shard_map/all_to_all | solution.py:888
  378.7 24.8 %collective-permute-start.19 = (bf16[2,2,96,768]{3,2,1,0:T(8,128)(2,1)S(1)}, bf16[2,2,96,768]{3,2,1,0:T(8,128)(2,1)S(1)}, u32[]{:S(2)}, u32[]{:S(2)}) collective-permute-start(bf16[2,2,96,768]{3,2,1,0:T(8,128)(2,1)S(1)} %fusion.17), channel_id=1, source_target_pairs={{0,4},{4,0},{8,12},{12,8},{16,20},{20,16},{24,28},{28,24},{1,5},{5... | collective-permute-start | bytes 1769480 | tf_op jit(solution)/shard_map/ppermute | solution.py:817
  400.4 16.6 %collective-permute-start.24 = (bf16[2,96,768]{2,1,0:T(8,128)(2,1)}, bf16[2,96,768]{2,1,0:T(8,128)(2,1)S(1)}, u32[]{:S(2)}, u32[]{:S(2)}) collective-permute-start(bf16[2,96,768]{2,1,0:T(8,128)(2,1)} %fusion.20), channel_id=1, source_target_pairs={{0,16},{4,20},{8,24},{12,28},{16,0},{20,4},{24,8},{28,12},{1,17},{... | collective-permute-start | bytes 884744 | tf_op jit(solution)/shard_map/ppermute | solution.py:817
  404.5 10.6 %collective-permute-start.22 = (bf16[2,96,768]{2,1,0:T(8,128)(2,1)S(1)}, bf16[2,96,768]{2,1,0:T(8,128)(2,1)S(1)}, u32[]{:S(2)}, u32[]{:S(2)}) collective-permute-start(bf16[2,96,768]{2,1,0:T(8,128)(2,1)S(1)} %fusion.19), channel_id=1, source_target_pairs={{0,8},{4,12},{8,0},{12,4},{16,24},{20,28},{24,16},{28,20},{1,9},{5... | collective-permute-start | bytes 884744 | tf_op jit(solution)/shard_map/ppermute | solution.py:817
  416.7 7.1 %collective-permute-start.23 = (bf16[96,768]{1,0:T(8,128)(2,1)}, bf16[96,768]{1,0:T(8,128)(2,1)}, u32[]{:S(2)}, u32[]{:S(2)}) collective-permute-start(bf16[96,768]{1,0:T(8,128)(2,1)} %fusion.27), channel_id=1, source_target_pairs={{0,16},{4,20},{8,24},{12,28},{16,0},{20,4},{24,8},{28,12},{1,17},{... | collective-permute-start | bytes 442376 | tf_op jit(solution)/shard_map/ppermute | solution.py:817

commit v6 on v5

--- a/solution.py
+++ b/solution.py
@@ -29,7 +29,7 @@
 F32 = jnp.float32
 BF16 = jnp.bfloat16
 VMEM_LIMIT = 60 * 1024 * 1024
-COST = 0.5
+COST = 0.75
 
 
 def dot_nn(a, b):

time: 433 us -> 429 us (level)
  waiting for transfers between devices: 51.7 us -> 47.3 us
  transfers between devices with their start and end apart: 30 -> 30, of which waited for: 10 -> 9; matrix products, arithmetic and copies ran while one was open for 12% -> 12% of each run, Pallas kernels for 54% -> 54%
where the time goes in v6:
time: 429 us; the launch traced here: 423 us
  Pallas kernels  261 us (61%)
  starting transfers between devices  50.2 us (12%)
  waiting for transfers between devices  47.3 us (11%)
  other arithmetic  45.9 us (11%)
  local copies, waits for them, and re-layouts  12 us (3%)
  matrix products  5.04 us (1%)
    pallas_call x2, Pallas kernels, backward(): pl.pallas_call(functools.partial(backward_kernel, local, fast, first_item...  60 us
    pallas_call x2, Pallas kernels, expert_second(): pl.pallas_call(expert_second_kernel, name='expert_second', grid=(rows.sha...  45.6 us
    ppermute x25, waiting for transfers between devices, swap(): lax.ppermute(value.astype(BF16), axis, [(i, i ^ bit) for i in range(size)])  42.9 us
    pallas_call x2, Pallas kernels, expert_first(): pl.pallas_call(functools.partial(expert_first_kernel, fast), name='expert...  33.9 us
    convert_element_type x14, other arithmetic, step(): self.send = self.total().astype(BF16)  32.4 us
    pallas_call x1, Pallas kernels, shared_main(): pl.pallas_call(functools.partial(shared_main_kernel, halved), name='share...  27.9 us
    ppermute x25, starting transfers between devices, swap(): lax.ppermute(value.astype(BF16), axis, [(i, i ^ bit) for i in range(size)])  27.7 us
    pallas_call x1, Pallas kernels, shared_grad(): pl.pallas_call(shared_grad_kernel, name='shared_grad', grid_spec=pltpu.Pr...  20.8 us
  transfers between devices with their start and end apart: 30, of which 9 were waited for; matrix products, arithmetic and copies ran while one was open for 12% of the time, Pallas kernels for 54%

profile of v6, /device:TPU:0, one launch (start us, length us, event | category | flops | bytes accessed | tf_op | source)
XLA Modules:
  0.0 423.1 jit_solution(6081064967532971689)
XLA Ops:
  0.6 4.0 fusion.33
  5.4 20.8 %attn_forward.1 = (bf16[1024,2304]{1,0:T(8,128)(2,1)}, f32[1024,128]{1,0:T(8,128)}, f32[1024,768]{1,0:T(8,128)}, bf16[4,1024,768]{2,1,0:T(8,128)(2,1)}) custom-call(s32[4]{0:T(128)} %len_ref.7, bf16[1024,768]{1,0:T(8,128)(2,1)} %tok_ref.3, bf16[1024,768]{1,0:T(8,128)(2,1)} %cot_ref.9, f32[4,6,768]{2,1,0:T(8,128)} %reshape.227.mod_ref, ...), custom_call_target="tpu_custom_call" | custom-call | flops 6074999808 | bytes 18000000 | tf_op jit(solution)/shard_map/attn_forward/pallas_call | solution.py:158
  26.2 3.3 route.1
  29.4 7.4 %dispatch.2 = bf16[4,2,256,768]{3,2,1,0:T(8,128)(2,1)} custom-call(bf16[4,1024,768]{2,1,0:T(8,128)(2,1)} %get-tuple-element.120.h_ref.x_ref.g_ref.mine_ref.refs_0_, bf16[1024,768]{1,0:T(8,128)(2,1)} %cot_ref.9, f32[4,6,768]{2,1,0:T(8,128)} %reshape.227.mod_ref, f32[8,1024]{1,0:T(8,128)} %get-tuple-element.91.line_ref, f32[8,1024]{1,0:T(8,128)} %get-tuple-element.92.pos_ref), custom_call_target="tpu_custom_call" | custom-call | flops 2475000064 | bytes 6000000 | tf_op jit(solution)/shard_map/dispatch/pallas_call | solution.py:280
  36.8 4.4 %all-to-all-start.1 = ((bf16[4,2,256,768]{3,2,1,0:T(8,128)(2,1)}), bf16[4,2,256,768]{3,2,1,0:T(8,128)(2,1)S(1)}, u32[]{:S(2)}, u32[]{:S(2)}) async-start(bf16[4,2,256,768]{3,2,1,0:T(8,128)(2,1)} %dispatch.2), calls=%async_computation.1 | async-start | bytes 6291456 | tf_op jit(solution)/shard_map/all_to_all | solution.py:927
  41.3 7.4 %dispatch.3 = bf16[4,2,256,768]{3,2,1,0:T(8,128)(2,1)} custom-call(bf16[4,1024,768]{2,1,0:T(8,128)(2,1)} %get-tuple-element.120.h_ref.x_ref.g_ref.mine_ref.refs_0_, bf16[1024,768]{1,0:T(8,128)(2,1)} %cot_ref.9, f32[4,6,768]{2,1,0:T(8,128)} %reshape.227.mod_ref, f32[8,1024]{1,0:T(8,128)} %get-tuple-element.91.line_ref, f32[8,1024]{1,0:T(8,128)} %get-tuple-element.92.pos_ref), custom_call_target="tpu_custom_call" | custom-call | flops 2475000064 | bytes 6000000 | tf_op jit(solution)/shard_map/dispatch/pallas_call | solution.py:280
  49.4 27.9 %shared_main.1 = (f32[1024,768]{1,0:T(8,128)}, f32[1024,768]{1,0:T(8,128)}, bf16[1024,3072]{1,0:T(8,128)(2,1)}, bf16[1024,1536]{1,0:T(8,128)(2,1)}, bf16[1024,1536]{1,0:T(8,128)(2,1)}) custom-call(s32[5]{0:T(128)} %stack.41.where_ref, bf16[4,1024,768]{2,1,0:T(8,128)(2,1)} %get-tuple-element.120.h_ref.x_ref.g_ref.mine_ref.refs_0_, ...), custom_call_target="tpu_custom_call" | custom-call | flops 14495514624 | bytes 22500000 | tf_op jit(solution)/shard_map/shared_main/pallas_call | solution.py:328
  77.3 1.0 all-to-all-done.1.rows_ref.a_ref
  78.3 1.9 copy-done.2
  80.1 4.9 %all-to-all-start = ((bf16[4,2,256,768]{3,2,1,0:T(8,128)(2,1)}), bf16[4,2,256,768]{3,2,1,0:T(8,128)(2,1)}, u32[]{:S(2)}, u32[]{:S(2)}) async-start(bf16[4,2,256,768]{3,2,1,0:T(8,128)(2,1)} %dispatch.3), calls=%async_computation | async-start | bytes 6291456 | tf_op jit(solution)/shard_map/all_to_all | solution.py:927
  86.3 16.9 %expert_first.2 = (bf16[1024,3072]{1,0:T(8,128)(2,1)}, f32[1024,3072]{1,0:T(8,128)}, bf16[2,2,96,3072]{3,2,1,0:T(8,128)(2,1)}, bf16[2,2,96,3072]{3,2,1,0:T(8,128)(2,1)}) custom-call(s32[3]{0:T(128)} %pad_add_fusion.where_ref, bf16[4,2,256,768]{3,2,1,0:T(8,128)(2,1)} %copy-done.2, bf16[2,768,3072]{2,1,0:T(8,128)(2,1)} %w1_ref.9), custom_call_target="tpu_custom_call" | custom-call | flops 7247757312 | bytes 22500000 | tf_op jit(solution)/shard_map/expert_first/pallas_call | solution.py:382
  103.2 2.3 collective-permute-start
  105.5 22.2 %expert_second.2 = (bf16[4,2,256,768]{3,2,1,0:T(8,128)(2,1)}, bf16[1024,3072]{1,0:T(8,128)(2,1)}) custom-call(bf16[4,2,256,768]{3,2,1,0:T(8,128)(2,1)} %copy-done.2, bf16[1024,3072]{1,0:T(8,128)(2,1)} %get-tuple-element.100.act_ref, f32[1024,3072]{1,0:T(8,128)} %get-tuple-element.101.slope_ref, bf16[2,768,3072]{2,1,0:T(8,128)(2,1)} %w1_ref.9, ...), custom_call_target="tpu_custom_call" | custom-call | flops 10871635968 | bytes 30000000 | tf_op jit(solution)/shard_map/expert_second/pallas_call | solution.py:418
  127.8 4.0 all-to-all-start.2
  133.2 10.0 %weight_grad.2 = (bf16[2,2,96,3072]{3,2,1,0:T(8,128)(2,1)}, bf16[2,2,96,3072]{3,2,1,0:T(8,128)(2,1)}) custom-call(s32[3]{0:T(128)} %pad_add_fusion.where_ref, bf16[4,2,256,768]{3,2,1,0:T(8,128)(2,1)} %copy-done.2, bf16[1024,3072]{1,0:T(8,128)(2,1)} %get-tuple-element.104.b_ref), custom_call_target="tpu_custom_call" | custom-call | flops 3623878656 | bytes 9750000 | tf_op jit(solution)/shard_map/weight_grad/pallas_call | solution.py:462
  143.2 17.0 %expert_first.3 = (bf16[1024,3072]{1,0:T(8,128)(2,1)}, f32[1024,3072]{1,0:T(8,128)}, bf16[2,2,96,3072]{3,2,1,0:T(8,128)(2,1)}, bf16[2,2,96,3072]{3,2,1,0:T(8,128)(2,1)}) custom-call(s32[3]{0:T(128)} %pad_add_fusion.where_ref, bf16[4,2,256,768]{3,2,1,0:T(8,128)(2,1)} %all-to-all-done.rows_ref.a_ref, bf16[2,768,3072]{2,1,0:T(8,128)(2,1)} %w1_ref.9), custom_call_target="tpu_custom_call" | custom-call | flops 7247757312 | bytes 22500000 | tf_op jit(solution)/shard_map/expert_first/pallas_call | solution.py:382
  160.2 3.0 fusion
  163.2 2.1 collective-permute-start.1
  165.3 3.4 all-to-all-done.2.rest_0_
  168.7 23.4 %expert_second.3 = (bf16[4,2,256,768]{3,2,1,0:T(8,128)(2,1)}, bf16[1024,3072]{1,0:T(8,128)(2,1)}) custom-call(bf16[4,2,256,768]{3,2,1,0:T(8,128)(2,1)} %all-to-all-done.rows_ref.a_ref, bf16[1024,3072]{1,0:T(8,128)(2,1)} %get-tuple-element.111.act_ref, f32[1024,3072]{1,0:T(8,128)} %get-tuple-element.112.slope_ref, bf16[2,768,3072]{2,1,0:T(8,128)(2,1)} %w1_ref.9, ...), custom_call_target="tpu_custom_call" | custom-call | flops 10871635968 | bytes 30000000 | tf_op jit(solution)/shard_map/expert_second/pallas_call | solution.py:418
  192.1 4.2 %all-to-all-start.3 = ((bf16[4,2,256,768]{3,2,1,0:T(8,128)(2,1)}), bf16[4,2,256,768]{3,2,1,0:T(8,128)(2,1)S(1)}, u32[]{:S(2)}, u32[]{:S(2)}) async-start(bf16[4,2,256,768]{3,2,1,0:T(8,128)(2,1)} %get-tuple-element.113), calls=%async_computation.3 | async-start | bytes 6291456 | tf_op jit(solution)/shard_map/all_to_all | solution.py:943
  196.3 9.9 %weight_grad.3 = (bf16[2,2,96,3072]{3,2,1,0:T(8,128)(2,1)}, bf16[2,2,96,3072]{3,2,1,0:T(8,128)(2,1)}) custom-call(s32[3]{0:T(128)} %pad_add_fusion.where_ref, bf16[4,2,256,768]{3,2,1,0:T(8,128)(2,1)} %all-to-all-done.rows_ref.a_ref, bf16[1024,3072]{1,0:T(8,128)(2,1)} %get-tuple-element.115.b_ref), custom_call_target="tpu_custom_call" | custom-call | flops 3623878656 | bytes 9750000 | tf_op jit(solution)/shard_map/weight_grad/pallas_call | solution.py:462
  206.3 2.0 collective-permute-done.2
  208.2 1.8 collective-permute-start.8
  210.0 3.1 fusion.1
  213.1 1.6 collective-permute-start.7
  214.7 2.5 fusion.15
  217.7 2.5 collective-permute-start.6
  220.2 20.8 %shared_grad.1 = (bf16[2,2,2,2,96,768]{5,4,3,2,1,0:T(8,128)(2,1)}, bf16[2,2,2,2,96,768]{5,4,3,2,1,0:T(8,128)(2,1)}) custom-call(s32[5]{0:T(128)} %stack.41.where_ref, bf16[4,1024,768]{2,1,0:T(8,128)(2,1)} %get-tuple-element.120.h_ref.x_ref.g_ref.mine_ref.refs_0_, bf16[4,1024,768]{2,1,0:T(8,128)(2,1)} %collective-permute-done.3.peer_ref.refs_1_, ...), custom_call_target="tpu_custom_call" | custom-call | flops 7247757312 | bytes 18750000 | tf_op jit(solution)/shard_map/shared_grad/pallas_call | solution.py:531
  241.1 1.7 collective-permute-start.9
  242.7 1.6 copy-done.1
  244.4 29.8 %backward.2 = (bf16[1024,768]{1,0:T(8,128)(2,1)}, f32[1024,768]{1,0:T(8,128)}, f32[4,8,768]{2,1,0:T(8,128)}, bf16[512,1664]{1,0:T(8,128)(2,1)}, bf16[512,1664]{1,0:T(8,128)(2,1)}) custom-call(s32[4]{0:T(128)} %len_ref.7, s32[5]{0:T(128)} %stack.41.where_ref, bf16[1024,768]{1,0:T(8,128)(2,1)} %tok_ref.3, bf16[1024,768]{1,0:T(8,128)(2,1)} %cot_ref.9, ...), custom_call_target="tpu_custom_call" | custom-call | flops 7500000256 | bytes 10500000 | tf_op jit(solution)/shard_map/backward/pallas_call | solution.py:676
  274.2 2.0 fusion.6
  276.6 2.7 fusion.2
  279.3 2.5 fusion.14
  282.5 30.1 %backward.3 = (bf16[1024,768]{1,0:T(8,128)(2,1)}, f32[1024,768]{1,0:T(8,128)}, f32[4,8,768]{2,1,0:T(8,128)}, bf16[512,1664]{1,0:T(8,128)(2,1)}, bf16[512,1664]{1,0:T(8,128)(2,1)}) custom-call(s32[4]{0:T(128)} %len_ref.7, s32[5]{0:T(128)} %stack.41.where_ref, ...), custom_call_target="tpu_custom_call", output_to_operand_aliasing={{0}: (16, {}), {1}: (17, {}), {2}: (18, {})} | custom-call | flops 7500000256 | bytes 10500000 | tf_op jit(solution)/shard_map/backward/pallas_call | solution.py:676
  313.2 2.7 fusion.4
  315.9 2.8 collective-permute-done.15
  318.7 2.3 collective-permute-start.12
  321.9 2.5 fusion.13
  324.7 2.6 fusion.3
  327.3 1.5 collective-permute-start.10
  328.8 14.2 %tail_grad.1 = (bf16[2,2,2,96,768]{4,3,2,1,0:T(8,128)(2,1)}, bf16[2,2,2,96,768]{4,3,2,1,0:T(8,128)(2,1)}, bf16[768,128]{1,0:T(8,128)(2,1)}) custom-call(s32[5]{0:T(128)} %stack.41.where_ref, bf16[4,1024,768]{2,1,0:T(8,128)(2,1)} %get-tuple-element.120.h_ref.x_ref.g_ref.mine_ref.refs_0_, bf16[4,1024,768]{2,1,0:T(8,128)(2,1)} %collective-permute-done.3.peer_ref.refs_1_, ...), custom_call_target="tpu_custom_call" | custom-call | flops 3750000128 | bytes 15000000 | tf_op jit(solution)/shard_map/tail_grad/pallas_call | solution.py:766
  343.7 12.9 %collective-permute-done.14 = bf16[96,3072]{1,0:T(8,128)(2,1)} collective-permute-done((bf16[96,3072]{1,0:T(8,128)(2,1)}, bf16[96,3072]{1,0:T(8,128)(2,1)}, u32[]{:S(2)}, u32[]{:S(2)}) %collective-permute-start.14) | collective-permute-done | bytes 589856 | tf_op jit(solution)/shard_map/ppermute | solution.py:817
  356.6 1.9 fusion.5
  358.6 2.3 fusion.12
  360.9 3.4 collective-permute-start.20
  364.2 2.5 fusion.11
  367.0 2.0 copy.79
  370.6 4.9 %all-to-all-start.4 = ((bf16[32,4,1408]{2,1,0:T(4,128)(2,1)}), bf16[32,4,1408]{2,1,0:T(4,128)(2,1)S(1)}, u32[]{:S(2)}, u32[]{:S(2)}) async-start(bf16[32,4,1408]{2,1,0:T(4,128)(2,1)} %bitcast.26), calls=%async_computation.4 | async-start | bytes 720896 | tf_op jit(solution)/shard_map/all_to_all | solution.py:888
  375.5 1.2 fusion.17
  376.7 1.9 collective-permute-start.19
  378.7 13.6 %collective-permute-done.21 = bf16[2,2,96,768]{3,2,1,0:T(8,128)(2,1)} collective-permute-done((bf16[2,2,96,768]{3,2,1,0:T(8,128)(2,1)}, bf16[2,2,96,768]{3,2,1,0:T(8,128)(2,1)}, u32[]{:S(2)}, u32[]{:S(2)}) %collective-permute-start.21) | collective-permute-done | bytes 589856 | tf_op jit(solution)/shard_map/ppermute | solution.py:817
  392.3 2.1 fusion.20
  394.4 2.0 collective-permute-start.24
  396.4 3.0 fusion.8
  399.4 1.1 fusion.19
  401.2 1.6 pad_maximum_fusion
  402.7 8.2 %collective-permute-done.22 = bf16[2,96,768]{2,1,0:T(8,128)(2,1)S(1)} collective-permute-done((bf16[2,96,768]{2,1,0:T(8,128)(2,1)S(1)}, bf16[2,96,768]{2,1,0:T(8,128)(2,1)S(1)}, u32[]{:S(2)}, u32[]{:S(2)}) %collective-permute-start.22) | collective-permute-done | bytes 294944 | tf_op jit(solution)/shard_map/ppermute | solution.py:817
  410.9 1.6 fusion.27
  412.8 1.4 fusion.18
  416.6 1.0 fusion.24
  417.6 2.5 collective-permute-done.23
  420.1 1.1 fusion.26
  (87 shorter events, 14.5 us)
Async XLA Ops:
  36.8 41.4 %all-to-all-start.1 = ((bf16[4,2,256,768]{3,2,1,0:T(8,128)(2,1)}), bf16[4,2,256,768]{3,2,1,0:T(8,128)(2,1)S(1)}, u32[]{:S(2)}, u32[]{:S(2)}) async-start(bf16[4,2,256,768]{3,2,1,0:T(8,128)(2,1)} %dispatch.2), calls=%async_computation.1 | async-start | bytes 6291456 | tf_op jit(solution)/shard_map/all_to_all | solution.py:927
  78.3 1.9 copy-start.2
  80.1 47.6 %all-to-all-start = ((bf16[4,2,256,768]{3,2,1,0:T(8,128)(2,1)}), bf16[4,2,256,768]{3,2,1,0:T(8,128)(2,1)}, u32[]{:S(2)}, u32[]{:S(2)}) async-start(bf16[4,2,256,768]{3,2,1,0:T(8,128)(2,1)} %dispatch.3), calls=%async_computation | async-start | bytes 6291456 | tf_op jit(solution)/shard_map/all_to_all | solution.py:927
  85.1 135.2 %collective-permute-start.3 = (bf16[4,1024,768]{2,1,0:T(8,128)(2,1)}, bf16[4,1024,768]{2,1,0:T(8,128)(2,1)}, u32[]{:S(2)}, u32[]{:S(2)}) collective-permute-start(bf16[4,1024,768]{2,1,0:T(8,128)(2,1)} %get-tuple-element.120.h_ref.x_ref.g_ref.mine_ref.refs_0_), channel_id=1, source_target_pairs={{0,1},{1,0},{2,3},{3,2},{4,5},{5,4},{6,7},{7,6},{8,9},{9,8},{10,11... | collective-permute-start | bytes 18874376 | tf_op jit(solution)/shard_map/ppermute | solution.py:817
  85.6 132.1 %collective-permute-start.5 = (bf16[1024,3072]{1,0:T(8,128)(2,1)}, bf16[1024,3072]{1,0:T(8,128)(2,1)}, u32[]{:S(2)}, u32[]{:S(2)}) collective-permute-start(bf16[1024,3072]{1,0:T(8,128)(2,1)} %get-tuple-element.123.act_ref), channel_id=1, source_target_pairs={{0,1},{1,0},{2,3},{3,2},{4,5},{5,4},{6,7},{7,6},{8,9},{9,8},{10,11... | collective-permute-start | bytes 18874376 | tf_op jit(solution)/shard_map/ppermute | solution.py:817
  103.2 57.0 %collective-permute-start = (bf16[2,2,96,3072]{3,2,1,0:T(8,128)(2,1)}, bf16[2,2,96,3072]{3,2,1,0:T(8,128)(2,1)}, u32[]{:S(2)}, u32[]{:S(2)}) collective-permute-start(bf16[2,2,96,3072]{3,2,1,0:T(8,128)(2,1)} %get-tuple-element.108), channel_id=1, source_target_pairs={{0,4},{4,0},{8,12},{12,8},{16,20},{20,16},{24,28},{28,24},{1,5},{5... | collective-permute-start | bytes 7077896 | tf_op jit(solution)/shard_map/ppermute | solution.py:817
  127.8 4.6 %copy-start.10 = (bf16[4,768]{1,0:T(4,128)(2,1)S(1)}, bf16[4,768]{1,0:T(4,128)(2,1)}, u32[]{:S(2)}) copy-start(bf16[4,768]{1,0:T(4,128)(2,1)} %param.14) | copy-start | bytes 18436
  127.8 4.7 %copy-start.9 = (bf16[768,8]{0,1:T(8,128)(2,1)S(1)}, bf16[768,8]{0,1:T(8,128)(2,1)}, u32[]{:S(2)}) copy-start(bf16[768,8]{0,1:T(8,128)(2,1)} %param.21) | copy-start | bytes 36868
  127.8 40.9 %all-to-all-start.2 = ((bf16[4,2,256,768]{3,2,1,0:T(8,128)(2,1)}), bf16[4,2,256,768]{3,2,1,0:T(8,128)(2,1)S(1)}, u32[]{:S(2)}, u32[]{:S(2)}) async-start(bf16[4,2,256,768]{3,2,1,0:T(8,128)(2,1)} %get-tuple-element.102), calls=%async_computation.2 | async-start | bytes 6291456 | tf_op jit(solution)/shard_map/all_to_all | solution.py:943
  131.8 85.4 %collective-permute-start.4 = (bf16[1024,1536]{1,0:T(8,128)(2,1)}, bf16[1024,1536]{1,0:T(8,128)(2,1)}, u32[]{:S(2)}, u32[]{:S(2)}) collective-permute-start(bf16[1024,1536]{1,0:T(8,128)(2,1)} %get-tuple-element.122), channel_id=1, source_target_pairs={{0,1},{1,0},{2,3},{3,2},{4,5},{5,4},{6,7},{7,6},{8,9},{9,8},{10,11... | collective-permute-start | bytes 9437192 | tf_op jit(solution)/shard_map/ppermute | solution.py:817
  143.2 65.1 %collective-permute-start.2 = (bf16[2,2,96,3072]{3,2,1,0:T(8,128)(2,1)}, bf16[2,2,96,3072]{3,2,1,0:T(8,128)(2,1)}, u32[]{:S(2)}, u32[]{:S(2)}) collective-permute-start(bf16[2,2,96,3072]{3,2,1,0:T(8,128)(2,1)} %get-tuple-element.118), channel_id=1, source_target_pairs={{0,4},{4,0},{8,12},{12,8},{16,20},{20,16},{24,28},{28,24},{1,5},{5... | collective-permute-start | bytes 7077896 | tf_op jit(solution)/shard_map/ppermute | solution.py:817
  163.2 49.9 %collective-permute-start.1 = (bf16[2,96,3072]{2,1,0:T(8,128)(2,1)}, bf16[2,96,3072]{2,1,0:T(8,128)(2,1)}, u32[]{:S(2)}, u32[]{:S(2)}) collective-permute-start(bf16[2,96,3072]{2,1,0:T(8,128)(2,1)} %fusion), channel_id=1, source_target_pairs={{0,8},{4,12},{8,0},{12,4},{16,24},{20,28},{24,16},{28,20},{1,9},{5... | collective-permute-start | bytes 3538952 | tf_op jit(solution)/shard_map/ppermute | solution.py:817
  168.7 23.4 %copy-start = (bf16[4,2,256,768]{3,2,1,0:T(8,128)(2,1)}, bf16[4,2,256,768]{3,2,1,0:T(8,128)(2,1)S(1)}, u32[]{:S(2)}) copy-start(bf16[4,2,256,768]{3,2,1,0:T(8,128)(2,1)S(1)} %all-to-all-done.2.rest_0_) | copy-start | bytes 9437188
  192.1 50.6 %all-to-all-start.3 = ((bf16[4,2,256,768]{3,2,1,0:T(8,128)(2,1)}), bf16[4,2,256,768]{3,2,1,0:T(8,128)(2,1)S(1)}, u32[]{:S(2)}, u32[]{:S(2)}) async-start(bf16[4,2,256,768]{3,2,1,0:T(8,128)(2,1)} %get-tuple-element.113), calls=%async_computation.3 | async-start | bytes 6291456 | tf_op jit(solution)/shard_map/all_to_all | solution.py:943
  208.2 68.0 %collective-permute-start.8 = (bf16[2,2,96,3072]{3,2,1,0:T(8,128)(2,1)}, bf16[2,2,96,3072]{3,2,1,0:T(8,128)(2,1)}, u32[]{:S(2)}, u32[]{:S(2)}) collective-permute-start(bf16[2,2,96,3072]{3,2,1,0:T(8,128)(2,1)} %get-tuple-element.135), channel_id=1, source_target_pairs={{0,4},{4,0},{8,12},{12,8},{16,20},{20,16},{24,28},{28,24},{1,5},{5... | collective-permute-start | bytes 7077896 | tf_op jit(solution)/shard_map/ppermute | solution.py:817
  213.1 63.2 %collective-permute-start.7 = (bf16[2,96,3072]{2,1,0:T(8,128)(2,1)}, bf16[2,96,3072]{2,1,0:T(8,128)(2,1)}, u32[]{:S(2)}, u32[]{:S(2)}) collective-permute-start(bf16[2,96,3072]{2,1,0:T(8,128)(2,1)} %fusion.1), channel_id=1, source_target_pairs={{0,8},{4,12},{8,0},{12,4},{16,24},{20,28},{24,16},{28,20},{1,9},{5... | collective-permute-start | bytes 3538952 | tf_op jit(solution)/shard_map/ppermute | solution.py:817
  217.2 95.5 %collective-permute-start.11 = (bf16[2,2,96,3072]{3,2,1,0:T(8,128)(2,1)}, bf16[2,2,96,3072]{3,2,1,0:T(8,128)(2,1)}, u32[]{:S(2)}, u32[]{:S(2)}) collective-permute-start(bf16[2,2,96,3072]{3,2,1,0:T(8,128)(2,1)} %get-tuple-element.145), channel_id=1, source_target_pairs={{0,4},{4,0},{8,12},{12,8},{16,20},{20,16},{24,28},{28,24},{1,5},{5... | collective-permute-start | bytes 7077896 | tf_op jit(solution)/shard_map/ppermute | solution.py:817
  217.7 56.5 %collective-permute-start.6 = (bf16[96,3072]{1,0:T(8,128)(2,1)}, bf16[96,3072]{1,0:T(8,128)(2,1)}, u32[]{:S(2)}, u32[]{:S(2)}) collective-permute-start(bf16[96,3072]{1,0:T(8,128)(2,1)} %fusion.15), channel_id=1, source_target_pairs={{0,16},{4,20},{8,24},{12,28},{16,0},{20,4},{24,8},{28,12},{1,17},{... | collective-permute-start | bytes 1769480 | tf_op jit(solution)/shard_map/ppermute | solution.py:817
  241.1 83.6 %collective-permute-start.9 = (bf16[2,2,2,2,96,768]{5,4,3,2,1,0:T(8,128)(2,1)}, bf16[2,2,2,2,96,768]{5,4,3,2,1,0:T(8,128)(2,1)}, u32[]{:S(2)}, u32[]{:S(2)}) collective-permute-start(bf16[2,2,2,2,96,768]{5,4,3,2,1,0:T(8,128)(2,1)} %get-tuple-element.143), channel_id=1, source_target_pairs={{0,2},{1,3},{2,0},{3,1},{4,6},{5,7},{6,4},{7,5},{8,10},{9,11},{10,... | collective-permute-start | bytes 7077896 | tf_op jit(solution)/shard_map/ppermute | solution.py:817
  242.7 1.7 copy-start.1
  274.2 2.4 copy-start.4
  281.9 40.0 %collective-permute-start.13 = (bf16[2,96,3072]{2,1,0:T(8,128)(2,1)}, bf16[2,96,3072]{2,1,0:T(8,128)(2,1)}, u32[]{:S(2)}, u32[]{:S(2)}) collective-permute-start(bf16[2,96,3072]{2,1,0:T(8,128)(2,1)} %fusion.2), channel_id=1, source_target_pairs={{0,8},{4,12},{8,0},{12,4},{16,24},{20,28},{24,16},{28,20},{1,9},{5... | collective-permute-start | bytes 3538952 | tf_op jit(solution)/shard_map/ppermute | solution.py:817
  282.4 36.3 %collective-permute-start.15 = (bf16[96,3072]{1,0:T(8,128)(2,1)}, bf16[96,3072]{1,0:T(8,128)(2,1)}, u32[]{:S(2)}, u32[]{:S(2)}) collective-permute-start(bf16[96,3072]{1,0:T(8,128)(2,1)} %fusion.14), channel_id=1, source_target_pairs={{0,16},{4,20},{8,24},{12,28},{16,0},{20,4},{24,8},{28,12},{1,17},{... | collective-permute-start | bytes 1769480 | tf_op jit(solution)/shard_map/ppermute | solution.py:817
  282.5 30.7 %copy-start.3 = (bf16[2,2,96,3072]{3,2,1,0:T(8,128)(2,1)S(1)}, bf16[2,2,96,3072]{3,2,1,0:T(8,128)(2,1)}, u32[]{:S(2)}) copy-start(bf16[2,2,96,3072]{3,2,1,0:T(8,128)(2,1)} %get-tuple-element.116) | copy-start | bytes 7077892
  312.7 16.1 %collective-permute-start.17 = (bf16[512,1664]{1,0:T(8,128)(2,1)}, bf16[512,1664]{1,0:T(8,128)(2,1)}, u32[]{:S(2)}, u32[]{:S(2)}) collective-permute-start(bf16[512,1664]{1,0:T(8,128)(2,1)} %get-tuple-element.153), channel_id=1, source_target_pairs={{0,1},{1,0},{2,3},{3,2},{4,5},{5,4},{6,7},{7,6},{8,9},{9,8},{10,11... | collective-permute-start | bytes 5111816 | tf_op jit(solution)/shard_map/ppermute | solution.py:817
  312.7 16.0 %collective-permute-start.16 = (bf16[512,1664]{1,0:T(8,128)(2,1)}, bf16[512,1664]{1,0:T(8,128)(2,1)}, u32[]{:S(2)}, u32[]{:S(2)}) collective-permute-start(bf16[512,1664]{1,0:T(8,128)(2,1)} %get-tuple-element.152), channel_id=1, source_target_pairs={{0,1},{1,0},{2,3},{3,2},{4,5},{5,4},{6,7},{7,6},{8,9},{9,8},{10,11... | collective-permute-start | bytes 5111816 | tf_op jit(solution)/shard_map/ppermute | solution.py:817
  315.9 8.7 %copy-start.5 = (bf16[2,2,2,2,96,768]{5,4,3,2,1,0:T(8,128)(2,1)S(1)}, bf16[2,2,2,2,96,768]{5,4,3,2,1,0:T(8,128)(2,1)}, u32[]{:S(2)}) copy-start(bf16[2,2,2,2,96,768]{5,4,3,2,1,0:T(8,128)(2,1)} %get-tuple-element.124) | copy-start | bytes 7077892
  318.7 39.9 %collective-permute-start.12 = (bf16[2,96,3072]{2,1,0:T(8,128)(2,1)}, bf16[2,96,3072]{2,1,0:T(8,128)(2,1)}, u32[]{:S(2)}, u32[]{:S(2)}) collective-permute-start(bf16[2,96,3072]{2,1,0:T(8,128)(2,1)} %fusion.4), channel_id=1, source_target_pairs={{0,8},{4,12},{8,0},{12,4},{16,24},{20,28},{24,16},{28,20},{1,9},{5... | collective-permute-start | bytes 3538952 | tf_op jit(solution)/shard_map/ppermute | solution.py:817
  324.4 32.1 %collective-permute-start.14 = (bf16[96,3072]{1,0:T(8,128)(2,1)}, bf16[96,3072]{1,0:T(8,128)(2,1)}, u32[]{:S(2)}, u32[]{:S(2)}) collective-permute-start(bf16[96,3072]{1,0:T(8,128)(2,1)} %fusion.13), channel_id=1, source_target_pairs={{0,16},{4,20},{8,24},{12,28},{16,0},{20,4},{24,8},{28,12},{1,17},{... | collective-permute-start | bytes 1769480 | tf_op jit(solution)/shard_map/ppermute | solution.py:817
  327.3 37.0 %collective-permute-start.10 = (bf16[2,2,2,96,768]{4,3,2,1,0:T(8,128)(2,1)}, bf16[2,2,2,96,768]{4,3,2,1,0:T(8,128)(2,1)}, u32[]{:S(2)}, u32[]{:S(2)}) collective-permute-start(bf16[2,2,2,96,768]{4,3,2,1,0:T(8,128)(2,1)} %fusion.3), channel_id=1, source_target_pairs={{0,4},{4,0},{8,12},{12,8},{16,20},{20,16},{24,28},{28,24},{1,5},{5... | collective-permute-start | bytes 3538952 | tf_op jit(solution)/shard_map/ppermute | solution.py:817
  343.0 32.5 %collective-permute-start.18 = (bf16[2,2,2,96,768]{4,3,2,1,0:T(8,128)(2,1)}, bf16[2,2,2,96,768]{4,3,2,1,0:T(8,128)(2,1)}, u32[]{:S(2)}, u32[]{:S(2)}) collective-permute-start(bf16[2,2,2,96,768]{4,3,2,1,0:T(8,128)(2,1)} %get-tuple-element.161), channel_id=1, source_target_pairs={{0,2},{1,3},{2,0},{3,1},{4,6},{5,7},{6,4},{7,5},{8,10},{9,11},{10,... | collective-permute-start | bytes 3538952 | tf_op jit(solution)/shard_map/ppermute | solution.py:817
  360.9 35.5 %collective-permute-start.20 = (bf16[96,3072]{1,0:T(8,128)(2,1)}, bf16[96,3072]{1,0:T(8,128)(2,1)}, u32[]{:S(2)}, u32[]{:S(2)}) collective-permute-start(bf16[96,3072]{1,0:T(8,128)(2,1)} %fusion.12), channel_id=1, source_target_pairs={{0,16},{4,20},{8,24},{12,28},{16,0},{20,4},{24,8},{28,12},{1,17},{... | collective-permute-start | bytes 1769480 | tf_op jit(solution)/shard_map/ppermute | solution.py:817
  366.7 25.6 %collective-permute-start.21 = (bf16[2,2,96,768]{3,2,1,0:T(8,128)(2,1)}, bf16[2,2,96,768]{3,2,1,0:T(8,128)(2,1)}, u32[]{:S(2)}, u32[]{:S(2)}) collective-permute-start(bf16[2,2,96,768]{3,2,1,0:T(8,128)(2,1)} %fusion.11), channel_id=1, source_target_pairs={{0,8},{4,12},{8,0},{12,4},{16,24},{20,28},{24,16},{28,20},{1,9},{5... | collective-permute-start | bytes 1769480 | tf_op jit(solution)/shard_map/ppermute | solution.py:817
  367.0 2.0 copy-start.7
  367.0 2.0 copy-start.8
  369.0 6.5 %copy-start.6 = (bf16[2,2,2,96,768]{4,3,2,1,0:T(8,128)(2,1)S(1)}, bf16[2,2,2,96,768]{4,3,2,1,0:T(8,128)(2,1)}, u32[]{:S(2)}) copy-start(bf16[2,2,2,96,768]{4,3,2,1,0:T(8,128)(2,1)} %get-tuple-element.154) | copy-start | bytes 3538948
  370.6 42.0 %all-to-all-start.4 = ((bf16[32,4,1408]{2,1,0:T(4,128)(2,1)}), bf16[32,4,1408]{2,1,0:T(4,128)(2,1)S(1)}, u32[]{:S(2)}, u32[]{:S(2)}) async-start(bf16[32,4,1408]{2,1,0:T(4,128)(2,1)} %bitcast.26), calls=%async_computation.4 | async-start | bytes 720896 | tf_op jit(solution)/shard_map/all_to_all | solution.py:888
  376.7 22.7 %collective-permute-start.19 = (bf16[2,2,96,768]{3,2,1,0:T(8,128)(2,1)S(1)}, bf16[2,2,96,768]{3,2,1,0:T(8,128)(2,1)S(1)}, u32[]{:S(2)}, u32[]{:S(2)}) collective-permute-start(bf16[2,2,96,768]{3,2,1,0:T(8,128)(2,1)S(1)} %fusion.17), channel_id=1, source_target_pairs={{0,4},{4,0},{8,12},{12,8},{16,20},{20,16},{24,28},{28,24},{1,5},{5... | collective-permute-start | bytes 1769480 | tf_op jit(solution)/shard_map/ppermute | solution.py:817
  394.4 18.4 %collective-permute-start.24 = (bf16[2,96,768]{2,1,0:T(8,128)(2,1)}, bf16[2,96,768]{2,1,0:T(8,128)(2,1)S(1)}, u32[]{:S(2)}, u32[]{:S(2)}) collective-permute-start(bf16[2,96,768]{2,1,0:T(8,128)(2,1)} %fusion.20), channel_id=1, source_target_pairs={{0,16},{4,20},{8,24},{12,28},{16,0},{20,4},{24,8},{28,12},{1,17},{... | collective-permute-start | bytes 884744 | tf_op jit(solution)/shard_map/ppermute | solution.py:817
  400.5 10.4 %collective-permute-start.22 = (bf16[2,96,768]{2,1,0:T(8,128)(2,1)S(1)}, bf16[2,96,768]{2,1,0:T(8,128)(2,1)S(1)}, u32[]{:S(2)}, u32[]{:S(2)}) collective-permute-start(bf16[2,96,768]{2,1,0:T(8,128)(2,1)S(1)} %fusion.19), channel_id=1, source_target_pairs={{0,8},{4,12},{8,0},{12,4},{16,24},{20,28},{24,16},{28,20},{1,9},{5... | collective-permute-start | bytes 884744 | tf_op jit(solution)/shard_map/ppermute | solution.py:817
  412.6 7.6 %collective-permute-start.23 = (bf16[96,768]{1,0:T(8,128)(2,1)}, bf16[96,768]{1,0:T(8,128)(2,1)}, u32[]{:S(2)}, u32[]{:S(2)}) collective-permute-start(bf16[96,768]{1,0:T(8,128)(2,1)} %fusion.27), channel_id=1, source_target_pairs={{0,16},{4,20},{8,24},{12,28},{16,0},{20,4},{24,8},{28,12},{1,17},{... | collective-permute-start | bytes 442376 | tf_op jit(solution)/shard_map/ppermute | solution.py:817
